TPU v7x, 256 devices: a whole 4x4x8 slice. The times are simulated.
256 devices in a mesh: row: 32 (over x, y, core), col: 8 (over z).
Axes of the slice: x: 4, y: 4, z: 8, core: 2. Of those that a mesh axis runs over, the one named last changes fastest.
Arguments:
- blocks: float32 [32, 8, 8, 32, 2, 8, 128], P('row', 'col'), may hold values from 0.5 to 1620
- plan: int32 [32, 8, 8, 32, 2], P('row', 'col'), may hold values from 0 to 4095, as said below
- live: int32 [32, 8, 8, 32], P('row', 'col'), may hold values from 1 to 2, as said below
- row_emb: float32 [300, 32768], P(None, ('row', 'col')), may hold values from -1.5 to 1.5
- col_emb: float32 [300, 32768], P(None, ('col', 'row')), may hold values from -1.5 to 1.5
- row_acc: float32 [300, 32768], P(None, ('row', 'col')), may hold values from 0.5 to 5
- col_acc: float32 [300, 32768], P(None, ('col', 'row')), may hold values from 0.5 to 5
Outputs:
- new_row_emb: float32 [300, 32768], P(None, ('row', 'col'))
- new_col_emb: float32 [300, 32768], P(None, ('col', 'row'))
- new_row_acc: float32 [300, 32768], P(None, ('row', 'col'))
- new_col_acc: float32 [300, 32768], P(None, ('col', 'row'))
Inputs may be any that keep to these rules, and one draw needn't show every extreme that they name: plan[r, c, c2, r2, p] is a sub-block number of tile (r, c); numbers may repeat and repeated slots add. Over all index pairs (r2, c2), slot 0 names every sub-block row and every sub-block column of each tile. Slots at or past live[r, c, c2, r2] hold values that are not counts. In every draw some tile gets 2 live slots from every index pair.
All inputs are finite; a program needn't handle non-finite values.
Results may differ from a plain program's by a relative error of at most 0.0003.
Values sent between devices are 32-bit elements; how exact they have to be, the bound alone decides.
No kernel may reach another device: no remote copies, remote signals or barrier semaphores. Data moves between devices by JAX's collectives and lax.ppermute only.
A program may use at most 192 MiB of HBM per device.

v0:
```python
import jax
import jax.numpy as jnp
from jax import lax
from jax.sharding import PartitionSpec as P

LEARNING_RATE = 0.2


def per_device(blocks, plan, live, row_emb, col_emb, row_acc, col_acc):
    rows_count = lax.axis_size("row")
    cols_count = lax.axis_size("col")
    highest = lax.Precision.HIGHEST
    outgoing = blocks[0, 0]
    arrived = lax.all_to_all(
        lax.all_to_all(outgoing, "row", split_axis=1, concat_axis=1, tiled=True),
        "col",
        split_axis=0,
        concat_axis=0,
        tiled=True,
    )
    sub_rows = blocks.shape[5]
    sub_cols = blocks.shape[6]
    tile_rows = row_emb.shape[1] * cols_count
    tile_cols = col_emb.shape[1] * rows_count
    grid_row_count = tile_rows // sub_rows
    grid_column_count = tile_cols // sub_cols
    block_total = grid_row_count * grid_column_count
    places = plan[0, 0]
    limits = live[0, 0]
    slot_ids = lax.broadcasted_iota(jnp.int32, places.shape, 2)
    target = jnp.where(slot_ids < limits[:, :, None], places, block_total)
    flat_layout = arrived.reshape(-1, sub_rows * sub_cols)
    dense_block_matrix = jax.ops.segment_sum(
        flat_layout, target.reshape(-1), num_segments=block_total + 1
    )[:block_total]
    tile_counts = (
        dense_block_matrix.reshape(grid_row_count, grid_column_count, sub_rows, sub_cols)
        .transpose(0, 2, 1, 3)
        .reshape(tile_rows, tile_cols)
    )
    row_part = jnp.sum(tile_counts, axis=1)
    col_part = jnp.sum(tile_counts, axis=0)
    col_mass = lax.psum(col_part, "row")
    row_mass = lax.psum(row_part, "col")
    grand_total = lax.psum(jnp.sum(row_part), ("row", "col"))
    row_block = lax.all_gather(row_emb, "col", axis=1, tiled=True)
    col_block = lax.all_gather(col_emb, "row", axis=1, tiled=True)
    rows_all = tile_rows * rows_count
    cols_all = tile_cols * cols_count
    loss_scale = 4.0 * float(rows_all * cols_all) ** (-0.25)
    col_base = jnp.log(grand_total) - jnp.log(col_mass)[None, :]
    row_logs = jnp.log(row_mass)
    step_rows = min(512, tile_rows)
    col_term = jnp.zeros((col_block.shape[0], tile_cols), jnp.float32)
    row_pieces = []
    for start in range(0, tile_rows, step_rows):
        counts_part = tile_counts[start : start + step_rows]
        vectors_part = row_block[:, start : start + step_rows]
        scores = lax.dot_general(
            vectors_part, col_block, (((0,), (0,)), ((), ())), precision=highest
        )
        baseline = col_base - row_logs[start : start + step_rows][:, None]
        positive = counts_part > 0
        pmi_target = jnp.log(jnp.where(positive, counts_part, 1.0)) + baseline
        confidence = 0.1 + 0.25 * jnp.sqrt(counts_part)
        loss_grad = (
            jnp.where(
                positive, confidence * (scores - pmi_target), jax.nn.sigmoid(scores - baseline)
            )
            * loss_scale
        )
        row_pieces.append(
            lax.dot_general(col_block, loss_grad, (((1,), (1,)), ((), ())), precision=highest)
        )
        col_term = col_term + jnp.dot(vectors_part, loss_grad, precision=highest)
    row_term = jnp.concatenate(row_pieces, axis=1)
    row_share = lax.psum_scatter(row_term, "col", scatter_dimension=1, tiled=True)
    col_share = lax.psum_scatter(col_term, "row", scatter_dimension=1, tiled=True)
    new_row_acc = row_acc + row_share * row_share
    new_col_acc = col_acc + col_share * col_share
    new_row_emb = row_emb - LEARNING_RATE * row_share / jnp.sqrt(new_row_acc)
    new_col_emb = col_emb - LEARNING_RATE * col_share / jnp.sqrt(new_col_acc)
    return (new_row_emb, new_col_emb, new_row_acc, new_col_acc)


def solution(mesh):
    return jax.shard_map(
        per_device,
        mesh=mesh,
        in_specs=(
            P("row", "col", None, None, None, None, None),
            P("row", "col", None, None, None),
            P("row", "col", None, None),
            P(None, ("row", "col")),
            P(None, ("col", "row")),
            P(None, ("row", "col")),
            P(None, ("col", "row")),
        ),
        out_specs=(
            P(None, ("row", "col")),
            P(None, ("col", "row")),
            P(None, ("row", "col")),
            P(None, ("col", "row")),
        ),
        check_vma=False,
    )
```

profile of v0, /device:TPU:16, one launch (start us, length us, event | category | flops | bytes accessed | tf_op | source)
XLA Modules:
  0.0 581.4 jit_solution(6106549809527180893)
XLA Ops:
  8.7 1.8 copy.27
  10.5 33.8 %all_to_all.10 = f32[8,32,2,8,128]{4,3,2,0,1:T(8,128)S(1)} all-to-all(f32[8,32,2,8,128]{4,3,2,0,1:T(8,128)S(1)} %bitcast.54), channel_id=1, replica_groups=mesh['row'=32,'col'=8] {'row'}, dimensions={1} | all-to-all | bytes 4194304 | tf_op jit(solution)/shard_map/all_to_all | solution.py:15
  44.3 1.5 copy.19
  45.8 8.5 %all-to-all-start.1 = ((f32[8,32,2,8,128]{4,3,2,1,0:T(8,128)}), f32[8,32,2,8,128]{4,3,2,1,0:T(8,128)S(1)}, u32[]{:S(2)}, u32[]{:S(2)}) async-start(f32[8,32,2,8,128]{4,3,2,1,0:T(8,128)} %copy.19), calls=%async_computation.1 | async-start | bytes 4194304 | tf_op jit(solution)/shard_map/all_to_all | solution.py:14
  54.9 50.2 %all-to-all-done.1 = f32[8,32,2,8,128]{4,3,2,1,0:T(8,128)S(1)} async-done(((f32[8,32,2,8,128]{4,3,2,1,0:T(8,128)}), f32[8,32,2,8,128]{4,3,2,1,0:T(8,128)S(1)}, u32[]{:S(2)}, u32[]{:S(2)}) %all-to-all-start.1) | async-done | bytes 2097184 | tf_op jit(solution)/shard_map/all_to_all | solution.py:14
  105.1 11.9 %scatter_custom_fusion = f32[4097,1024]{1,0:T(8,128)} fusion(s32[512]{0:T(512)S(1)} %bitcast.58, f32[]{:T(128)} %constant.7.clone.1, f32[64,8,8,128]{3,2,1,0:T(8,128)S(1)} %bitcast.55), kind=kCustom, calls=%fused_computation.12 | custom fusion | flops 524288 | bytes 18878468 | tf_op jit(solution)/shard_map/scatter-add | solution.py:33
  116.9 13.3 %slice_reduce_fusion = (f32[]{:T(128)}, f32[512,8,8,128]{3,1,2,0:T(8,128)}) fusion(f32[4097,1024]{1,0:T(8,128)} %scatter_custom_fusion), kind=kLoop, calls=%fused_computation.2 | loop fusion | flops 4194303 | bytes 33554436 | tf_op jit(solution)/shard_map/reduce_sum | solution.py:45
  130.3 73.7 %psum.21 = f32[]{:T(128)} all-reduce(f32[]{:T(128)} %get-tuple-element.10), channel_id=1, replica_groups=mesh['row'=32,'col'=8] {'row','col'}, use_global_device_ids=true, to_apply=%region_2.3 | all-reduce | flops 1 | bytes 8 | tf_op jit(solution)/shard_map/psum | solution.py:45
  204.7 14.3 %copy.21 = f32[512,8,8,128]{3,2,1,0:T(8,128)} copy(f32[512,8,8,128]{3,1,2,0:T(8,128)} %get-tuple-element.11) | data formatting | bytes 33554432
  218.9 7.2 %fusion.27 = (f32[32,128]{1,0:T(8,128)S(1)}, f32[128,8]{1,0:T(8,128)S(1)}) fusion(f32[128,32,8,128]{3,2,1,0:T(8,128)} %bitcast.52), kind=kLoop, calls=%fused_computation.53 | loop fusion | flops 8383488 | bytes 16797696 | tf_op jit(solution)/shard_map/reduce_sum | solution.py:42
  226.2 16.2 %psum.23 = f32[1024]{0:T(1024)S(1)} all-reduce(f32[1024]{0:T(1024)S(1)} %reduce_sum.35), channel_id=1, replica_groups=mesh['row'=32,'col'=8] {'col'}, use_global_device_ids=true, to_apply=%region_6.7 | all-reduce | flops 1024 | bytes 8192 | tf_op jit(solution)/shard_map/psum | solution.py:44
  242.5 115.2 %psum.22 = f32[4096]{0:T(1024)S(1)} all-reduce(f32[4096]{0:T(1024)S(1)} %bitcast.56), channel_id=1, replica_groups=mesh['row'=32,'col'=8] {'row'}, use_global_device_ids=true, to_apply=%region_4.5 | all-reduce | flops 4096 | bytes 32768 | tf_op jit(solution)/shard_map/psum | solution.py:43
  357.7 11.7 %bitcast_bitcast_fusion = f32[128,8,32,128]{3,1,2,0:T(8,128)} fusion(f32[128,32,8,128]{3,2,1,0:T(8,128)} %bitcast.53), kind=kLoop, calls=%fused_computation.1 | loop fusion | bytes 33554432 | tf_op jit(solution)/shard_map/transpose | solution.py:38
  369.4 21.9 %fusion.5 = f32[512,4096]{1,0:T(8,128)S(1)} fusion(f32[128,8,32,128]{3,1,2,0:T(8,128)} %bitcast_bitcast_fusion, f32[512]{0:T(512)S(1)} %get-tuple-element.13, f32[4096]{0:T(1024)S(1)} %log_subtract_fusion, f32[300,4096]{1,0:T(8,128)} %all-gather.5.cloned.1.call-done, f32[300,1024]{1,0:T(8,128)} %all-gather.3.cloned.1.call-done), kind=kOutput, calls=%fused_computation.17 | convolution fusion | flops 7579107328 | bytes 22398976 | tf_op jit(solution)/shard_map/dot_general | solution.py:59
  391.4 25.5 %fusion.3 = f32[512,4096]{1,0:T(8,128)S(1)} fusion(f32[128,8,32,128]{3,1,2,0:T(8,128)} %bitcast_bitcast_fusion, f32[512]{0:T(512)S(1)} %get-tuple-element.12, f32[4096]{0:T(1024)S(1)} %log_subtract_fusion, f32[300,4096]{1,0:T(8,128)S(1)} %copy-done.2, f32[300,1024]{1,0:T(8,128)S(1)} %copy-done.3), kind=kOutput, calls=%fused_computation.15 | convolution fusion | flops 7579107328 | bytes 22398976 | tf_op jit(solution)/shard_map/dot_general | solution.py:59
  416.9 8.6 %convolution_bitcast_fusion.1 = f32[300,512]{1,0:T(8,128)S(1)} fusion(f32[512,4096]{1,0:T(8,128)S(1)} %fusion.3, f32[300,4096]{1,0:T(8,128)S(1)} %copy-done.2), kind=kOutput, calls=%fused_computation.38 | convolution fusion | flops 7549747200 | bytes 13918208 | tf_op jit(solution)/shard_map/dot_general | solution.py:73
  425.5 8.9 %convolution_bitcast_fusion = f32[300,512]{1,0:T(8,128)S(1)} fusion(f32[512,4096]{1,0:T(8,128)S(1)} %fusion.5, f32[300,4096]{1,0:T(8,128)S(1)} %copy-done.2), kind=kOutput, calls=%fused_computation.37 | convolution fusion | flops 7549747200 | bytes 13918208 | tf_op jit(solution)/shard_map/dot_general | solution.py:73
  434.3 1.1 pad_maximum_fusion
  435.6 11.3 %fusion.23 = f32[4096,300]{0,1:T(8,128)S(1)} fusion(f32[512,4096]{1,0:T(8,128)} %copy-done.1, f32[300,1024]{1,0:T(8,128)S(1)} %copy-done.3), kind=kOutput, calls=%fused_computation.42 | convolution fusion | flops 7549747200 | bytes 13926400 | tf_op jit(solution)/shard_map/dot_general | solution.py:75
  446.9 12.8 %fusion.18 = f32[300,4096]{1,0:T(8,128)} fusion(f32[4096,300]{0,1:T(8,128)S(1)} %fusion.23, f32[512,4096]{1,0:T(8,128)} %copy-done, f32[300,1024]{1,0:T(8,128)S(1)} %copy-done.3), kind=kOutput, calls=%fused_computation.33 | convolution fusion | flops 7550976000 | bytes 18907136 | tf_op jit(solution)/shard_map/dot_general | solution.py:75
  459.7 18.2 %reduce-scatter.3.cloned.1.call-done = f32[300,128]{1,0:T(8,128)} async-done(((f32[300,1024]{1,0:T(8,128)}), f32[300,128]{1,0:T(8,128)}) %reduce-scatter.3.cloned.1.call-update) | async-done | bytes 153616 | tf_op jit(solution)/shard_map/reduce_scatter | solution.py:77
  477.9 1.7 multiply_subtract_fusion.1
  479.6 93.1 %reduce-scatter.5.cloned.1.call-done = f32[300,128]{1,0:T(8,128)} async-done(((f32[300,4096]{1,0:T(8,128)}), f32[300,128]{1,0:T(8,128)}) %reduce-scatter.5.cloned.1.call-update) | async-done | bytes 153616 | tf_op jit(solution)/shard_map/reduce_scatter | solution.py:78
  572.7 1.7 multiply_subtract_fusion
  (39 shorter events, 2.3 us)
Async XLA Ops:
  7.2 362.2 %all-gather.3.cloned.1.call-start = ((), (), s32[]{:S(2)}) async-start(), calls=%async_computation.4 | async-start | bytes 1400832 | tf_op jit(solution)/shard_map/all_gather | solution.py:46
  7.9 361.5 %all-gather.5.cloned.1.call-start = ((), (), s32[]{:S(2)}) async-start(), calls=%async_computation.5 | async-start | bytes 5136384 | tf_op jit(solution)/shard_map/all_gather | solution.py:47
  8.7 45.7 %copy-start.9 = (s32[1,1,8,32]{3,2,1,0:T(8,128)S(1)}, s32[1,1,8,32]{3,2,1,0:T(8,128)}, u32[]{:S(2)}) copy-start(s32[1,1,8,32]{3,2,1,0:T(8,128)} %param.9) | copy-start | bytes 3076
  8.7 45.9 %copy-start.8 = (s32[1,1,8,32,2]{3,4,2,1,0:T(2,128)S(1)}, s32[1,1,8,32,2]{3,4,2,1,0:T(2,128)}, u32[]{:S(2)}) copy-start(s32[1,1,8,32,2]{3,4,2,1,0:T(2,128)} %param.8) | copy-start | bytes 6148
  45.8 59.3 %all-to-all-start.1 = ((f32[8,32,2,8,128]{4,3,2,1,0:T(8,128)}), f32[8,32,2,8,128]{4,3,2,1,0:T(8,128)S(1)}, u32[]{:S(2)}, u32[]{:S(2)}) async-start(f32[8,32,2,8,128]{4,3,2,1,0:T(8,128)} %copy.19), calls=%async_computation.1 | async-start | bytes 4194304 | tf_op jit(solution)/shard_map/all_to_all | solution.py:14
  54.3 423.7 %reduce-scatter.3.cloned.1.call-start = ((), (), s32[]{:S(2)}) async-start(), calls=%async_computation.6 | async-start | bytes 1400832 | tf_op jit(solution)/shard_map/reduce_scatter | solution.py:77
  369.4 22.0 %copy-start.2 = (f32[300,4096]{1,0:T(8,128)S(1)}, f32[300,4096]{1,0:T(8,128)}, u32[]{:S(2)}) copy-start(f32[300,4096]{1,0:T(8,128)} %all-gather.5.cloned.1.call-done) | copy-start | bytes 14745604
  369.4 22.0 %copy-start.3 = (f32[300,1024]{1,0:T(8,128)S(1)}, f32[300,1024]{1,0:T(8,128)}, u32[]{:S(2)}) copy-start(f32[300,1024]{1,0:T(8,128)} %all-gather.3.cloned.1.call-done) | copy-start | bytes 3686404
  391.3 34.1 %copy-start = (f32[512,4096]{1,0:T(8,128)}, f32[512,4096]{1,0:T(8,128)S(1)}, u32[]{:S(2)}) copy-start(f32[512,4096]{1,0:T(8,128)S(1)} %fusion.5) | copy-start | bytes 25165828
  416.8 8.6 %copy-start.1 = (f32[512,4096]{1,0:T(8,128)}, f32[512,4096]{1,0:T(8,128)S(1)}, u32[]{:S(2)}) copy-start(f32[512,4096]{1,0:T(8,128)S(1)} %fusion.3) | copy-start | bytes 25165828
  435.5 137.2 %reduce-scatter.5.cloned.1.call-start = ((), (), s32[]{:S(2)}) async-start(), calls=%async_computation.7 | async-start | bytes 5136384 | tf_op jit(solution)/shard_map/reduce_scatter | solution.py:78
  446.8 31.1 %copy-start.4 = (f32[300,128]{1,0:T(8,128)S(1)}, f32[300,128]{1,0:T(8,128)}, u32[]{:S(2)}) copy-start(f32[300,128]{1,0:T(8,128)} %param.10) | copy-start | bytes 460804
  446.8 31.1 %copy-start.6 = (f32[300,128]{1,0:T(8,128)S(1)}, f32[300,128]{1,0:T(8,128)}, u32[]{:S(2)}) copy-start(f32[300,128]{1,0:T(8,128)} %param.12) | copy-start | bytes 460804
  446.9 125.9 %copy-start.5 = (f32[300,128]{1,0:T(8,128)S(1)}, f32[300,128]{1,0:T(8,128)}, u32[]{:S(2)}) copy-start(f32[300,128]{1,0:T(8,128)} %param.11) | copy-start | bytes 460804
  446.9 125.9 %copy-start.7 = (f32[300,128]{1,0:T(8,128)S(1)}, f32[300,128]{1,0:T(8,128)}, u32[]{:S(2)}) copy-start(f32[300,128]{1,0:T(8,128)} %param.13) | copy-start | bytes 460804
Sparse Core Ops, SparseCore 0:
  9.7 43.8 all-gather.2
  56.1 53.7 all-gather.4
  435.6 42.2 reduce-scatter.2
  481.9 90.8 reduce-scatter.4
where the time goes:
time: 589 us; the launch traced here: 581 us
  blocking collectives  239 us (41%)
  waiting for transfers between devices  163 us (28%)
  matrix products  88.9 us (15%)
  other arithmetic  37 us (6%)
  local copies, waits for them, and re-layouts  29.9 us (5%)
  between operations  15.1 us (3%)
  starting transfers between devices  8.62 us (1%)
    psum x1, blocking collectives, per_device(): col_mass = lax.psum(col_part, 'row')  115 us
    reduce_scatter x1, waiting for transfers between devices, per_device(): lax.psum_scatter(col_term, 'row', scatter_dimension=1, tiled=True)  93.1 us
    psum x1, blocking collectives, per_device(): grand_total = lax.psum(jnp.sum(row_part), ('row', 'col'))  73.7 us
    all_to_all x1, waiting for transfers between devices, per_device(): lax.all_to_all(lax.all_to_all(outgoing, 'row', split_axis=1, concat_axis=...  50.2 us
    dot_general x2, matrix products, per_device(): lax.dot_general(vectors_part, col_block, (((0,), (0,)), ((), ())), precis...  47.4 us
    all_to_all x1, blocking collectives, per_device(): lax.all_to_all(outgoing, 'row', split_axis=1, concat_axis=1, tiled=True)  33.8 us
    dot_general x2, matrix products, per_device(): col_term = col_term + jnp.dot(vectors_part, loss_grad, precision=highest)  24.1 us
    reduce_scatter x1, waiting for transfers between devices, per_device(): lax.psum_scatter(row_term, 'col', scatter_dimension=1, tiled=True)  18.2 us
  transfers between devices with their start and end apart: 5, of which 3 were waited for; matrix products, arithmetic and copies ran while one was open for 15% of the time, Pallas kernels for 0%

commit v1 on v0

v1 whole, which is shorter than its diff:
```python
import jax
import jax.numpy as jnp
from jax import lax
from jax.experimental import pallas as pl
from jax.experimental.pallas import tpu as pltpu
from jax.sharding import Mesh, PartitionSpec as P

LEARNING_RATE = 0.2
GRID_X, GRID_Y, CORES = 4, 4, 2
ROW = ("x", "y", "core")
ALL = ("col", "x", "y", "core")
LANES = 128
F32 = jnp.float32
BF16 = jnp.bfloat16


def split(value):
    high = value.astype(BF16)
    return high, (value - high.astype(F32)).astype(BF16)


def place_kernel(target, alive, arrived, counts_out, mass_out, dense, row_sums, col_sums):
    slots = arrived.shape[0]
    columns = col_sums.shape[0]
    row_words = row_sums.shape[0] // LANES * 8
    row_sums[...] = jnp.zeros(row_sums.shape, F32)
    col_sums[...] = jnp.zeros(col_sums.shape, F32)
    blank = jnp.zeros(arrived.shape[1:], F32)

    def clear(p, carry):
        dense[target[p]] = blank
        return carry

    lax.fori_loop(0, slots, clear, 0, unroll=8)

    def add(p, carry):
        place = target[p]
        value = jnp.where(alive[p] > 0, arrived[p], 0.0)
        dense[place] = dense[place] + value
        row_sums[place // columns] = row_sums[place // columns] + value
        col_sums[place % columns] = col_sums[place % columns] + value
        return carry

    lax.fori_loop(0, slots, add, 0, unroll=4)

    def read(p, carry):
        counts_out[p] = dense[target[p]]
        return carry

    lax.fori_loop(0, slots, read, 0, unroll=8)
    col_part = jnp.sum(col_sums[...], axis=1)
    mass_out[0:columns, :] = col_part
    ones = jnp.ones((8, LANES), F32)
    row_part = lax.dot_general(
        ones,
        row_sums[...].reshape(-1, LANES),
        (((1,), (1,)), ((), ())),
        precision=lax.Precision.HIGHEST,
        preferred_element_type=F32,
    )
    for i in range(row_words):
        mass_out[columns + i : columns + i + 1, :] = row_part[0:1, i * LANES : (i + 1) * LANES]
    mass_out[columns + row_words :, :] = jnp.full((8, LANES), jnp.sum(col_part), F32)


def place(target, alive, arrived, grid_rows, grid_columns):
    slots = arrived.shape[0]
    return pl.pallas_call(
        place_kernel,
        name="place_counts",
        grid_spec=pltpu.PrefetchScalarGridSpec(
            num_scalar_prefetch=2,
            grid=(1,),
            in_specs=[pl.BlockSpec(memory_space=pltpu.VMEM)],
            out_specs=[pl.BlockSpec(memory_space=pltpu.VMEM)] * 2,
            scratch_shapes=[
                pltpu.VMEM((grid_rows * grid_columns, 8, LANES), F32),
                pltpu.VMEM((grid_rows, 8, LANES), F32),
                pltpu.VMEM((grid_columns, 8, LANES), F32),
            ],
        ),
        out_shape=[
            jax.ShapeDtypeStruct((slots, 8, LANES), F32),
            jax.ShapeDtypeStruct((grid_columns + grid_rows * 8 // LANES + 8, LANES), F32),
        ],
        compiler_params=pltpu.CompilerParams(vmem_limit_bytes=40 << 20),
    )(target, alive, arrived)


def grad_kernel(
    target, core, row_blocks, col_blocks, counts, masses,
    row_term, col_term,
    scores, col_stack, row_stack, row_turned, row_bias, col_bias, fresh,
):
    n_row, dim, _ = row_blocks.shape
    n_col = col_blocks.shape[0]
    slots = counts.shape[0]
    deep = col_stack.shape[0]
    tile_rows = n_row * LANES
    chunk = 512
    per_chunk = chunk // LANES
    n_chunks = n_col // per_chunk
    row_tile = 256

    log_total = jnp.log(masses[n_col + n_row : n_col + n_row + 1, :])
    col_bias[...] = 0.5 * (jnp.log(masses[0:n_col, :]) - log_total)
    row_logs = 0.5 * jnp.log(masses[n_col : n_col + n_row, :])
    col_stack[3 * dim :, :] = jnp.zeros((deep - 3 * dim, n_col * LANES), BF16)

    def load_col(j, carry):
        high, low = split(col_blocks[j])
        here = pl.ds(pl.multiple_of(j * LANES, LANES), LANES)
        col_stack[0:dim, here] = high
        col_stack[dim : 2 * dim, here] = low
        col_stack[2 * dim : 3 * dim, here] = high
        return carry

    lax.fori_loop(0, n_col, load_col, 0)
    for i in range(n_row):
        value = row_blocks[i]
        high, low = split(value)
        here = slice(i * LANES, (i + 1) * LANES)
        row_stack[0:dim, here] = high
        row_stack[dim : 2 * dim, here] = low
        high32, low32 = high.astype(F32), low.astype(F32)
        tall = jnp.concatenate(
            [high32, high32, low32, jnp.zeros((deep - 3 * dim, LANES), F32)], axis=0
        )
        row_turned[here, :] = (0.5 * tall.T).astype(BF16)
        row_bias[here, :] = jnp.broadcast_to(row_logs[i : i + 1, :], (LANES, LANES)).T

    def score(step, carry):
        rt = step // n_chunks
        ct = step % n_chunks
        rows = pl.ds(pl.multiple_of(rt * row_tile, row_tile), row_tile)
        cols = pl.ds(pl.multiple_of(ct * chunk, chunk), chunk)
        product = jnp.dot(row_turned[rows, :], col_stack[:, cols], preferred_element_type=F32)
        bias = row_bias[rows, :]
        for k in range(per_chunk):
            out = product[:, k * LANES : (k + 1) * LANES] + bias + col_bias[pl.ds(ct * per_chunk + k, 1), :]
            scores[rows, pl.ds(pl.multiple_of(ct * chunk + k * LANES, LANES), LANES)] = out
        return carry

    lax.fori_loop(0, n_chunks * (tile_rows // row_tile), score, 0)

    def spot(p):
        where = target[p]
        return (
            pl.ds(pl.multiple_of(where // n_col * 8, 8), 8),
            pl.ds(pl.multiple_of(where % n_col * LANES, LANES), LANES),
        )

    def counted(p, carry):
        count = counts[p]
        fresh[p] = (0.1 + 0.25 * jnp.sqrt(count)) * (2.0 * scores[spot(p)] - jnp.log(count))
        return carry

    lax.fori_loop(0, slots, counted, 0, unroll=8)

    def smooth(step, carry):
        rows = pl.ds(pl.multiple_of(step * 32, 32), 32)
        scores[rows, :] = 0.5 * jnp.tanh(scores[rows, :]) + 0.5
        return carry

    lax.fori_loop(0, tile_rows // 32, smooth, 0)

    def put(p, carry):
        scores[spot(p)] = fresh[p]
        return carry

    lax.fori_loop(0, slots, put, 0, unroll=8)

    for i in range(n_row):
        row_term[i] = jnp.zeros((dim, LANES), F32)

    def grads(ct, carry):
        cols = pl.ds(pl.multiple_of(ct * chunk, chunk), chunk)
        high, low = split(scores[:, cols])
        both = jnp.dot(row_stack[...], high, preferred_element_type=F32)
        rest = jnp.dot(row_stack[0:dim, :], low, preferred_element_type=F32)
        total = both[0:dim] + both[dim:] + rest
        for k in range(per_chunk):
            j = ct * per_chunk + k
            col_term[(j % 2) ^ core[0], j // 2] = total[:, k * LANES : (k + 1) * LANES]
        turn = (((1,), (1,)), ((), ()))
        both = lax.dot_general(col_stack[0 : 2 * dim, cols], high, turn, preferred_element_type=F32)
        rest = lax.dot_general(col_stack[0:dim, cols], low, turn, preferred_element_type=F32)
        total = both[0:dim] + both[dim:] + rest
        for i in range(n_row):
            row_term[i] = row_term[i] + total[:, i * LANES : (i + 1) * LANES]
        return carry

    lax.fori_loop(0, n_chunks, grads, 0)


def grads(target, core, row_blocks, col_blocks, counts, masses):
    n_row, dim, _ = row_blocks.shape
    n_col = col_blocks.shape[0]
    deep = -(-3 * dim // 256) * 256
    tile_rows = n_row * LANES
    tile_cols = n_col * LANES
    return pl.pallas_call(
        grad_kernel,
        name="tile_grads",
        grid_spec=pltpu.PrefetchScalarGridSpec(
            num_scalar_prefetch=2,
            grid=(1,),
            in_specs=[pl.BlockSpec(memory_space=pltpu.VMEM)] * 4,
            out_specs=[pl.BlockSpec(memory_space=pltpu.VMEM)] * 2,
            scratch_shapes=[
                pltpu.VMEM((tile_rows, tile_cols), F32),
                pltpu.VMEM((deep, tile_cols), BF16),
                pltpu.VMEM((2 * dim, tile_rows), BF16),
                pltpu.VMEM((tile_rows, deep), BF16),
                pltpu.VMEM((tile_rows, LANES), F32),
                pltpu.VMEM((n_col, LANES), F32),
                pltpu.VMEM(counts.shape, F32),
            ],
        ),
        out_shape=[
            jax.ShapeDtypeStruct((n_row, dim, LANES), F32),
            jax.ShapeDtypeStruct((CORES, n_col // CORES, dim, LANES), F32),
        ],
        compiler_params=pltpu.CompilerParams(vmem_limit_bytes=60 << 20),
    )(target, core, row_blocks, col_blocks, counts, masses)


def swap_sum(value, axis, size, bit):
    return value + lax.ppermute(value, axis, [(i, i ^ bit) for i in range(size)])


def per_device(blocks, plan, live, row_emb, col_emb, row_acc, col_acc):
    n_z = lax.axis_size("col")
    n_row_axis = GRID_X * GRID_Y * CORES
    dim, words = row_emb.shape
    padded = -(-dim // 16) * 16
    pad = ((0, padded - dim), (0, 0))
    row_blocks = lax.all_gather(jnp.pad(row_emb, pad), "col", axis=0)
    col_blocks = lax.all_gather(jnp.pad(col_emb, pad), ROW, axis=0)
    sub_rows, sub_cols = blocks.shape[5:]
    slots_each = blocks.shape[4]
    arrived = lax.all_to_all(
        blocks.reshape(-1, slots_each, sub_rows, sub_cols), ALL, split_axis=0, concat_axis=0, tiled=True
    ).reshape(-1, sub_rows, sub_cols)
    places = plan[0, 0]
    alive = lax.broadcasted_iota(jnp.int32, places.shape, 2) < live[0, 0][:, :, None]
    target = jnp.where(alive, places, places[:, :, :1]).reshape(-1)
    tile_rows, tile_cols = words * n_z, words * n_row_axis
    counts, part = place(
        target, alive.astype(jnp.int32).reshape(-1), arrived, tile_rows // sub_rows, tile_cols // sub_cols
    )
    n_col, n_row = tile_cols // LANES, tile_rows // LANES
    row_part = part[n_col:]
    for bit in (1, 2, 4):
        row_part = swap_sum(row_part, "col", n_z, bit)
    col_part = jnp.concatenate([part[:n_col], row_part[n_row:]], axis=0)
    col_part = swap_sum(col_part, "core", CORES, 1)
    for axis, size in (("y", GRID_Y), ("x", GRID_X)):
        for bit in (1, 2):
            col_part = swap_sum(col_part, axis, size, bit)
    masses = jnp.concatenate([col_part[:n_col], row_part[:n_row], col_part[n_col:]], axis=0)
    core = lax.axis_index("core").astype(jnp.int32)
    row_term, col_term = grads(target, core.reshape(1), row_blocks, col_blocks, counts, masses)
    row_grad = lax.psum_scatter(row_term, "col", scatter_dimension=0, tiled=False)
    half = col_term[0] + lax.ppermute(col_term[1], "core", [(0, 1), (1, 0)])
    col_grad = jnp.sum(lax.all_to_all(half, ("x", "y"), split_axis=0, concat_axis=0, tiled=True), axis=0)
    loss_scale = 4.0 * float(words * n_z * n_row_axis) ** (-0.5)
    row_share = row_grad[:dim] * loss_scale
    col_share = col_grad[:dim] * loss_scale
    new_row_acc = row_acc + row_share * row_share
    new_col_acc = col_acc + col_share * col_share
    new_row_emb = row_emb - LEARNING_RATE * row_share / jnp.sqrt(new_row_acc)
    new_col_emb = col_emb - LEARNING_RATE * col_share / jnp.sqrt(new_col_acc)
    return (new_row_emb, new_col_emb, new_row_acc, new_col_acc)


def solution(mesh):
    n_z = mesh.devices.shape[1]
    inner = Mesh(mesh.devices.reshape(GRID_X, GRID_Y, CORES, n_z), ROW + ("col",))
    row_words = P(None, ROW + ("col",))
    col_words = P(None, ("col",) + ROW)
    return jax.shard_map(
        per_device,
        mesh=inner,
        in_specs=(P(ROW, "col"), P(ROW, "col"), P(ROW, "col"), row_words, col_words, row_words, col_words),
        out_specs=(row_words, col_words, row_words, col_words),
        check_vma=False,
    )
```

time: 589 us -> 246 us (0.42); the launches traced: 581 us -> 246 us
  blocking collectives: 239 us -> 0 us
  matrix products: 88.9 us -> 0 us
  Pallas kernels: 0 us -> 60.4 us
  waiting for transfers between devices: 163 us -> 129 us
  other arithmetic: 37 us -> 6.71 us
  local copies, waits for them, and re-layouts: 29.9 us -> 8.5 us
  starting transfers between devices: 8.62 us -> 27.3 us
    psum x3 -> x0, blocking collectives: 205 us -> none  [the longest x1 115 us: per_device(): col_mass = lax.psum(col_part, 'row')]
    reduce_scatter x2 -> x1, waiting for transfers between devices: 111 us -> 20.6 us  [per_device(): lax.psum_scatter(row_term, 'col', scatter_dimension=0, tiled=False)]
    dot_general x6 -> x0, matrix products: 88.9 us -> none  [the longest x2 47.4 us: per_device(): lax.dot_general(vectors_part, col_block, (((0,), (0,)), ((), ())), precis...]
    pallas_call x0 -> x2, Pallas kernels: none -> 60.4 us  [the longest x1 52.6 us: grads(): pl.pallas_call(grad_kernel, name='tile_grads', grid_spec=pltpu.PrefetchSc...]
    all_to_all x1 -> x0, blocking collectives: 33.8 us -> none  [per_device(): lax.all_to_all(outgoing, 'row', split_axis=1, concat_axis=1, tiled=True)]
    ppermute x0 -> x9, waiting for transfers between devices: none -> 33.4 us  [the longest x8 28.5 us: swap_sum(): lax.ppermute(value, axis, [(i, i ^ bit) for i in range(size)])]
    all_to_all x1 -> x2, waiting for transfers between devices: 50.2 us -> 74.9 us  [the longest x1 63.2 us: per_device(): lax.all_to_all(blocks.reshape(-1, slots_each, sub_rows, sub_cols), ALL, s...]
    reduce_sum x2 -> x1, other arithmetic: 20.6 us -> 0.12 us  [per_device(): jnp.sum(lax.all_to_all(half, ('x', 'y'), split_axis=0, concat_axis=0, til...]
  transfers between devices with their start and end apart: 5 -> 14, of which waited for: 3 -> 12; matrix products, arithmetic and copies ran while one was open for 15% -> 3% of each run, Pallas kernels for 0% -> 3%
where the time goes in v1:
time: 246 us
  waiting for transfers between devices  129 us (52%)
  Pallas kernels  60.4 us (25%)
  starting transfers between devices  27.3 us (11%)
  between operations  13.9 us (6%)
  local copies, waits for them, and re-layouts  8.5 us (3%)
  other arithmetic  6.71 us (3%)
    all_to_all x1, waiting for transfers between devices, per_device(): lax.all_to_all(blocks.reshape(-1, slots_each, sub_rows, sub_cols), ALL, s...  63.2 us
    pallas_call x1, Pallas kernels, grads(): pl.pallas_call(grad_kernel, name='tile_grads', grid_spec=pltpu.PrefetchSc...  52.6 us
    ppermute x8, waiting for transfers between devices, swap_sum(): lax.ppermute(value, axis, [(i, i ^ bit) for i in range(size)])  28.5 us
    reduce_scatter x1, waiting for transfers between devices, per_device(): lax.psum_scatter(row_term, 'col', scatter_dimension=0, tiled=False)  20.6 us
    all_to_all x1, starting transfers between devices, per_device(): lax.all_to_all(blocks.reshape(-1, slots_each, sub_rows, sub_cols), ALL, s...  14.5 us
    all_to_all x1, waiting for transfers between devices, per_device(): lax.all_to_all(half, ('x', 'y'), split_axis=0, concat_axis=0, tiled=True)  11.7 us
    pallas_call x1, Pallas kernels, place(): pl.pallas_call(place_kernel, name='place_counts', grid_spec=pltpu.Prefetc...  7.79 us
    ppermute x8, starting transfers between devices, swap_sum(): lax.ppermute(value, axis, [(i, i ^ bit) for i in range(size)])  6.86 us
  transfers between devices with their start and end apart: 14, of which 12 were waited for; matrix products, arithmetic and copies ran while one was open for 3% of the time, Pallas kernels for 3%

profile of v1, /device:TPU:16, one launch (start us, length us, event | category | flops | bytes accessed | tf_op | source)
XLA Modules:
  0.0 245.7 jit_solution(16562980574455904674)
XLA Ops:
  7.2 1.6 pad.7
  8.9 1.6 pad.8
  10.5 14.5 %all-to-all-start = ((f32[256,2,8,128]{3,2,1,0:T(8,128)}), f32[256,2,8,128]{3,2,1,0:T(8,128)S(1)}, u32[]{:S(2)}, u32[]{:S(2)}) async-start(f32[256,2,8,128]{3,2,1,0:T(8,128)} %bitcast.23), calls=%async_computation | async-start | bytes 4194304 | tf_op jit(solution)/shard_map/all_to_all | solution.py:242
  25.9 63.2 %all-to-all-done = f32[256,2,8,128]{3,2,1,0:T(8,128)S(1)} async-done(((f32[256,2,8,128]{3,2,1,0:T(8,128)}), f32[256,2,8,128]{3,2,1,0:T(8,128)S(1)}, u32[]{:S(2)}, u32[]{:S(2)}) %all-to-all-start) | async-done | bytes 2097184 | tf_op jit(solution)/shard_map/all_to_all | solution.py:242
  89.1 7.8 %place_counts.1 = (f32[512,8,128]{2,1,0:T(8,128)S(1)}, f32[48,128]{1,0:T(8,128)S(1)}) custom-call(s32[512]{0:T(512)S(1)} %select_n.5.target, s32[512]{0:T(512)S(1)} %convert_element_type.7.alive, f32[512,8,128]{2,1,0:T(8,128)S(1)} %bitcast.21), custom_call_target="tpu_custom_call" | custom-call | tf_op jit(solution)/shard_map/place_counts/pallas_call | solution.py:68
  96.9 1.3 copy-done
  99.3 2.5 %collective-permute-done = f32[16,128]{1,0:T(8,128)S(1)} collective-permute-done((f32[16,128]{1,0:T(8,128)S(1)}, f32[16,128]{1,0:T(8,128)S(1)}, u32[]{:S(2)}, u32[]{:S(2)}) %collective-permute-start) | collective-permute-done | bytes 8224 | tf_op jit(solution)/shard_map/ppermute | solution.py:229
  102.3 4.1 %collective-permute-done.1 = f32[16,128]{1,0:T(8,128)S(1)} collective-permute-done((f32[16,128]{1,0:T(8,128)S(1)}, f32[16,128]{1,0:T(8,128)S(1)}, u32[]{:S(2)}, u32[]{:S(2)}) %collective-permute-start.1) | collective-permute-done | bytes 8224 | tf_op jit(solution)/shard_map/ppermute | solution.py:229
  106.9 7.1 %collective-permute-done.2 = f32[16,128]{1,0:T(8,128)S(1)} collective-permute-done((f32[16,128]{1,0:T(8,128)S(1)}, f32[16,128]{1,0:T(8,128)S(1)}, u32[]{:S(2)}, u32[]{:S(2)}) %collective-permute-start.2) | collective-permute-done | bytes 8224 | tf_op jit(solution)/shard_map/ppermute | solution.py:229
  114.1 1.2 collective-permute-done.3
  115.3 2.1 collective-permute-start.4
  117.3 1.9 collective-permute-done.4
  119.2 1.3 collective-permute-start.5
  120.5 4.0 %collective-permute-done.5 = f32[40,128]{1,0:T(8,128)S(1)} collective-permute-done((f32[40,128]{1,0:T(8,128)S(1)}, f32[40,128]{1,0:T(8,128)S(1)}, u32[]{:S(2)}, u32[]{:S(2)}) %collective-permute-start.5) | collective-permute-done | bytes 20512 | tf_op jit(solution)/shard_map/ppermute | solution.py:229
  125.1 3.3 %collective-permute-done.6 = f32[40,128]{1,0:T(8,128)S(1)} collective-permute-done((f32[40,128]{1,0:T(8,128)S(1)}, f32[40,128]{1,0:T(8,128)S(1)}, u32[]{:S(2)}, u32[]{:S(2)}) %collective-permute-start.6) | collective-permute-done | bytes 20512 | tf_op jit(solution)/shard_map/ppermute | solution.py:229
  129.2 4.4 %collective-permute-done.7 = f32[40,128]{1,0:T(8,128)S(1)} collective-permute-done((f32[40,128]{1,0:T(8,128)S(1)}, f32[40,128]{1,0:T(8,128)S(1)}, u32[]{:S(2)}, u32[]{:S(2)}) %collective-permute-start.7) | collective-permute-done | bytes 20512 | tf_op jit(solution)/shard_map/ppermute | solution.py:229
  134.2 52.6 %tile_grads.1 = (f32[8,304,128]{2,1,0:T(8,128)}, f32[2,16,304,128]{3,2,1,0:T(8,128)}) custom-call(s32[512]{0:T(512)} %copy-done.1, s32[1]{0:T(128)} %bitcast.3.core, f32[8,304,128]{2,1,0:T(8,128)} %bitcast.24, f32[32,304,128]{2,1,0:T(8,128)} %bitcast.22, f32[512,8,128]{2,1,0:T(8,128)} %copy-done, f32[48,128]{1,0:T(8,128)} %pad_maximum_fusion.masses), custom_call_target="tpu_custom_call" | custom-call | tf_op jit(solution)/shard_map/tile_grads/pallas_call | solution.py:202
  186.9 3.3 %slice_bitcast_fusion = f32[16,304,128]{2,1,0:T(8,128)} fusion(f32[2,16,304,128]{3,2,1,0:T(8,128)} %get-tuple-element.11), kind=kLoop, calls=%fused_computation.1 | loop fusion | bytes 4980736 | tf_op jit(solution)/shard_map/squeeze | solution.py:265
  190.2 4.9 %collective-permute-done.8 = f32[16,304,128]{2,1,0:T(8,128)S(1)} collective-permute-done((f32[16,304,128]{2,1,0:T(8,128)}, f32[16,304,128]{2,1,0:T(8,128)S(1)}, u32[]{:S(2)}, u32[]{:S(2)}) %collective-permute-start.8) | collective-permute-done | bytes 2490400 | tf_op jit(solution)/shard_map/ppermute | solution.py:265
  195.1 3.4 %bitcast_add_fusion = f32[16,304,128]{2,1,0:T(8,128)} fusion(f32[16,304,128]{2,1,0:T(8,128)S(1)} %collective-permute-done.8, f32[2,16,304,128]{3,2,1,0:T(8,128)} %get-tuple-element.11), kind=kLoop, calls=%fused_computation | loop fusion | flops 622592 | bytes 7471104 | tf_op jit(solution)/shard_map/add | solution.py:265
  198.5 5.8 %all-to-all-start.1 = ((f32[16,304,128]{2,1,0:T(8,128)}), f32[16,304,128]{2,1,0:T(8,128)S(1)}, u32[]{:S(2)}, u32[]{:S(2)}) async-start(f32[16,304,128]{2,1,0:T(8,128)} %bitcast_add_fusion), calls=%async_computation.2 | async-start | bytes 4980736 | tf_op jit(solution)/shard_map/all_to_all | solution.py:266
  204.3 20.6 %reduce-scatter.2.cloned.1.call-done = f32[1,304,128]{2,1,0:T(8,128)} async-done(((f32[8,304,128]{2,1,0:T(8,128)}), f32[1,304,128]{2,1,0:T(8,128)}) %reduce-scatter.2.cloned.1.call-update) | async-done | bytes 155664 | tf_op jit(solution)/shard_map/reduce_scatter | solution.py:264
  224.9 1.7 fusion
  226.6 11.7 %all-to-all-done.1 = f32[16,304,128]{2,1,0:T(8,128)S(1)} async-done(((f32[16,304,128]{2,1,0:T(8,128)}), f32[16,304,128]{2,1,0:T(8,128)S(1)}, u32[]{:S(2)}, u32[]{:S(2)}) %all-to-all-start.1) | async-done | bytes 2490400 | tf_op jit(solution)/shard_map/all_to_all | solution.py:266
  (56 shorter events, 6.1 us)
Async XLA Ops:
  7.2 127.1 %all-gather.5.cloned.1.call-start = ((), (), s32[]{:S(2)}) async-start(), calls=%async_computation.4 | async-start | bytes 1400832 | tf_op jit(solution)/shard_map/all_gather | solution.py:238
  8.8 16.3 %copy-start.6 = (s32[1,1,8,32,2]{3,4,2,1,0:T(2,128)S(1)}, s32[1,1,8,32,2]{3,4,2,1,0:T(2,128)}, u32[]{:S(2)}) copy-start(s32[1,1,8,32,2]{3,4,2,1,0:T(2,128)} %param.8) | copy-start | bytes 6148
  8.8 16.4 %copy-start.7 = (s32[1,1,8,32]{3,2,1,0:T(8,128)S(1)}, s32[1,1,8,32]{3,2,1,0:T(8,128)}, u32[]{:S(2)}) copy-start(s32[1,1,8,32]{3,2,1,0:T(8,128)} %param.9) | copy-start | bytes 3076
  8.8 125.4 %all-gather.7.cloned.1.call-start = ((), (), s32[]{:S(2)}) async-start(), calls=%async_computation.5 | async-start | bytes 5136384 | tf_op jit(solution)/shard_map/all_gather | solution.py:239
  10.5 78.6 %all-to-all-start = ((f32[256,2,8,128]{3,2,1,0:T(8,128)}), f32[256,2,8,128]{3,2,1,0:T(8,128)S(1)}, u32[]{:S(2)}, u32[]{:S(2)}) async-start(f32[256,2,8,128]{3,2,1,0:T(8,128)} %bitcast.23), calls=%async_computation | async-start | bytes 4194304 | tf_op jit(solution)/shard_map/all_to_all | solution.py:242
  25.0 199.9 %reduce-scatter.2.cloned.1.call-start = ((), (), s32[]{:S(2)}) async-start(), calls=%async_computation.3 | async-start | bytes 1400832 | tf_op jit(solution)/shard_map/reduce_scatter | solution.py:264
  25.9 108.4 %copy-start.1 = (s32[512]{0:T(512)}, s32[512]{0:T(512)S(1)}, u32[]{:S(2)}) copy-start(s32[512]{0:T(512)S(1)} %select_n.5.target) | copy-start | bytes 6148
  96.9 1.3 copy-start
  98.2 3.7 %collective-permute-start = (f32[16,128]{1,0:T(8,128)S(1)}, f32[16,128]{1,0:T(8,128)S(1)}, u32[]{:S(2)}, u32[]{:S(2)}) collective-permute-start(f32[16,128]{1,0:T(8,128)S(1)} %slice.36), channel_id=1, source_target_pairs={{0,1},{1,0},{2,3},{3,2},{4,5},{5,4},{6,7},{7,6},{8,9},{9,8},{10,11... | collective-permute-start | bytes 24584 | tf_op jit(solution)/shard_map/ppermute | solution.py:229
  101.9 4.5 %collective-permute-start.1 = (f32[16,128]{1,0:T(8,128)S(1)}, f32[16,128]{1,0:T(8,128)S(1)}, u32[]{:S(2)}, u32[]{:S(2)}) collective-permute-start(f32[16,128]{1,0:T(8,128)S(1)} %slice_add_fusion), channel_id=1, source_target_pairs={{0,2},{1,3},{2,0},{3,1},{4,6},{5,7},{6,4},{7,5},{8,10},{9,11},{10,... | collective-permute-start | bytes 24584 | tf_op jit(solution)/shard_map/ppermute | solution.py:229
  106.4 7.6 %collective-permute-start.2 = (f32[16,128]{1,0:T(8,128)S(1)}, f32[16,128]{1,0:T(8,128)S(1)}, u32[]{:S(2)}, u32[]{:S(2)}) collective-permute-start(f32[16,128]{1,0:T(8,128)S(1)} %add.40), channel_id=1, source_target_pairs={{0,4},{1,5},{2,6},{3,7},{4,0},{5,1},{6,2},{7,3},{8,12},{9,13},{10,... | collective-permute-start | bytes 24584 | tf_op jit(solution)/shard_map/ppermute | solution.py:229
  114.0 1.3 collective-permute-start.3
  115.3 4.0 %collective-permute-start.4 = (f32[40,128]{1,0:T(8,128)S(1)}, f32[40,128]{1,0:T(8,128)S(1)}, u32[]{:S(2)}, u32[]{:S(2)}) collective-permute-start(f32[40,128]{1,0:T(8,128)S(1)} %fusion.1), channel_id=1, source_target_pairs={{0,16},{16,0},{32,48},{48,32},{1,17},{17,1},{33,49},{49,33},{2,18}... | collective-permute-start | bytes 61448 | tf_op jit(solution)/shard_map/ppermute | solution.py:229
  119.2 5.3 %collective-permute-start.5 = (f32[40,128]{1,0:T(8,128)S(1)}, f32[40,128]{1,0:T(8,128)S(1)}, u32[]{:S(2)}, u32[]{:S(2)}) collective-permute-start(f32[40,128]{1,0:T(8,128)S(1)} %add.43), channel_id=1, source_target_pairs={{0,32},{16,48},{32,0},{48,16},{1,33},{17,49},{33,1},{49,17},{2,34}... | collective-permute-start | bytes 61448 | tf_op jit(solution)/shard_map/ppermute | solution.py:229
  124.5 3.8 %collective-permute-start.6 = (f32[40,128]{1,0:T(8,128)S(1)}, f32[40,128]{1,0:T(8,128)S(1)}, u32[]{:S(2)}, u32[]{:S(2)}) collective-permute-start(f32[40,128]{1,0:T(8,128)S(1)} %add.44), channel_id=1, source_target_pairs={{0,64},{64,0},{128,192},{192,128},{1,65},{65,1},{129,193},{193,129... | collective-permute-start | bytes 61448 | tf_op jit(solution)/shard_map/ppermute | solution.py:229
  128.3 5.3 %collective-permute-start.7 = (f32[40,128]{1,0:T(8,128)S(1)}, f32[40,128]{1,0:T(8,128)S(1)}, u32[]{:S(2)}, u32[]{:S(2)}) collective-permute-start(f32[40,128]{1,0:T(8,128)S(1)} %add.45), channel_id=1, source_target_pairs={{0,128},{64,192},{128,0},{192,64},{1,129},{65,193},{129,1},{193,65... | collective-permute-start | bytes 61448 | tf_op jit(solution)/shard_map/ppermute | solution.py:229
  190.2 4.9 %collective-permute-start.8 = (f32[16,304,128]{2,1,0:T(8,128)}, f32[16,304,128]{2,1,0:T(8,128)S(1)}, u32[]{:S(2)}, u32[]{:S(2)}) collective-permute-start(f32[16,304,128]{2,1,0:T(8,128)} %slice_bitcast_fusion), channel_id=1, source_target_pairs={{0,8},{8,0},{1,9},{9,1},{2,10},{10,2},{3,11},{11,3},{4,12},{12,4},... | collective-permute-start | bytes 7471112 | tf_op jit(solution)/shard_map/ppermute | solution.py:265
  198.5 26.4 %copy-start.2 = (f32[300,128]{1,0:T(8,128)S(1)}, f32[300,128]{1,0:T(8,128)}, u32[]{:S(2)}) copy-start(f32[300,128]{1,0:T(8,128)} %param.10) | copy-start | bytes 460804
  198.5 26.4 %copy-start.4 = (f32[300,128]{1,0:T(8,128)S(1)}, f32[300,128]{1,0:T(8,128)}, u32[]{:S(2)}) copy-start(f32[300,128]{1,0:T(8,128)} %param.12) | copy-start | bytes 460804
  198.5 39.7 %all-to-all-start.1 = ((f32[16,304,128]{2,1,0:T(8,128)}), f32[16,304,128]{2,1,0:T(8,128)S(1)}, u32[]{:S(2)}, u32[]{:S(2)}) async-start(f32[16,304,128]{2,1,0:T(8,128)} %bitcast_add_fusion), calls=%async_computation.2 | async-start | bytes 4980736 | tf_op jit(solution)/shard_map/all_to_all | solution.py:266
  204.3 34.1 %copy-start.3 = (f32[300,128]{1,0:T(8,128)S(1)}, f32[300,128]{1,0:T(8,128)}, u32[]{:S(2)}) copy-start(f32[300,128]{1,0:T(8,128)} %param.11) | copy-start | bytes 460804
  204.3 34.1 %copy-start.5 = (f32[300,128]{1,0:T(8,128)S(1)}, f32[300,128]{1,0:T(8,128)}, u32[]{:S(2)}) copy-start(f32[300,128]{1,0:T(8,128)} %param.13) | copy-start | bytes 460804
Sparse Core Ops, SparseCore 0:
  10.4 59.5 all-gather.4
  73.1 51.8 all-gather.6
  190.3 34.5 reduce-scatter.1

commit v2 on v1

v2 whole, which is shorter than its diff:
```python
import functools

import jax
import jax.numpy as jnp
from jax import lax
from jax.experimental import pallas as pl
from jax.experimental.pallas import tpu as pltpu
from jax.sharding import Mesh, PartitionSpec as P

LEARNING_RATE = 0.2
GRID_X, GRID_Y, CORES = 4, 4, 2
ROW = ("x", "y", "core")
ALL = ("col", "x", "y", "core")
LANES = 128
BLOCKS = 4
F32 = jnp.float32
BF16 = jnp.bfloat16


def split(value):
    high = value.astype(BF16)
    return high, (value - high.astype(F32)).astype(BF16)


def place_kernel(target, alive, arrived, counts_out, mass_out, dense, row_sums, col_sums):
    slots = arrived.shape[0]
    columns = col_sums.shape[0]
    shift = columns.bit_length() - 1
    row_words = row_sums.shape[0] // LANES * 8
    row_sums[...] = jnp.zeros(row_sums.shape, F32)
    col_sums[...] = jnp.zeros(col_sums.shape, F32)
    blank = jnp.zeros(arrived.shape[1:], F32)

    def clear(p, carry):
        dense[target[p]] = blank
        return carry

    lax.fori_loop(0, slots, clear, 0, unroll=8)

    def add(p, carry):
        place = target[p]
        value = jnp.where(alive[p] > 0, arrived[p], 0.0)
        row, column = lax.shift_right_logical(place, shift), place & (columns - 1)
        dense[place] = dense[place] + value
        row_sums[row] = row_sums[row] + value
        col_sums[column] = col_sums[column] + value
        return carry

    lax.fori_loop(0, slots, add, 0, unroll=8)

    def read(p, carry):
        counts_out[p] = dense[target[p]]
        return carry

    lax.fori_loop(0, slots, read, 0, unroll=8)
    col_part = jnp.sum(col_sums[...], axis=1)
    mass_out[0:columns, :] = col_part
    row_part = lax.dot_general(
        jnp.ones((8, LANES), F32),
        row_sums[...].reshape(-1, LANES),
        (((1,), (1,)), ((), ())),
        precision=lax.Precision.HIGHEST,
        preferred_element_type=F32,
    )
    for i in range(row_words):
        mass_out[columns + i : columns + i + 1, :] = row_part[0:1, i * LANES : (i + 1) * LANES]
    mass_out[columns + row_words :, :] = jnp.full((8, LANES), jnp.sum(col_part), F32)


def whole(count):
    return [pl.BlockSpec(memory_space=pltpu.VMEM)] * count


def place(target, alive, arrived, grid_rows, grid_columns):
    slots = arrived.shape[0]
    return pl.pallas_call(
        place_kernel,
        name="place_counts",
        grid_spec=pltpu.PrefetchScalarGridSpec(
            num_scalar_prefetch=2,
            grid=(1,),
            in_specs=whole(1),
            out_specs=whole(2),
            scratch_shapes=[
                pltpu.VMEM((grid_rows * grid_columns, 8, LANES), F32),
                pltpu.VMEM((grid_rows, 8, LANES), F32),
                pltpu.VMEM((grid_columns, 8, LANES), F32),
            ],
        ),
        out_shape=[
            jax.ShapeDtypeStruct((slots, 8, LANES), F32),
            jax.ShapeDtypeStruct((grid_columns + grid_rows * 8 // LANES + 8, LANES), F32),
        ],
        compiler_params=pltpu.CompilerParams(vmem_limit_bytes=22 << 20),
    )(target, alive, arrived)


def sort_kernel(target, order, offsets, cursor, *, columns):
    slots = target.shape[0]
    chunks = columns // BLOCKS
    mask = columns - 1
    low = BLOCKS.bit_length() - 1
    for k in range(chunks + 1):
        cursor[k] = 0

    def count(p, carry):
        k = lax.shift_right_logical(target[p] & mask, low)
        cursor[k] = cursor[k] + 1
        return carry

    lax.fori_loop(0, slots, count, 0, unroll=4)
    first = jnp.int32(0)
    for k in range(chunks):
        size = cursor[k]
        offsets[k] = first
        cursor[k] = first
        first = first + size
    offsets[chunks] = first

    def drop(p, carry):
        k = lax.shift_right_logical(target[p] & mask, low)
        at = cursor[k]
        order[at] = p
        cursor[k] = at + 1
        return carry

    lax.fori_loop(0, slots, drop, 0, unroll=4)


def sort_slots(target, columns):
    chunks = columns // BLOCKS
    smem = pl.BlockSpec(memory_space=pltpu.SMEM)
    return pl.pallas_call(
        functools.partial(sort_kernel, columns=columns),
        name="sort_slots",
        in_specs=[smem],
        out_specs=[smem, smem],
        out_shape=[
            jax.ShapeDtypeStruct(target.shape, jnp.int32),
            jax.ShapeDtypeStruct((chunks + 1,), jnp.int32),
        ],
        scratch_shapes=[pltpu.SMEM((chunks + 1,), jnp.int32)],
    )(target)


def taller(value, padded):
    return jnp.concatenate([value, jnp.zeros((padded - value.shape[0], LANES), F32)], axis=0)


def turn_kernel(row_blocks, row_stack, row_turned):
    padded = row_stack.shape[0] // 2
    deep = row_turned.shape[1]
    for i in range(row_blocks.shape[0]):
        high, low = split(taller(row_blocks[i], padded))
        here = slice(i * LANES, (i + 1) * LANES)
        row_stack[0:padded, here] = high
        row_stack[padded:, here] = low
        high32, low32 = high.astype(F32), low.astype(F32)
        tall = jnp.concatenate(
            [high32, high32, low32, jnp.zeros((deep - 3 * padded, LANES), F32)], axis=0
        )
        row_turned[here, :] = (0.5 * tall.T).astype(BF16)


def turn(row_blocks, padded, deep):
    words = row_blocks.shape[0] * LANES
    return pl.pallas_call(
        turn_kernel,
        name="turn_rows",
        in_specs=whole(1),
        out_specs=whole(2),
        out_shape=[
            jax.ShapeDtypeStruct((2 * padded, words), BF16),
            jax.ShapeDtypeStruct((words, deep), BF16),
        ],
        compiler_params=pltpu.CompilerParams(vmem_limit_bytes=24 << 20),
    )(row_blocks)


def score_kernel(row_turned, col_blocks, *rest):
    scores, col_stack, tall = rest[-3:]
    padded = col_stack.shape[0] // 2
    tall[3 * padded :, :] = jnp.zeros((tall.shape[0] - 3 * padded, tall.shape[1]), BF16)
    for k in range(BLOCKS):
        high, low = split(taller(col_blocks[k], padded))
        here = slice(k * LANES, (k + 1) * LANES)
        col_stack[0:padded, here] = high
        col_stack[padded:, here] = low
        tall[0:padded, here] = high
        tall[padded : 2 * padded, here] = low
        tall[2 * padded : 3 * padded, here] = high
    product = jnp.dot(row_turned[...], tall[...], preferred_element_type=F32)
    for k in range(BLOCKS):
        scores[:, k] = product[:, k * LANES : (k + 1) * LANES].reshape(-1, 8, LANES)


def score(row_turned, col_blocks, padded, first, count, earlier):
    words, deep = row_turned.shape
    n_col, dim, _ = col_blocks.shape
    width = BLOCKS * LANES
    ready = [] if earlier is None else list(earlier)
    return pl.pallas_call(
        score_kernel,
        name="score_piece",
        grid_spec=pltpu.PrefetchScalarGridSpec(
            num_scalar_prefetch=0,
            grid=(count,),
            in_specs=[
                pl.BlockSpec((words, deep), lambda g: (0, 0)),
                pl.BlockSpec((BLOCKS, dim, LANES), lambda g: (first + g, 0, 0)),
            ]
            + [pl.BlockSpec(memory_space=pltpu.HBM)] * len(ready),
            out_specs=[
                pl.BlockSpec((words // 8, BLOCKS, 8, LANES), lambda g: (0, first + g, 0, 0)),
                pl.BlockSpec((2 * padded, width), lambda g: (0, first + g)),
            ],
            scratch_shapes=[pltpu.VMEM((deep, width), BF16)],
        ),
        out_shape=[
            pltpu.HBM((words // 8, n_col, 8, LANES), F32),
            pltpu.HBM((2 * padded, n_col * LANES), BF16),
        ],
        input_output_aliases={2: 0, 3: 1} if ready else {},
        compiler_params=pltpu.CompilerParams(vmem_limit_bytes=24 << 20),
    )(row_turned, pltpu.with_memory_space_constraint(col_blocks, pltpu.HBM), *ready)


def grad_kernel(
    target, order, offsets, core, scores, counts, masses, row_stack,
    own, other, high_out, low_out,
    grads, row_bias, col_bias,
):
    ct = pl.program_id(0)
    n_col = col_bias.shape[0]
    n_row = row_stack.shape[1] // LANES
    padded = row_stack.shape[0] // 2
    shift = n_col.bit_length() - 1

    @pl.when(ct == 0)
    def _():
        log_total = jnp.log(masses[n_col + n_row : n_col + n_row + 1, :])
        col_bias[...] = 0.5 * (jnp.log(masses[0:n_col, :]) - log_total)
        row_logs = 0.5 * jnp.log(masses[n_col : n_col + n_row, :])
        for i in range(n_row):
            turned = jnp.broadcast_to(row_logs[i : i + 1, :], (LANES, LANES)).T
            row_bias[i * LANES // 8 : (i + 1) * LANES // 8] = turned.reshape(-1, 8, LANES)

    for k in range(BLOCKS):
        near = col_bias[pl.ds(ct * BLOCKS + k, 1), :]
        grads[:, k] = 0.5 * jnp.tanh(scores[:, k] + row_bias[...] + near) + 0.5
    begin = offsets[ct]
    end = offsets[ct + 1]

    def counted(step, carry):
        found = []
        for u in range(8):
            p = order[jnp.minimum(begin + step * 8 + u, end - 1)]
            place = target[p]
            row = lax.shift_right_logical(place, shift)
            column = place & (n_col - 1)
            k = column & (BLOCKS - 1)
            count = counts[p]
            score = scores[row, k] + row_bias[row] + col_bias[pl.ds(column, 1), :]
            fresh = (0.1 + 0.25 * jnp.sqrt(count)) * (2.0 * score - jnp.log(count))
            found.append((row, k, fresh))
        for row, k, fresh in found:
            grads[row, k] = fresh
        return carry

    lax.fori_loop(0, lax.shift_right_logical(end - begin + 7, 3), counted, 0)
    for k in range(BLOCKS):
        here = slice(k * LANES, (k + 1) * LANES)
        high, low = split(grads[:, k].reshape(-1, LANES))
        high_out[:, here] = high
        low_out[:, here] = low
    both = jnp.dot(row_stack[...], high_out[...], preferred_element_type=F32)
    rest = jnp.dot(row_stack[0:padded, :], low_out[...], preferred_element_type=F32)
    total = both[0:padded] + both[padded:] + rest
    parts = [total[:, k * LANES : (k + 1) * LANES] for k in range(BLOCKS)]
    mine = core[0] == 0
    for k in range(0, BLOCKS, 2):
        own[k // 2] = jnp.where(mine, parts[k], parts[k + 1])
        other[k // 2] = jnp.where(mine, parts[k + 1], parts[k])


def col_grads(target, order, offsets, core, scores, counts, masses, row_stack):
    grid_rows, n_col = scores.shape[:2]
    padded = row_stack.shape[0] // 2
    words = grid_rows * 8
    width = BLOCKS * LANES
    halves = BLOCKS // CORES
    term = jax.ShapeDtypeStruct((n_col // CORES, padded, LANES), F32)
    wide = pltpu.HBM((words, n_col * LANES), BF16)
    return pl.pallas_call(
        grad_kernel,
        name="col_grads",
        grid_spec=pltpu.PrefetchScalarGridSpec(
            num_scalar_prefetch=4,
            grid=(n_col // BLOCKS,),
            in_specs=[pl.BlockSpec((grid_rows, BLOCKS, 8, LANES), lambda g, *_: (0, g, 0, 0))] + whole(3),
            out_specs=[
                pl.BlockSpec((halves, padded, LANES), lambda g, *_: (g, 0, 0)),
                pl.BlockSpec((halves, padded, LANES), lambda g, *_: (g, 0, 0)),
                pl.BlockSpec((words, width), lambda g, *_: (0, g)),
                pl.BlockSpec((words, width), lambda g, *_: (0, g)),
            ],
            scratch_shapes=[
                pltpu.VMEM((grid_rows, BLOCKS, 8, LANES), F32),
                pltpu.VMEM((grid_rows, 8, LANES), F32),
                pltpu.VMEM((n_col, LANES), F32),
            ],
        ),
        out_shape=[term, term, wide, wide],
        compiler_params=pltpu.CompilerParams(vmem_limit_bytes=26 << 20),
    )(target, order, offsets, core, pltpu.with_memory_space_constraint(scores, pltpu.HBM), counts, masses, row_stack)


def row_kernel(col_stack, high, low, row_term):
    padded = col_stack.shape[0] // 2

    @pl.when(pl.program_id(0) == 0)
    def _():
        row_term[...] = jnp.zeros(row_term.shape, F32)

    turned = (((1,), (1,)), ((), ()))
    both = lax.dot_general(col_stack[...], high[...], turned, preferred_element_type=F32)
    rest = lax.dot_general(col_stack[0:padded, :], low[...], turned, preferred_element_type=F32)
    total = both[0:padded] + both[padded:] + rest
    for i in range(row_term.shape[0]):
        row_term[i] = row_term[i] + total[:, i * LANES : (i + 1) * LANES]


def row_grads(col_stack, high, low):
    words, n_words = high.shape
    width = BLOCKS * LANES
    padded = col_stack.shape[0] // 2
    return pl.pallas_call(
        row_kernel,
        name="row_grads",
        grid=(n_words // width,),
        in_specs=[
            pl.BlockSpec((2 * padded, width), lambda g: (0, g)),
            pl.BlockSpec((words, width), lambda g: (0, g)),
            pl.BlockSpec((words, width), lambda g: (0, g)),
        ],
        out_specs=pl.BlockSpec((words // LANES, padded, LANES), lambda g: (0, 0, 0)),
        out_shape=jax.ShapeDtypeStruct((words // LANES, padded, LANES), F32),
        compiler_params=pltpu.CompilerParams(vmem_limit_bytes=32 << 20),
    )(*(pltpu.with_memory_space_constraint(value, pltpu.HBM) for value in (col_stack, high, low)))


def swap_sum(value, axis, size, bit):
    return value + lax.ppermute(value, axis, [(i, i ^ bit) for i in range(size)])


def per_device(blocks, plan, live, row_emb, col_emb, row_acc, col_acc):
    n_z = lax.axis_size("col")
    n_row_axis = GRID_X * GRID_Y * CORES
    dim, words = row_emb.shape
    padded = -(-dim // 16) * 16
    deep = -(-3 * padded // 256) * 256
    col_blocks = lax.all_gather(col_emb, ROW, axis=0)
    row_emb_late, col_blocks = lax.optimization_barrier((row_emb, col_blocks))
    row_blocks = lax.all_gather(row_emb_late, "col", axis=0)
    sub_rows, sub_cols = blocks.shape[5:]
    slots_each = blocks.shape[4]
    arrived = lax.all_to_all(
        blocks.reshape(-1, slots_each, sub_rows, sub_cols), ALL, split_axis=0, concat_axis=0, tiled=True
    ).reshape(-1, sub_rows, sub_cols)
    places = plan[0, 0]
    alive = lax.broadcasted_iota(jnp.int32, places.shape, 2) < live[0, 0][:, :, None]
    target = jnp.where(alive, places, places[:, :, :1]).reshape(-1)
    tile_rows, tile_cols = words * n_z, words * n_row_axis
    n_col, n_row = tile_cols // LANES, tile_rows // LANES
    order, offsets = sort_slots(target, n_col)
    target, order, offsets = lax.optimization_barrier((target, order, offsets))
    counts, part = place(
        target, alive.astype(jnp.int32).reshape(-1), arrived, tile_rows // sub_rows, n_col
    )
    row_part = part[n_col:]
    for bit in (1, 2, 4):
        row_part = swap_sum(row_part, "col", n_z, bit)
    col_part = jnp.concatenate([part[:n_col], row_part[n_row:]], axis=0)
    col_part, row_blocks = lax.optimization_barrier((col_part, row_blocks))
    row_stack, row_turned = turn(row_blocks, padded, deep)
    col_part = swap_sum(col_part, "core", CORES, 1)
    scored = None
    first = 0
    chunks = n_col // BLOCKS
    for axis, bit in (("y", 1), ("y", 2), ("x", 1), ("x", 2)):
        col_part, row_turned = lax.optimization_barrier((col_part, row_turned))
        col_part = swap_sum(col_part, axis, GRID_X, bit)
        scored = score(row_turned, col_blocks, padded, first, chunks // 4, scored)
        col_part, scored = lax.optimization_barrier((col_part, scored))
        first += chunks // 4
    scores, col_stack = scored
    masses = jnp.concatenate([col_part[:n_col], row_part[:n_row], col_part[n_col:]], axis=0)
    core = lax.axis_index("core").astype(jnp.int32).reshape(1)
    own, other, high, low = col_grads(target, order, offsets, core, scores, counts, masses, row_stack)
    swapped = lax.ppermute(other, "core", [(0, 1), (1, 0)])
    row_term = row_grads(col_stack, high, low)
    row_grad = lax.psum_scatter(row_term, "col", scatter_dimension=0, tiled=False)
    half = own + swapped
    col_grad = jnp.sum(lax.all_to_all(half, ("x", "y"), split_axis=0, concat_axis=0, tiled=True), axis=0)
    loss_scale = 4.0 * float(words * n_z * n_row_axis) ** (-0.5)
    row_share = row_grad[:dim] * loss_scale
    col_share = col_grad[:dim] * loss_scale
    new_row_acc = row_acc + row_share * row_share
    new_col_acc = col_acc + col_share * col_share
    new_row_emb = row_emb - LEARNING_RATE * row_share / jnp.sqrt(new_row_acc)
    new_col_emb = col_emb - LEARNING_RATE * col_share / jnp.sqrt(new_col_acc)
    return (new_row_emb, new_col_emb, new_row_acc, new_col_acc)


def solution(mesh):
    n_z = mesh.devices.shape[1]
    inner = Mesh(mesh.devices.reshape(GRID_X, GRID_Y, CORES, n_z), ROW + ("col",))
    row_words = P(None, ROW + ("col",))
    col_words = P(None, ("col",) + ROW)
    return jax.shard_map(
        per_device,
        mesh=inner,
        in_specs=(P(ROW, "col"), P(ROW, "col"), P(ROW, "col"), row_words, col_words, row_words, col_words),
        out_specs=(row_words, col_words, row_words, col_words),
        check_vma=False,
    )
```

time: 246 us -> 233 us (0.947)
  waiting for transfers between devices: 129 us -> 101 us
  Pallas kernels: 60.4 us -> 70.2 us
  starting transfers between devices: 27.3 us -> 36.4 us
  local copies, waits for them, and re-layouts: 8.5 us -> 4.02 us
    all_to_all x1, waiting for transfers between devices: 63.2 us -> 0.01 us  [per_device(): lax.all_to_all(blocks.reshape(-1, slots_each, sub_rows, sub_cols), ALL, s...]
    all_gather x2, waiting for transfers between devices: 0.01 us -> 59 us  [the longest x1 50.9 us: per_device(): col_blocks = lax.all_gather(col_emb, ROW, axis=0)]
    ppermute x8, waiting for transfers between devices: 28.5 us -> 7.26 us  [swap_sum(): lax.ppermute(value, axis, [(i, i ^ bit) for i in range(size)])]
    pallas_call x1 -> x8, Pallas kernels: 52.6 us -> 64.6 us  [the longest x4 22.1 us: score(): pl.pallas_call(score_kernel, name='score_piece', grid_spec=pltpu.Prefetch...]
    ppermute x8, starting transfers between devices: 6.86 us -> 15.3 us  [swap_sum(): lax.ppermute(value, axis, [(i, i ^ bit) for i in range(size)])]
    reduce_scatter x1, waiting for transfers between devices: 20.6 us -> 26.1 us  [per_device(): lax.psum_scatter(row_term, 'col', scatter_dimension=0, tiled=False)]
    ppermute x1, waiting for transfers between devices: 4.91 us -> 0.01 us  [per_device(): swapped = lax.ppermute(other, 'core', [(0, 1), (1, 0)])]
    all_to_all x1, waiting for transfers between devices: 11.7 us -> 7.58 us  [per_device(): lax.all_to_all(half, ('x', 'y'), split_axis=0, concat_axis=0, tiled=True)]
  transfers between devices with their start and end apart: 14 -> 14, of which waited for: 12 -> 7; matrix products, arithmetic and copies ran while one was open for 3% -> 3% of each run, Pallas kernels for 3% -> 21%
where the time goes in v2:
time: 233 us; the launch traced here: 232 us
  waiting for transfers between devices  101 us (43%)
  Pallas kernels  70.2 us (30%)
  starting transfers between devices  36.4 us (16%)
  between operations  14 us (6%)
  other arithmetic  6.75 us (3%)
  local copies, waits for them, and re-layouts  4.02 us (2%)
    all_gather x1, waiting for transfers between devices, per_device(): col_blocks = lax.all_gather(col_emb, ROW, axis=0)  50.9 us
    reduce_scatter x1, waiting for transfers between devices, per_device(): lax.psum_scatter(row_term, 'col', scatter_dimension=0, tiled=False)  26.1 us
    pallas_call x4, Pallas kernels, score(): pl.pallas_call(score_kernel, name='score_piece', grid_spec=pltpu.Prefetch...  22.1 us
    pallas_call x1, Pallas kernels, col_grads(): pl.pallas_call(grad_kernel, name='col_grads', grid_spec=pltpu.PrefetchSca...  20.5 us
    ppermute x8, starting transfers between devices, swap_sum(): lax.ppermute(value, axis, [(i, i ^ bit) for i in range(size)])  15.3 us
    all_to_all x1, starting transfers between devices, per_device(): lax.all_to_all(blocks.reshape(-1, slots_each, sub_rows, sub_cols), ALL, s...  14.5 us
    pallas_call x1, Pallas kernels, row_grads(): pl.pallas_call(row_kernel, name='row_grads', grid=(n_words // width,), in...  14.3 us
    all_gather x1, waiting for transfers between devices, per_device(): row_blocks = lax.all_gather(row_emb_late, 'col', axis=0)  8.11 us
  transfers between devices with their start and end apart: 14, of which 7 were waited for; matrix products, arithmetic and copies ran while one was open for 3% of the time, Pallas kernels for 21%

profile of v2, /device:TPU:16, one launch (start us, length us, event | category | flops | bytes accessed | tf_op | source)
XLA Modules:
  0.0 232.1 jit_solution(17755439568717572602)
XLA Ops:
  7.9 14.5 %all-to-all-start = ((f32[256,2,8,128]{3,2,1,0:T(8,128)}), f32[256,2,8,128]{3,2,1,0:T(8,128)S(1)}, u32[]{:S(2)}, u32[]{:S(2)}) async-start(f32[256,2,8,128]{3,2,1,0:T(8,128)} %bitcast.18), calls=%async_computation | async-start | bytes 4194304 | tf_op jit(solution)/shard_map/all_to_all | solution.py:367
  22.5 50.9 %all-gather.7.cloned.1.call-done.col_blocks = f32[32,300,128]{2,1,0:T(8,128)} async-done(((f32[1,300,128]{2,1,0:T(8,128)}), f32[32,300,128]{2,1,0:T(8,128)}) %all-gather.7.cloned.1.call-update) | async-done | bytes 4915216 | tf_op jit(solution)/shard_map/all_gather | solution.py:362
  74.8 7.0 %sort_slots.1 = (s32[512]{0:T(512)}, s32[9]{0:T(128)}) custom-call(s32[512]{0:T(512)} %select_n.5.target), custom_call_target="tpu_custom_call" | custom-call | tf_op jit(solution)/shard_map/sort_slots/pallas_call | solution.py:133
  82.6 5.6 %place_counts.1 = (f32[512,8,128]{2,1,0:T(8,128)S(1)}, f32[48,128]{1,0:T(8,128)S(1)}) custom-call(s32[512]{0:T(512)S(1)} %copy-done.5, s32[512]{0:T(512)S(1)} %convert_element_type.4.alive, f32[512,8,128]{2,1,0:T(8,128)S(1)} %bitcast.17), custom_call_target="tpu_custom_call" | custom-call | tf_op jit(solution)/shard_map/place_counts/pallas_call | solution.py:76
  88.2 1.3 copy-done
  90.7 2.4 %collective-permute-done = f32[16,128]{1,0:T(8,128)S(1)} collective-permute-done((f32[16,128]{1,0:T(8,128)S(1)}, f32[16,128]{1,0:T(8,128)S(1)}, u32[]{:S(2)}, u32[]{:S(2)}) %collective-permute-start) | collective-permute-done | bytes 8224 | tf_op jit(solution)/shard_map/ppermute | solution.py:353
  93.1 2.4 %collective-permute-start.1 = (f32[16,128]{1,0:T(8,128)S(1)}, f32[16,128]{1,0:T(8,128)S(1)}, u32[]{:S(2)}, u32[]{:S(2)}) collective-permute-start(f32[16,128]{1,0:T(8,128)S(1)} %slice_add_fusion), channel_id=1, source_target_pairs={{0,2},{1,3},{2,0},{3,1},{4,6},{5,7},{6,4},{7,5},{8,10},{9,11},{10,... | collective-permute-start | bytes 24584 | tf_op jit(solution)/shard_map/ppermute | solution.py:353
  95.5 2.2 collective-permute-done.1
  97.7 5.1 %collective-permute-start.2 = (f32[16,128]{1,0:T(8,128)S(1)}, f32[16,128]{1,0:T(8,128)S(1)}, u32[]{:S(2)}, u32[]{:S(2)}) collective-permute-start(f32[16,128]{1,0:T(8,128)S(1)} %add.36), channel_id=1, source_target_pairs={{0,4},{1,5},{2,6},{3,7},{4,0},{5,1},{6,2},{7,3},{8,12},{9,13},{10,... | collective-permute-start | bytes 24584 | tf_op jit(solution)/shard_map/ppermute | solution.py:353
  102.8 2.6 %collective-permute-done.2 = f32[16,128]{1,0:T(8,128)S(1)} collective-permute-done((f32[16,128]{1,0:T(8,128)S(1)}, f32[16,128]{1,0:T(8,128)S(1)}, u32[]{:S(2)}, u32[]{:S(2)}) %collective-permute-start.2) | collective-permute-done | bytes 8224 | tf_op jit(solution)/shard_map/ppermute | solution.py:353
  105.4 8.1 %all-gather.9.cloned.1.call-done.row_blocks = f32[8,300,128]{2,1,0:T(8,128)} async-done(((f32[1,300,128]{2,1,0:T(8,128)}), f32[8,300,128]{2,1,0:T(8,128)}) %all-gather.9.cloned.1.call-update) | async-done | bytes 1228816 | tf_op jit(solution)/shard_map/all_gather | solution.py:364
  116.9 5.5 %score_piece.4 = (f32[128,32,8,128]{3,2,1,0:T(8,128)}, bf16[608,4096]{1,0:T(8,128)(2,1)}) custom-call(bf16[1024,1024]{1,0:T(8,128)(2,1)S(1)} %get-tuple-element.78.row_turned, f32[32,300,128]{2,1,0:T(8,128)} %all-gather.7.cloned.1.call-done.col_blocks), custom_call_target="tpu_custom_call" | custom-call | tf_op jit(solution)/shard_map/score_piece/pallas_call | solution.py:202
  123.3 5.5 %score_piece.5 = (f32[128,32,8,128]{3,2,1,0:T(8,128)}, bf16[608,4096]{1,0:T(8,128)(2,1)}) custom-call(bf16[1024,1024]{1,0:T(8,128)(2,1)S(1)} %get-tuple-element.78.row_turned, f32[32,300,128]{2,1,0:T(8,128)} %all-gather.7.cloned.1.call-done.col_blocks, f32[128,32,8,128]{3,2,1,0:T(8,128)} %get-tuple-element.65.rest_0_, ...), custom_call_target="tpu_custom_call", output_to_operand_aliasing={{0}: (2, {}), {1}: (3, {})} | custom-call | tf_op jit(solution)/shard_map/score_piece/pallas_call | solution.py:202
  128.8 1.5 collective-permute-start.6
  130.3 5.5 %score_piece.6 = (f32[128,32,8,128]{3,2,1,0:T(8,128)}, bf16[608,4096]{1,0:T(8,128)(2,1)}) custom-call(bf16[1024,1024]{1,0:T(8,128)(2,1)S(1)} %get-tuple-element.78.row_turned, f32[32,300,128]{2,1,0:T(8,128)} %all-gather.7.cloned.1.call-done.col_blocks, f32[128,32,8,128]{3,2,1,0:T(8,128)} %get-tuple-element.72.rest_0_, ...), custom_call_target="tpu_custom_call", output_to_operand_aliasing={{0}: (2, {}), {1}: (3, {})} | custom-call | tf_op jit(solution)/shard_map/score_piece/pallas_call | solution.py:202
  135.8 2.9 %collective-permute-start.7 = (f32[40,128]{1,0:T(8,128)S(1)}, f32[40,128]{1,0:T(8,128)S(1)}, u32[]{:S(2)}, u32[]{:S(2)}) collective-permute-start(f32[40,128]{1,0:T(8,128)S(1)} %add.41), channel_id=1, source_target_pairs={{0,128},{64,192},{128,0},{192,64},{1,129},{65,193},{129,1},{193,65... | collective-permute-start | bytes 61448 | tf_op jit(solution)/shard_map/ppermute | solution.py:353
  138.8 5.6 %score_piece.7 = (f32[128,32,8,128]{3,2,1,0:T(8,128)}, bf16[608,4096]{1,0:T(8,128)(2,1)}) custom-call(bf16[1024,1024]{1,0:T(8,128)(2,1)S(1)} %get-tuple-element.78.row_turned, f32[32,300,128]{2,1,0:T(8,128)} %all-gather.7.cloned.1.call-done.col_blocks, f32[128,32,8,128]{3,2,1,0:T(8,128)} %get-tuple-element.79.rest_0_, ...), custom_call_target="tpu_custom_call", output_to_operand_aliasing={{0}: (2, {}), {1}: (3, {})} | custom-call | tf_op jit(solution)/shard_map/score_piece/pallas_call | solution.py:202
  144.5 20.5 %col_grads.1 = (f32[16,304,128]{2,1,0:T(8,128)S(1)}, f32[16,304,128]{2,1,0:T(8,128)}, bf16[1024,4096]{1,0:T(8,128)(2,1)}, bf16[1024,4096]{1,0:T(8,128)(2,1)}) custom-call(s32[512]{0:T(512)S(1)} %copy-done.6, s32[512]{0:T(512)S(1)} %copy-done.7, s32[9]{0:T(128)S(1)} %copy-done.8, s32[1]{0:T(128)} %bitcast.7.core, ...), custom_call_target="tpu_custom_call" | custom-call | tf_op jit(solution)/shard_map/col_grads/pallas_call | solution.py:294
  165.0 14.3 %row_grads.1 = f32[8,304,128]{2,1,0:T(8,128)} custom-call(bf16[608,4096]{1,0:T(8,128)(2,1)} %get-tuple-element.83.col_stack, bf16[1024,4096]{1,0:T(8,128)(2,1)} %get-tuple-element.90.high, bf16[1024,4096]{1,0:T(8,128)(2,1)} %get-tuple-element.91.low), custom_call_target="tpu_custom_call" | custom-call | tf_op jit(solution)/shard_map/row_grads/pallas_call | solution.py:337
  179.3 3.5 %add.44 = f32[16,304,128]{2,1,0:T(8,128)} add(f32[16,304,128]{2,1,0:T(8,128)S(1)} %get-tuple-element.92, f32[16,304,128]{2,1,0:T(8,128)} %collective-permute-done.8) | non-fusion elementwise | flops 622592 | bytes 7471104 | tf_op jit(solution)/shard_map/add | solution.py:403
  182.8 6.5 %all-to-all-start.1 = ((f32[16,304,128]{2,1,0:T(8,128)}), f32[16,304,128]{2,1,0:T(8,128)S(1)}, u32[]{:S(2)}, u32[]{:S(2)}) async-start(f32[16,304,128]{2,1,0:T(8,128)} %add.44), calls=%async_computation.2 | async-start | bytes 4980736 | tf_op jit(solution)/shard_map/all_to_all | solution.py:404
  189.3 26.1 %reduce-scatter.2.cloned.1.call-done = f32[1,304,128]{2,1,0:T(8,128)} async-done(((f32[8,304,128]{2,1,0:T(8,128)}), f32[1,304,128]{2,1,0:T(8,128)}) %reduce-scatter.2.cloned.1.call-update) | async-done | bytes 155664 | tf_op jit(solution)/shard_map/reduce_scatter | solution.py:402
  215.4 1.7 fusion
  217.1 7.6 %all-to-all-done.1 = f32[16,304,128]{2,1,0:T(8,128)S(1)} async-done(((f32[16,304,128]{2,1,0:T(8,128)}), f32[16,304,128]{2,1,0:T(8,128)S(1)}, u32[]{:S(2)}, u32[]{:S(2)}) %all-to-all-start.1) | async-done | bytes 2490400 | tf_op jit(solution)/shard_map/all_to_all | solution.py:404
  (74 shorter events, 9.3 us)
Async XLA Ops:
  7.2 66.3 %copy-start.14 = (s32[1,1,8,32]{3,2,1,0:T(8,128)S(1)}, s32[1,1,8,32]{3,2,1,0:T(8,128)}, u32[]{:S(2)}) copy-start(s32[1,1,8,32]{3,2,1,0:T(8,128)} %param.9) | copy-start | bytes 3076
  7.2 66.5 %copy-start.13 = (s32[1,1,8,32,2]{3,4,2,1,0:T(2,128)S(1)}, s32[1,1,8,32,2]{3,4,2,1,0:T(2,128)}, u32[]{:S(2)}) copy-start(s32[1,1,8,32,2]{3,4,2,1,0:T(2,128)} %param.8) | copy-start | bytes 6148
  7.2 66.2 %all-gather.7.cloned.1.call-start = ((), (), s32[]{:S(2)}) async-start(), calls=%async_computation.4 | async-start | bytes 5136384 | tf_op jit(solution)/shard_map/all_gather | solution.py:362
  7.9 73.9 %all-to-all-start = ((f32[256,2,8,128]{3,2,1,0:T(8,128)}), f32[256,2,8,128]{3,2,1,0:T(8,128)S(1)}, u32[]{:S(2)}, u32[]{:S(2)}) async-start(f32[256,2,8,128]{3,2,1,0:T(8,128)} %bitcast.18), calls=%async_computation | async-start | bytes 4194304 | tf_op jit(solution)/shard_map/all_to_all | solution.py:367
  22.4 91.1 %all-gather.9.cloned.1.call-start = ((), (), s32[]{:S(2)}) async-start(), calls=%async_computation.5 | async-start | bytes 1400832 | tf_op jit(solution)/shard_map/all_gather | solution.py:364
  73.4 142.0 %reduce-scatter.2.cloned.1.call-start = ((), (), s32[]{:S(2)}) async-start(), calls=%async_computation.3 | async-start | bytes 1400832 | tf_op jit(solution)/shard_map/reduce_scatter | solution.py:402
  89.5 3.7 %collective-permute-start = (f32[16,128]{1,0:T(8,128)S(1)}, f32[16,128]{1,0:T(8,128)S(1)}, u32[]{:S(2)}, u32[]{:S(2)}) collective-permute-start(f32[16,128]{1,0:T(8,128)S(1)} %slice.30), channel_id=1, source_target_pairs={{0,1},{1,0},{2,3},{3,2},{4,5},{5,4},{6,7},{7,6},{8,9},{9,8},{10,11... | collective-permute-start | bytes 24584 | tf_op jit(solution)/shard_map/ppermute | solution.py:353
  93.1 4.6 %collective-permute-start.1 = (f32[16,128]{1,0:T(8,128)S(1)}, f32[16,128]{1,0:T(8,128)S(1)}, u32[]{:S(2)}, u32[]{:S(2)}) collective-permute-start(f32[16,128]{1,0:T(8,128)S(1)} %slice_add_fusion), channel_id=1, source_target_pairs={{0,2},{1,3},{2,0},{3,1},{4,6},{5,7},{6,4},{7,5},{8,10},{9,11},{10,... | collective-permute-start | bytes 24584 | tf_op jit(solution)/shard_map/ppermute | solution.py:353
  97.7 7.7 %collective-permute-start.2 = (f32[16,128]{1,0:T(8,128)S(1)}, f32[16,128]{1,0:T(8,128)S(1)}, u32[]{:S(2)}, u32[]{:S(2)}) collective-permute-start(f32[16,128]{1,0:T(8,128)S(1)} %add.36), channel_id=1, source_target_pairs={{0,4},{1,5},{2,6},{3,7},{4,0},{5,1},{6,2},{7,3},{8,12},{9,13},{10,... | collective-permute-start | bytes 24584 | tf_op jit(solution)/shard_map/ppermute | solution.py:353
  113.5 2.0 collective-permute-start.3
  115.6 6.8 %copy-start.2 = (bf16[608,1024]{1,0:T(8,128)(2,1)}, bf16[608,1024]{1,0:T(8,128)(2,1)S(1)}, u32[]{:S(2)}) copy-start(bf16[608,1024]{1,0:T(8,128)(2,1)S(1)} %get-tuple-element.89.row_stack) | copy-start | bytes 3735556
  115.6 6.8 %collective-permute-start.4 = (f32[40,128]{1,0:T(8,128)S(1)}, f32[40,128]{1,0:T(8,128)S(1)}, u32[]{:S(2)}, u32[]{:S(2)}) collective-permute-start(f32[40,128]{1,0:T(8,128)S(1)} %add.38), channel_id=1, source_target_pairs={{0,16},{16,0},{32,48},{48,32},{1,17},{17,1},{33,49},{49,33},{2,18}... | collective-permute-start | bytes 61448 | tf_op jit(solution)/shard_map/ppermute | solution.py:353
  122.4 6.4 %collective-permute-start.5 = (f32[40,128]{1,0:T(8,128)S(1)}, f32[40,128]{1,0:T(8,128)S(1)}, u32[]{:S(2)}, u32[]{:S(2)}) collective-permute-start(f32[40,128]{1,0:T(8,128)S(1)} %add.39), channel_id=1, source_target_pairs={{0,32},{16,48},{32,0},{48,16},{1,33},{17,49},{33,1},{49,17},{2,34}... | collective-permute-start | bytes 61448 | tf_op jit(solution)/shard_map/ppermute | solution.py:353
  128.8 7.0 %collective-permute-start.6 = (f32[40,128]{1,0:T(8,128)S(1)}, f32[40,128]{1,0:T(8,128)S(1)}, u32[]{:S(2)}, u32[]{:S(2)}) collective-permute-start(f32[40,128]{1,0:T(8,128)S(1)} %add.40), channel_id=1, source_target_pairs={{0,64},{64,0},{128,192},{192,128},{1,65},{65,1},{129,193},{193,129... | collective-permute-start | bytes 61448 | tf_op jit(solution)/shard_map/ppermute | solution.py:353
  135.8 8.6 %collective-permute-start.7 = (f32[40,128]{1,0:T(8,128)S(1)}, f32[40,128]{1,0:T(8,128)S(1)}, u32[]{:S(2)}, u32[]{:S(2)}) collective-permute-start(f32[40,128]{1,0:T(8,128)S(1)} %add.41), channel_id=1, source_target_pairs={{0,128},{64,192},{128,0},{192,64},{1,129},{65,193},{129,1},{193,65... | collective-permute-start | bytes 61448 | tf_op jit(solution)/shard_map/ppermute | solution.py:353
  138.8 5.7 %copy-start.6 = (s32[512]{0:T(512)S(1)}, s32[512]{0:T(512)}, u32[]{:S(2)}) copy-start(s32[512]{0:T(512)} %select_n.5.target) | copy-start | bytes 6148
  138.8 5.7 %copy-start.7 = (s32[512]{0:T(512)S(1)}, s32[512]{0:T(512)}, u32[]{:S(2)}) copy-start(s32[512]{0:T(512)} %get-tuple-element.84.order) | copy-start | bytes 6148
  138.8 5.7 %copy-start.8 = (s32[9]{0:T(128)S(1)}, s32[9]{0:T(128)}, u32[]{:S(2)}) copy-start(s32[9]{0:T(128)} %get-tuple-element.85.offsets) | copy-start | bytes 112
  165.0 14.3 %collective-permute-start.8 = (f32[16,304,128]{2,1,0:T(8,128)}, f32[16,304,128]{2,1,0:T(8,128)}, u32[]{:S(2)}, u32[]{:S(2)}) collective-permute-start(f32[16,304,128]{2,1,0:T(8,128)} %get-tuple-element.93), channel_id=1, source_target_pairs={{0,8},{8,0},{1,9},{9,1},{2,10},{10,2},{3,11},{11,3},{4,12},{12,4},... | collective-permute-start | bytes 7471112 | tf_op jit(solution)/shard_map/ppermute | solution.py:400
  182.8 32.6 %copy-start.9 = (f32[300,128]{1,0:T(8,128)S(1)}, f32[300,128]{1,0:T(8,128)}, u32[]{:S(2)}) copy-start(f32[300,128]{1,0:T(8,128)} %param.10) | copy-start | bytes 460804
  182.8 32.6 %copy-start.11 = (f32[300,128]{1,0:T(8,128)S(1)}, f32[300,128]{1,0:T(8,128)}, u32[]{:S(2)}) copy-start(f32[300,128]{1,0:T(8,128)} %param.12) | copy-start | bytes 460804
  182.8 41.8 %all-to-all-start.1 = ((f32[16,304,128]{2,1,0:T(8,128)}), f32[16,304,128]{2,1,0:T(8,128)S(1)}, u32[]{:S(2)}, u32[]{:S(2)}) async-start(f32[16,304,128]{2,1,0:T(8,128)} %add.44), calls=%async_computation.2 | async-start | bytes 4980736 | tf_op jit(solution)/shard_map/all_to_all | solution.py:404
  189.3 35.5 %copy-start.10 = (f32[300,128]{1,0:T(8,128)S(1)}, f32[300,128]{1,0:T(8,128)}, u32[]{:S(2)}) copy-start(f32[300,128]{1,0:T(8,128)} %param.11) | copy-start | bytes 460804
  189.3 35.5 %copy-start.12 = (f32[300,128]{1,0:T(8,128)S(1)}, f32[300,128]{1,0:T(8,128)}, u32[]{:S(2)}) copy-start(f32[300,128]{1,0:T(8,128)} %param.13) | copy-start | bytes 460804
  (5 other events, 14.7 us)
Sparse Core Ops, SparseCore 0:
  10.6 62.7 all-gather.6
  75.2 38.3 all-gather.8
  179.5 35.8 reduce-scatter.1

commit v3 on v2

v3 whole, which is shorter than its diff:
```python
import functools

import jax
import jax.numpy as jnp
from jax import lax
from jax.experimental import pallas as pl
from jax.experimental.pallas import tpu as pltpu
from jax.sharding import Mesh, PartitionSpec as P

LEARNING_RATE = 0.2
GRID_X, GRID_Y, CORES = 4, 4, 2
ROW = ("x", "y", "core")
ALL = ("col", "x", "y", "core")
LANES = 128
BLOCKS = 4
F32 = jnp.float32
BF16 = jnp.bfloat16


def split(value):
    high = value.astype(BF16)
    return high, (value - high.astype(F32)).astype(BF16)


def place_kernel(target, alive, arrived, counts_out, mass_out, dense, row_sums, col_sums):
    slots = arrived.shape[0]
    columns = col_sums.shape[0]
    shift = columns.bit_length() - 1
    row_words = row_sums.shape[0] // LANES * 8
    row_sums[...] = jnp.zeros(row_sums.shape, F32)
    col_sums[...] = jnp.zeros(col_sums.shape, F32)
    blank = jnp.zeros(arrived.shape[1:], F32)

    def clear(p, carry):
        dense[target[p]] = blank
        return carry

    lax.fori_loop(0, slots, clear, 0, unroll=8)

    def add(p, carry):
        place = target[p]
        value = jnp.where(alive[p] > 0, arrived[p], 0.0)
        row, column = lax.shift_right_logical(place, shift), place & (columns - 1)
        dense[place] = dense[place] + value
        row_sums[row] = row_sums[row] + value
        col_sums[column] = col_sums[column] + value
        return carry

    lax.fori_loop(0, slots, add, 0, unroll=8)

    def read(p, carry):
        counts_out[p] = dense[target[p]]
        return carry

    lax.fori_loop(0, slots, read, 0, unroll=8)
    col_part = jnp.sum(col_sums[...], axis=1)
    mass_out[0:columns, :] = col_part
    row_part = lax.dot_general(
        jnp.ones((8, LANES), F32),
        row_sums[...].reshape(-1, LANES),
        (((1,), (1,)), ((), ())),
        precision=lax.Precision.HIGHEST,
        preferred_element_type=F32,
    )
    for i in range(row_words):
        mass_out[columns + i : columns + i + 1, :] = row_part[0:1, i * LANES : (i + 1) * LANES]
    mass_out[columns + row_words :, :] = jnp.full((8, LANES), jnp.sum(col_part), F32)


def whole(count):
    return [pl.BlockSpec(memory_space=pltpu.VMEM)] * count


def place(target, alive, arrived, grid_rows, grid_columns):
    slots = arrived.shape[0]
    return pl.pallas_call(
        place_kernel,
        name="place_counts",
        grid_spec=pltpu.PrefetchScalarGridSpec(
            num_scalar_prefetch=2,
            grid=(1,),
            in_specs=whole(1),
            out_specs=whole(2),
            scratch_shapes=[
                pltpu.VMEM((grid_rows * grid_columns, 8, LANES), F32),
                pltpu.VMEM((grid_rows, 8, LANES), F32),
                pltpu.VMEM((grid_columns, 8, LANES), F32),
            ],
        ),
        out_shape=[
            jax.ShapeDtypeStruct((slots, 8, LANES), F32),
            jax.ShapeDtypeStruct((grid_columns + grid_rows * 8 // LANES + 8, LANES), F32),
        ],
        compiler_params=pltpu.CompilerParams(vmem_limit_bytes=22 << 20),
    )(target, alive, arrived)


def chunk_of(place, core, columns):
    column = place & (columns - 1)
    seat = lax.shift_right_logical(column, 1)
    far = (column & 1) ^ core
    chunk = (1 - far) * (columns // 2 // BLOCKS) + lax.shift_right_logical(seat, BLOCKS.bit_length() - 1)
    return chunk, seat & (BLOCKS - 1), column


def sort_kernel(target, core, order, offsets, cursor, *, columns):
    slots = target.shape[0]
    chunks = columns // BLOCKS
    for k in range(chunks + 1):
        cursor[k] = 0

    def count(p, carry):
        k = chunk_of(target[p], core[0], columns)[0]
        cursor[k] = cursor[k] + 1
        return carry

    lax.fori_loop(0, slots, count, 0, unroll=4)
    first = jnp.int32(0)
    for k in range(chunks):
        size = cursor[k]
        offsets[k] = first
        cursor[k] = first
        first = first + size
    offsets[chunks] = first

    def drop(p, carry):
        k = chunk_of(target[p], core[0], columns)[0]
        at = cursor[k]
        order[at] = p
        cursor[k] = at + 1
        return carry

    lax.fori_loop(0, slots, drop, 0, unroll=4)


def sort_slots(target, core, columns):
    chunks = columns // BLOCKS
    smem = pl.BlockSpec(memory_space=pltpu.SMEM)
    return pl.pallas_call(
        functools.partial(sort_kernel, columns=columns),
        name="sort_slots",
        in_specs=[smem, smem],
        out_specs=[smem, smem],
        out_shape=[
            jax.ShapeDtypeStruct(target.shape, jnp.int32),
            jax.ShapeDtypeStruct((chunks + 1,), jnp.int32),
        ],
        scratch_shapes=[pltpu.SMEM((chunks + 1,), jnp.int32)],
    )(target, core)


def taller(value, padded):
    return jnp.concatenate([value, jnp.zeros((padded - value.shape[0], LANES), F32)], axis=0)


def turn_kernel(row_blocks, row_stack, row_turned):
    padded = row_stack.shape[0] // 2
    deep = row_turned.shape[1]
    for i in range(row_blocks.shape[0]):
        high, low = split(taller(row_blocks[i], padded))
        here = slice(i * LANES, (i + 1) * LANES)
        row_stack[0:padded, here] = high
        row_stack[padded:, here] = low
        high32, low32 = high.astype(F32), low.astype(F32)
        tall = jnp.concatenate(
            [high32, high32, low32, jnp.zeros((deep - 3 * padded, LANES), F32)], axis=0
        )
        row_turned[here, :] = (0.5 * tall.T).astype(BF16)


def turn(row_blocks, padded, deep):
    words = row_blocks.shape[0] * LANES
    return pl.pallas_call(
        turn_kernel,
        name="turn_rows",
        in_specs=whole(1),
        out_specs=whole(2),
        out_shape=[
            jax.ShapeDtypeStruct((2 * padded, words), BF16),
            jax.ShapeDtypeStruct((words, deep), BF16),
        ],
        compiler_params=pltpu.CompilerParams(vmem_limit_bytes=24 << 20),
    )(row_blocks)


def stack_kernel(core, col_blocks, far, near):
    pairs = col_blocks.shape[0] // CORES
    deep = far.shape[0]
    dim = -(-col_blocks.shape[1] // 16) * 16
    mine = core[0] == 0
    for i in range(pairs):
        first, second = col_blocks[2 * i], col_blocks[2 * i + 1]
        here = slice(i * LANES, (i + 1) * LANES)
        for out, value in ((far, jnp.where(mine, second, first)), (near, jnp.where(mine, first, second))):
            high, low = split(taller(value, dim))
            out[0:dim, here] = high
            out[dim : 2 * dim, here] = low
            out[2 * dim : 3 * dim, here] = high
            out[3 * dim :, here] = jnp.zeros((deep - 3 * dim, LANES), BF16)


def stack_cols(core, col_blocks, deep):
    n_col, dim, _ = col_blocks.shape
    half = pltpu.HBM((deep, n_col // CORES * LANES), BF16)
    out = pl.BlockSpec((deep, BLOCKS * LANES), lambda g, *_: (0, g))
    return pl.pallas_call(
        stack_kernel,
        name="stack_columns",
        grid_spec=pltpu.PrefetchScalarGridSpec(
            num_scalar_prefetch=1,
            grid=(n_col // BLOCKS // CORES,),
            in_specs=[pl.BlockSpec((BLOCKS * CORES, dim, LANES), lambda g, *_: (g, 0, 0))],
            out_specs=[out, out],
        ),
        out_shape=[half, half],
        compiler_params=pltpu.CompilerParams(vmem_limit_bytes=14 << 20),
    )(core, pltpu.with_memory_space_constraint(col_blocks, pltpu.HBM))


def part_kernel(
    target, order, offsets, core, row_turned, row_stack, col_stack, counts, masses, *rest, near
):
    col_term, row_term, scores, grads, row_bias, col_bias = rest[-6:]
    padded, n_row = row_term.shape[1], row_term.shape[0]
    n_col = col_bias.shape[0]
    ct = pl.program_id(0)
    chunks = pl.num_programs(0)
    shift = n_col.bit_length() - 1
    side = core[0] if near else 1 - core[0]

    @pl.when(ct == 0)
    def _():
        log_total = jnp.log(masses[n_col + n_row : n_col + n_row + 1, :])
        col_bias[...] = 0.5 * (jnp.log(masses[0:n_col, :]) - log_total)
        row_logs = 0.5 * jnp.log(masses[n_col : n_col + n_row, :])
        for i in range(n_row):
            turned = jnp.broadcast_to(row_logs[i : i + 1, :], (LANES, LANES)).T
            row_bias[i * LANES // 8 : (i + 1) * LANES // 8] = turned.reshape(-1, 8, LANES)
        row_term[...] = rest[0][...] if near else jnp.zeros(row_term.shape, F32)

    product = jnp.dot(row_turned[...], col_stack[...], preferred_element_type=F32)
    for k in range(BLOCKS):
        bias = col_bias[pl.ds((ct * BLOCKS + k) * 2 + side, 1), :]
        value = product[:, k * LANES : (k + 1) * LANES].reshape(-1, 8, LANES) + row_bias[...] + bias
        scores[:, k] = value
        grads[:, k] = 0.5 * jnp.tanh(value) + 0.5
    at = ct + (chunks if near else 0)
    begin = offsets[at]
    end = offsets[at + 1]

    def counted(step, carry):
        found = []
        for u in range(8):
            p = order[jnp.minimum(begin + step * 8 + u, end - 1)]
            place = target[p]
            row = lax.shift_right_logical(place, shift)
            k = lax.shift_right_logical(place & (n_col - 1), 1) & (BLOCKS - 1)
            count = counts[p]
            fresh = (0.1 + 0.25 * jnp.sqrt(count)) * (2.0 * scores[row, k] - jnp.log(count))
            found.append((row, k, fresh))
        for row, k, fresh in found:
            grads[row, k] = fresh
        return carry

    lax.fori_loop(0, lax.shift_right_logical(end - begin + 7, 3), counted, 0)
    pieces = [split(grads[:, k].reshape(-1, LANES)) for k in range(BLOCKS)]
    high = jnp.concatenate([piece[0] for piece in pieces], axis=1)
    low = jnp.concatenate([piece[1] for piece in pieces], axis=1)
    both = jnp.dot(row_stack[...], high, preferred_element_type=F32)
    rest_ = jnp.dot(row_stack[0:padded, :], low, preferred_element_type=F32)
    total = both[0:padded] + both[padded:] + rest_
    for k in range(BLOCKS):
        col_term[k] = total[:, k * LANES : (k + 1) * LANES]
    turned = (((1,), (1,)), ((), ()))
    both = lax.dot_general(col_stack[0 : 2 * padded, :], high, turned, preferred_element_type=F32)
    rest_ = lax.dot_general(col_stack[0:padded, :], low, turned, preferred_element_type=F32)
    total = both[0:padded] + both[padded:] + rest_
    for i in range(n_row):
        row_term[i] = row_term[i] + total[:, i * LANES : (i + 1) * LANES]


def part_grads(scalars, row_turned, row_stack, col_stack, counts, masses, earlier):
    words, deep = row_turned.shape
    padded = row_stack.shape[0] // 2
    blocks = col_stack.shape[1] // LANES
    near = earlier is not None
    ready = [earlier] if near else []
    return pl.pallas_call(
        functools.partial(part_kernel, near=near),
        name="near_grads" if near else "far_grads",
        grid_spec=pltpu.PrefetchScalarGridSpec(
            num_scalar_prefetch=4,
            grid=(blocks // BLOCKS,),
            in_specs=whole(2)
            + [pl.BlockSpec((deep, BLOCKS * LANES), lambda g, *_: (0, g))]
            + whole(2 + len(ready)),
            out_specs=[pl.BlockSpec((BLOCKS, padded, LANES), lambda g, *_: (g, 0, 0))] + whole(1),
            scratch_shapes=[
                pltpu.VMEM((words // 8, BLOCKS, 8, LANES), F32),
                pltpu.VMEM((words // 8, BLOCKS, 8, LANES), F32),
                pltpu.VMEM((words // 8, 8, LANES), F32),
                pltpu.VMEM((blocks * CORES, LANES), F32),
            ],
        ),
        out_shape=[
            jax.ShapeDtypeStruct((blocks, padded, LANES), F32),
            jax.ShapeDtypeStruct((words // LANES, padded, LANES), F32),
        ],
        compiler_params=pltpu.CompilerParams(vmem_limit_bytes=36 << 20),
    )(*scalars, row_turned, row_stack, pltpu.with_memory_space_constraint(col_stack, pltpu.HBM), counts, masses, *ready)


def swap_sum(value, axis, size, bit):
    return value + lax.ppermute(value, axis, [(i, i ^ bit) for i in range(size)])


def per_device(blocks, plan, live, row_emb, col_emb, row_acc, col_acc):
    n_z = lax.axis_size("col")
    n_row_axis = GRID_X * GRID_Y * CORES
    dim, words = row_emb.shape
    padded = -(-dim // 16) * 16
    deep = -(-3 * padded // 256) * 256
    core = lax.axis_index("core").astype(jnp.int32).reshape(1)
    places = plan[0, 0]
    alive = lax.broadcasted_iota(jnp.int32, places.shape, 2) < live[0, 0][:, :, None]
    target = jnp.where(alive, places, places[:, :, :1]).reshape(-1)
    tile_rows, tile_cols = words * n_z, words * n_row_axis
    n_col, n_row = tile_cols // LANES, tile_rows // LANES
    order, offsets = sort_slots(target, core, n_col)
    col_blocks = lax.all_gather(col_emb, ROW, axis=0)
    row_emb_late, col_blocks, order, offsets = lax.optimization_barrier((row_emb, col_blocks, order, offsets))
    row_blocks = lax.all_gather(row_emb_late, "col", axis=0)
    sub_rows, sub_cols = blocks.shape[5:]
    slots_each = blocks.shape[4]
    arrived = lax.all_to_all(
        blocks.reshape(-1, slots_each, sub_rows, sub_cols), ALL, split_axis=0, concat_axis=0, tiled=True
    ).reshape(-1, sub_rows, sub_cols)
    counts, part = place(
        target, alive.astype(jnp.int32).reshape(-1), arrived, tile_rows // sub_rows, n_col
    )
    row_part = part[n_col:]
    row_part = swap_sum(row_part, "col", n_z, 1)
    row_part = swap_sum(row_part, "col", n_z, 2)
    row_part, core = lax.optimization_barrier((row_part, core))
    far_stack, near_stack = stack_cols(core, col_blocks, deep)
    row_part = swap_sum(row_part, "col", n_z, 4)
    row_part, far_stack, near_stack = lax.optimization_barrier((row_part, far_stack, near_stack))
    col_part = jnp.concatenate([part[:n_col], row_part[n_row:]], axis=0)
    col_part = swap_sum(col_part, "core", CORES, 1)
    for axis, bit in (("y", 1), ("y", 2), ("x", 1)):
        col_part = swap_sum(col_part, axis, GRID_X, bit)
    col_part, row_blocks = lax.optimization_barrier((col_part, row_blocks))
    row_stack, row_turned = turn(row_blocks, padded, deep)
    col_part = swap_sum(col_part, "x", GRID_X, 2)
    masses = jnp.concatenate([col_part[:n_col], row_part[:n_row], col_part[n_col:]], axis=0)
    scalars = (target, order, offsets, core)
    far_term, row_term = part_grads(scalars, row_turned, row_stack, far_stack, counts, masses, None)
    swapped = lax.ppermute(far_term, "core", [(0, 1), (1, 0)])
    near_term, row_term = part_grads(scalars, row_turned, row_stack, near_stack, counts, masses, row_term)
    row_grad = lax.psum_scatter(row_term, "col", scatter_dimension=0, tiled=False)
    half = near_term + swapped
    col_grad = jnp.sum(lax.all_to_all(half, ("x", "y"), split_axis=0, concat_axis=0, tiled=True), axis=0)
    loss_scale = 4.0 * float(words * n_z * n_row_axis) ** (-0.5)
    row_share = row_grad[:dim] * loss_scale
    col_share = col_grad[:dim] * loss_scale
    new_row_acc = row_acc + row_share * row_share
    new_col_acc = col_acc + col_share * col_share
    new_row_emb = row_emb - LEARNING_RATE * row_share / jnp.sqrt(new_row_acc)
    new_col_emb = col_emb - LEARNING_RATE * col_share / jnp.sqrt(new_col_acc)
    return (new_row_emb, new_col_emb, new_row_acc, new_col_acc)


def solution(mesh):
    n_z = mesh.devices.shape[1]
    inner = Mesh(mesh.devices.reshape(GRID_X, GRID_Y, CORES, n_z), ROW + ("col",))
    row_words = P(None, ROW + ("col",))
    col_words = P(None, ("col",) + ROW)
    return jax.shard_map(
        per_device,
        mesh=inner,
        in_specs=(P(ROW, "col"), P(ROW, "col"), P(ROW, "col"), row_words, col_words, row_words, col_words),
        out_specs=(row_words, col_words, row_words, col_words),
        check_vma=False,
    )
```

time: 233 us -> 215 us (0.923)
  Pallas kernels: 70.2 us -> 55.9 us
  starting transfers between devices: 36.4 us -> 31.6 us
    ppermute x8, waiting for transfers between devices: 7.26 us -> 22.5 us  [swap_sum(): lax.ppermute(value, axis, [(i, i ^ bit) for i in range(size)])]
    pallas_call x6 -> x3, Pallas kernels: 56.9 us -> 42.1 us  [the longest x2 35.3 us: part_grads(): pl.pallas_call(functools.partial(part_kernel, near=near), name='near_grad...]
    all_gather x1, waiting for transfers between devices: 50.9 us -> 42 us  [per_device(): col_blocks = lax.all_gather(col_emb, ROW, axis=0)]
    all_gather x1, waiting for transfers between devices: 8.11 us -> 0.01 us  [per_device(): row_blocks = lax.all_gather(row_emb_late, 'col', axis=0)]
    ppermute x8, starting transfers between devices: 15.3 us -> 11 us  [swap_sum(): lax.ppermute(value, axis, [(i, i ^ bit) for i in range(size)])]
    unnamed x31 -> x29, local copies, waits for them, and re-layouts: 3.48 us -> 4.79 us
  transfers between devices with their start and end apart: 14 -> 14, of which waited for: 7 -> 12; matrix products, arithmetic and copies ran while one was open for 3% -> 3% of each run, Pallas kernels for 21% -> 18%
where the time goes in v3:
time: 215 us; the launch traced here: 214 us
  waiting for transfers between devices  100 us (47%)
  Pallas kernels  55.9 us (26%)
  starting transfers between devices  31.6 us (15%)
  between operations  14 us (7%)
  other arithmetic  6.8 us (3%)
  local copies, waits for them, and re-layouts  5.33 us (2%)
    all_gather x1, waiting for transfers between devices, per_device(): col_blocks = lax.all_gather(col_emb, ROW, axis=0)  42 us
    pallas_call x2, Pallas kernels, part_grads(): pl.pallas_call(functools.partial(part_kernel, near=near), name='near_grad...  35.3 us
    reduce_scatter x1, waiting for transfers between devices, per_device(): lax.psum_scatter(row_term, 'col', scatter_dimension=0, tiled=False)  27.6 us
    ppermute x8, waiting for transfers between devices, swap_sum(): lax.ppermute(value, axis, [(i, i ^ bit) for i in range(size)])  22.5 us
    all_to_all x1, starting transfers between devices, per_device(): lax.all_to_all(blocks.reshape(-1, slots_each, sub_rows, sub_cols), ALL, s...  14.5 us
    ppermute x8, starting transfers between devices, swap_sum(): lax.ppermute(value, axis, [(i, i ^ bit) for i in range(size)])  11 us
    pallas_call x1, Pallas kernels, sort_slots(): pl.pallas_call(functools.partial(sort_kernel, columns=columns), name='sor...  7.49 us
    pallas_call x1, Pallas kernels, stack_cols(): pl.pallas_call(stack_kernel, name='stack_columns', grid_spec=pltpu.Prefet...  6.77 us
  transfers between devices with their start and end apart: 14, of which 12 were waited for; matrix products, arithmetic and copies ran while one was open for 3% of the time, Pallas kernels for 18%

profile of v3, /device:TPU:16, one launch (start us, length us, event | category | flops | bytes accessed | tf_op | source)
XLA Modules:
  0.0 213.7 jit_solution(6808881825572801777)
XLA Ops:
  7.9 14.5 %all-to-all-start = ((f32[256,2,8,128]{3,2,1,0:T(8,128)}), f32[256,2,8,128]{3,2,1,0:T(8,128)S(1)}, u32[]{:S(2)}, u32[]{:S(2)}) async-start(f32[256,2,8,128]{3,2,1,0:T(8,128)} %bitcast.18), calls=%async_computation | async-start | bytes 4194304 | tf_op jit(solution)/shard_map/all_to_all | solution.py:335
  23.9 7.5 %sort_slots.1 = (s32[512]{0:T(512)}, s32[9]{0:T(128)}) custom-call(s32[512]{0:T(512)} %select_n.5.target, s32[1]{0:T(128)} %bitcast.4.core), custom_call_target="tpu_custom_call" | custom-call | tf_op jit(solution)/shard_map/sort_slots/pallas_call | solution.py:139
  31.4 42.0 %all-gather.7.cloned.1.call-done.col_blocks = f32[32,300,128]{2,1,0:T(8,128)} async-done(((f32[1,300,128]{2,1,0:T(8,128)}), f32[32,300,128]{2,1,0:T(8,128)}) %all-gather.7.cloned.1.call-update) | async-done | bytes 4915216 | tf_op jit(solution)/shard_map/all_gather | solution.py:330
  73.4 1.6 all-to-all-done
  75.7 5.6 %place_counts.1 = (f32[512,8,128]{2,1,0:T(8,128)S(1)}, f32[48,128]{1,0:T(8,128)S(1)}) custom-call(s32[512]{0:T(512)S(1)} %copy-done.4, s32[512]{0:T(512)S(1)} %convert_element_type.4.alive, f32[512,8,128]{2,1,0:T(8,128)S(1)} %bitcast.17), custom_call_target="tpu_custom_call" | custom-call | tf_op jit(solution)/shard_map/place_counts/pallas_call | solution.py:76
  82.6 2.4 %collective-permute-done = f32[16,128]{1,0:T(8,128)S(1)} collective-permute-done((f32[16,128]{1,0:T(8,128)S(1)}, f32[16,128]{1,0:T(8,128)S(1)}, u32[]{:S(2)}, u32[]{:S(2)}) %collective-permute-start) | collective-permute-done | bytes 8224 | tf_op jit(solution)/shard_map/ppermute | solution.py:314
  85.9 3.7 %collective-permute-done.1 = f32[16,128]{1,0:T(8,128)S(1)} collective-permute-done((f32[16,128]{1,0:T(8,128)S(1)}, f32[16,128]{1,0:T(8,128)S(1)}, u32[]{:S(2)}, u32[]{:S(2)}) %collective-permute-start.1) | collective-permute-done | bytes 8224 | tf_op jit(solution)/shard_map/ppermute | solution.py:314
  89.6 3.5 %collective-permute-start.2 = (f32[16,128]{1,0:T(8,128)S(1)}, f32[16,128]{1,0:T(8,128)S(1)}, u32[]{:S(2)}, u32[]{:S(2)}) collective-permute-start(f32[16,128]{1,0:T(8,128)S(1)} %add.36), channel_id=1, source_target_pairs={{0,4},{1,5},{2,6},{3,7},{4,0},{5,1},{6,2},{7,3},{8,12},{9,13},{10,... | collective-permute-start | bytes 24584 | tf_op jit(solution)/shard_map/ppermute | solution.py:314
  93.1 4.1 %collective-permute-done.2 = f32[16,128]{1,0:T(8,128)S(1)} collective-permute-done((f32[16,128]{1,0:T(8,128)S(1)}, f32[16,128]{1,0:T(8,128)S(1)}, u32[]{:S(2)}, u32[]{:S(2)}) %collective-permute-start.2) | collective-permute-done | bytes 8224 | tf_op jit(solution)/shard_map/ppermute | solution.py:314
  97.2 6.8 %stack_columns.1 = (bf16[1024,2048]{1,0:T(8,128)(2,1)}, bf16[1024,2048]{1,0:T(8,128)(2,1)}) custom-call(s32[1]{0:T(128)} %bitcast.4.core, f32[32,300,128]{2,1,0:T(8,128)} %all-gather.7.cloned.1.call-done.col_blocks), custom_call_target="tpu_custom_call" | custom-call | tf_op jit(solution)/shard_map/stack_columns/pallas_call | solution.py:206
  105.3 2.2 %collective-permute-start.4 = (f32[40,128]{1,0:T(8,128)S(1)}, f32[40,128]{1,0:T(8,128)S(1)}, u32[]{:S(2)}, u32[]{:S(2)}) collective-permute-start(f32[40,128]{1,0:T(8,128)S(1)} %fusion.1), channel_id=1, source_target_pairs={{0,16},{16,0},{32,48},{48,32},{1,17},{17,1},{33,49},{49,33},{2,18}... | collective-permute-start | bytes 61448 | tf_op jit(solution)/shard_map/ppermute | solution.py:314
  107.5 1.8 collective-permute-done.4
  109.2 1.7 collective-permute-start.5
  110.9 3.6 %collective-permute-done.5 = f32[40,128]{1,0:T(8,128)S(1)} collective-permute-done((f32[40,128]{1,0:T(8,128)S(1)}, f32[40,128]{1,0:T(8,128)S(1)}, u32[]{:S(2)}, u32[]{:S(2)}) %collective-permute-start.5) | collective-permute-done | bytes 20512 | tf_op jit(solution)/shard_map/ppermute | solution.py:314
  115.1 3.2 %collective-permute-done.6 = f32[40,128]{1,0:T(8,128)S(1)} collective-permute-done((f32[40,128]{1,0:T(8,128)S(1)}, f32[40,128]{1,0:T(8,128)S(1)}, u32[]{:S(2)}, u32[]{:S(2)}) %collective-permute-start.6) | collective-permute-done | bytes 20512 | tf_op jit(solution)/shard_map/ppermute | solution.py:314
  121.0 2.6 %collective-permute-done.7 = f32[40,128]{1,0:T(8,128)S(1)} collective-permute-done((f32[40,128]{1,0:T(8,128)S(1)}, f32[40,128]{1,0:T(8,128)S(1)}, u32[]{:S(2)}, u32[]{:S(2)}) %collective-permute-start.7) | collective-permute-done | bytes 20512 | tf_op jit(solution)/shard_map/ppermute | solution.py:314
  123.7 1.6 copy-done.1
  125.3 17.7 %far_grads.1 = (f32[16,304,128]{2,1,0:T(8,128)}, f32[8,304,128]{2,1,0:T(8,128)S(1)}) custom-call(s32[512]{0:T(512)S(1)} %copy-done.5, s32[512]{0:T(512)S(1)} %copy-done.6, s32[9]{0:T(128)S(1)} %copy-done.7, s32[1]{0:T(128)} %bitcast.4.core, bf16[1024,1024]{1,0:T(8,128)(2,1)S(1)} %get-tuple-element.40.row_turned, ...), custom_call_target="tpu_custom_call" | custom-call | tf_op jit(solution)/shard_map/far_grads/pallas_call | solution.py:288
  143.3 17.6 %near_grads.1 = (f32[16,304,128]{2,1,0:T(8,128)S(1)}, f32[8,304,128]{2,1,0:T(8,128)S(1)}) custom-call(s32[512]{0:T(512)S(1)} %copy-done.5, s32[512]{0:T(512)S(1)} %copy-done.6, s32[9]{0:T(128)S(1)} %copy-done.7, s32[1]{0:T(128)} %bitcast.4.core, bf16[1024,1024]{1,0:T(8,128)(2,1)S(1)} %get-tuple-element.40.row_turned, ...), custom_call_target="tpu_custom_call" | custom-call | tf_op jit(solution)/shard_map/near_grads/pallas_call | solution.py:288
  162.0 3.5 %add.44 = f32[16,304,128]{2,1,0:T(8,128)} add(f32[16,304,128]{2,1,0:T(8,128)S(1)} %get-tuple-element.48, f32[16,304,128]{2,1,0:T(8,128)} %collective-permute-done.8) | non-fusion elementwise | flops 622592 | bytes 7471104 | tf_op jit(solution)/shard_map/add | solution.py:361
  165.5 5.7 %all-to-all-start.1 = ((f32[16,304,128]{2,1,0:T(8,128)}), f32[16,304,128]{2,1,0:T(8,128)S(1)}, u32[]{:S(2)}, u32[]{:S(2)}) async-start(f32[16,304,128]{2,1,0:T(8,128)} %add.44), calls=%async_computation.2 | async-start | bytes 4980736 | tf_op jit(solution)/shard_map/all_to_all | solution.py:362
  171.2 27.6 %reduce-scatter.2.cloned.1.call-done = f32[1,304,128]{2,1,0:T(8,128)} async-done(((f32[8,304,128]{2,1,0:T(8,128)}), f32[1,304,128]{2,1,0:T(8,128)}) %reduce-scatter.2.cloned.1.call-update) | async-done | bytes 155664 | tf_op jit(solution)/shard_map/reduce_scatter | solution.py:360
  198.8 1.7 fusion
  200.5 5.8 %all-to-all-done.1 = f32[16,304,128]{2,1,0:T(8,128)S(1)} async-done(((f32[16,304,128]{2,1,0:T(8,128)}), f32[16,304,128]{2,1,0:T(8,128)S(1)}, u32[]{:S(2)}, u32[]{:S(2)}) %all-to-all-start.1) | async-done | bytes 2490400 | tf_op jit(solution)/shard_map/all_to_all | solution.py:362
  (69 shorter events, 11.9 us)
Async XLA Ops:
  7.2 15.3 %copy-start.12 = (s32[1,1,8,32,2]{3,4,2,1,0:T(2,128)S(1)}, s32[1,1,8,32,2]{3,4,2,1,0:T(2,128)}, u32[]{:S(2)}) copy-start(s32[1,1,8,32,2]{3,4,2,1,0:T(2,128)} %param.8) | copy-start | bytes 6148
  7.2 15.5 %copy-start.13 = (s32[1,1,8,32]{3,2,1,0:T(8,128)S(1)}, s32[1,1,8,32]{3,2,1,0:T(8,128)}, u32[]{:S(2)}) copy-start(s32[1,1,8,32]{3,2,1,0:T(8,128)} %param.9) | copy-start | bytes 3076
  7.2 66.2 %all-gather.7.cloned.1.call-start = ((), (), s32[]{:S(2)}) async-start(), calls=%async_computation.4 | async-start | bytes 5136384 | tf_op jit(solution)/shard_map/all_gather | solution.py:330
  7.9 67.1 %all-to-all-start = ((f32[256,2,8,128]{3,2,1,0:T(8,128)}), f32[256,2,8,128]{3,2,1,0:T(8,128)S(1)}, u32[]{:S(2)}, u32[]{:S(2)}) async-start(f32[256,2,8,128]{3,2,1,0:T(8,128)} %bitcast.18), calls=%async_computation | async-start | bytes 4194304 | tf_op jit(solution)/shard_map/all_to_all | solution.py:335
  22.4 95.9 %all-gather.9.cloned.1.call-start = ((), (), s32[]{:S(2)}) async-start(), calls=%async_computation.5 | async-start | bytes 1400832 | tf_op jit(solution)/shard_map/all_gather | solution.py:332
  73.4 125.4 %reduce-scatter.2.cloned.1.call-start = ((), (), s32[]{:S(2)}) async-start(), calls=%async_computation.3 | async-start | bytes 1400832 | tf_op jit(solution)/shard_map/reduce_scatter | solution.py:360
  81.3 22.7 %copy-start = (f32[512,8,128]{2,1,0:T(8,128)}, f32[512,8,128]{2,1,0:T(8,128)S(1)}, u32[]{:S(2)}) copy-start(f32[512,8,128]{2,1,0:T(8,128)S(1)} %get-tuple-element.43.counts) | copy-start | bytes 6291460
  81.3 3.7 %collective-permute-start = (f32[16,128]{1,0:T(8,128)S(1)}, f32[16,128]{1,0:T(8,128)S(1)}, u32[]{:S(2)}, u32[]{:S(2)}) collective-permute-start(f32[16,128]{1,0:T(8,128)S(1)} %slice.29), channel_id=1, source_target_pairs={{0,1},{1,0},{2,3},{3,2},{4,5},{5,4},{6,7},{7,6},{8,9},{9,8},{10,11... | collective-permute-start | bytes 24584 | tf_op jit(solution)/shard_map/ppermute | solution.py:314
  85.0 4.6 %collective-permute-start.1 = (f32[16,128]{1,0:T(8,128)S(1)}, f32[16,128]{1,0:T(8,128)S(1)}, u32[]{:S(2)}, u32[]{:S(2)}) collective-permute-start(f32[16,128]{1,0:T(8,128)S(1)} %slice_add_fusion), channel_id=1, source_target_pairs={{0,2},{1,3},{2,0},{3,1},{4,6},{5,7},{6,4},{7,5},{8,10},{9,11},{10,... | collective-permute-start | bytes 24584 | tf_op jit(solution)/shard_map/ppermute | solution.py:314
  89.6 7.6 %collective-permute-start.2 = (f32[16,128]{1,0:T(8,128)S(1)}, f32[16,128]{1,0:T(8,128)S(1)}, u32[]{:S(2)}, u32[]{:S(2)}) collective-permute-start(f32[16,128]{1,0:T(8,128)S(1)} %add.36), channel_id=1, source_target_pairs={{0,4},{1,5},{2,6},{3,7},{4,0},{5,1},{6,2},{7,3},{8,12},{9,13},{10,... | collective-permute-start | bytes 24584 | tf_op jit(solution)/shard_map/ppermute | solution.py:314
  97.2 26.4 %copy-start.5 = (s32[512]{0:T(512)S(1)}, s32[512]{0:T(512)}, u32[]{:S(2)}) copy-start(s32[512]{0:T(512)} %select_n.5.target) | copy-start | bytes 6148
  97.2 26.4 %copy-start.6 = (s32[512]{0:T(512)S(1)}, s32[512]{0:T(512)}, u32[]{:S(2)}) copy-start(s32[512]{0:T(512)} %get-tuple-element.29.order) | copy-start | bytes 6148
  97.2 26.4 %copy-start.7 = (s32[9]{0:T(128)S(1)}, s32[9]{0:T(128)}, u32[]{:S(2)}) copy-start(s32[9]{0:T(128)} %get-tuple-element.30.offsets) | copy-start | bytes 112
  104.0 1.3 collective-permute-start.3
  105.3 4.0 %collective-permute-start.4 = (f32[40,128]{1,0:T(8,128)S(1)}, f32[40,128]{1,0:T(8,128)S(1)}, u32[]{:S(2)}, u32[]{:S(2)}) collective-permute-start(f32[40,128]{1,0:T(8,128)S(1)} %fusion.1), channel_id=1, source_target_pairs={{0,16},{16,0},{32,48},{48,32},{1,17},{17,1},{33,49},{49,33},{2,18}... | collective-permute-start | bytes 61448 | tf_op jit(solution)/shard_map/ppermute | solution.py:314
  109.2 5.3 %collective-permute-start.5 = (f32[40,128]{1,0:T(8,128)S(1)}, f32[40,128]{1,0:T(8,128)S(1)}, u32[]{:S(2)}, u32[]{:S(2)}) collective-permute-start(f32[40,128]{1,0:T(8,128)S(1)} %add.39), channel_id=1, source_target_pairs={{0,32},{16,48},{32,0},{48,16},{1,33},{17,49},{33,1},{49,17},{2,34}... | collective-permute-start | bytes 61448 | tf_op jit(solution)/shard_map/ppermute | solution.py:314
  114.5 3.8 %collective-permute-start.6 = (f32[40,128]{1,0:T(8,128)S(1)}, f32[40,128]{1,0:T(8,128)S(1)}, u32[]{:S(2)}, u32[]{:S(2)}) collective-permute-start(f32[40,128]{1,0:T(8,128)S(1)} %add.40), channel_id=1, source_target_pairs={{0,64},{64,0},{128,192},{192,128},{1,65},{65,1},{129,193},{193,129... | collective-permute-start | bytes 61448 | tf_op jit(solution)/shard_map/ppermute | solution.py:314
  118.3 5.3 %collective-permute-start.7 = (f32[40,128]{1,0:T(8,128)S(1)}, f32[40,128]{1,0:T(8,128)S(1)}, u32[]{:S(2)}, u32[]{:S(2)}) collective-permute-start(f32[40,128]{1,0:T(8,128)S(1)} %add.41), channel_id=1, source_target_pairs={{0,128},{64,192},{128,0},{192,64},{1,129},{65,193},{129,1},{193,65... | collective-permute-start | bytes 61448 | tf_op jit(solution)/shard_map/ppermute | solution.py:314
  143.0 19.0 %collective-permute-start.8 = (f32[16,304,128]{2,1,0:T(8,128)}, f32[16,304,128]{2,1,0:T(8,128)}, u32[]{:S(2)}, u32[]{:S(2)}) collective-permute-start(f32[16,304,128]{2,1,0:T(8,128)} %get-tuple-element.49), channel_id=1, source_target_pairs={{0,8},{8,0},{1,9},{9,1},{2,10},{10,2},{3,11},{11,3},{4,12},{12,4},... | collective-permute-start | bytes 7471112 | tf_op jit(solution)/shard_map/ppermute | solution.py:358
  165.5 33.3 %copy-start.8 = (f32[300,128]{1,0:T(8,128)S(1)}, f32[300,128]{1,0:T(8,128)}, u32[]{:S(2)}) copy-start(f32[300,128]{1,0:T(8,128)} %param.10) | copy-start | bytes 460804
  165.5 33.3 %copy-start.10 = (f32[300,128]{1,0:T(8,128)S(1)}, f32[300,128]{1,0:T(8,128)}, u32[]{:S(2)}) copy-start(f32[300,128]{1,0:T(8,128)} %param.12) | copy-start | bytes 460804
  165.5 40.8 %all-to-all-start.1 = ((f32[16,304,128]{2,1,0:T(8,128)}), f32[16,304,128]{2,1,0:T(8,128)S(1)}, u32[]{:S(2)}, u32[]{:S(2)}) async-start(f32[16,304,128]{2,1,0:T(8,128)} %add.44), calls=%async_computation.2 | async-start | bytes 4980736 | tf_op jit(solution)/shard_map/all_to_all | solution.py:362
  171.2 35.2 %copy-start.9 = (f32[300,128]{1,0:T(8,128)S(1)}, f32[300,128]{1,0:T(8,128)}, u32[]{:S(2)}) copy-start(f32[300,128]{1,0:T(8,128)} %param.11) | copy-start | bytes 460804
  171.2 35.2 %copy-start.11 = (f32[300,128]{1,0:T(8,128)S(1)}, f32[300,128]{1,0:T(8,128)}, u32[]{:S(2)}) copy-start(f32[300,128]{1,0:T(8,128)} %param.13) | copy-start | bytes 460804
  (4 other events, 4.6 us)
Sparse Core Ops, SparseCore 0:
  10.6 62.7 all-gather.6
  75.1 38.4 all-gather.8
  162.1 36.6 reduce-scatter.1

commit v4 on v3

--- a/solution.py
+++ b/solution.py
@@ -100,10 +100,10 @@
     seat = lax.shift_right_logical(column, 1)
     far = (column & 1) ^ core
     chunk = (1 - far) * (columns // 2 // BLOCKS) + lax.shift_right_logical(seat, BLOCKS.bit_length() - 1)
-    return chunk, seat & (BLOCKS - 1), column
-
-
-def sort_kernel(target, core, order, offsets, cursor, *, columns):
+    return chunk, seat & (BLOCKS - 1)
+
+
+def sort_kernel(target, core, order, spots, offsets, cursor, *, columns):
     slots = target.shape[0]
     chunks = columns // BLOCKS
     for k in range(chunks + 1):
@@ -124,9 +124,11 @@
     offsets[chunks] = first
 
     def drop(p, carry):
-        k = chunk_of(target[p], core[0], columns)[0]
+        place = target[p]
+        k, seat = chunk_of(place, core[0], columns)
         at = cursor[k]
         order[at] = p
+        spots[at] = lax.shift_right_logical(place, columns.bit_length() - 1) * BLOCKS + seat
         cursor[k] = at + 1
         return carry
 
@@ -140,8 +142,9 @@
         functools.partial(sort_kernel, columns=columns),
         name="sort_slots",
         in_specs=[smem, smem],
-        out_specs=[smem, smem],
+        out_specs=[smem] * 3,
         out_shape=[
+            jax.ShapeDtypeStruct(target.shape, jnp.int32),
             jax.ShapeDtypeStruct(target.shape, jnp.int32),
             jax.ShapeDtypeStruct((chunks + 1,), jnp.int32),
         ],
@@ -183,53 +186,52 @@
     )(row_blocks)
 
 
-def stack_kernel(core, col_blocks, far, near):
-    pairs = col_blocks.shape[0] // CORES
-    deep = far.shape[0]
-    dim = -(-col_blocks.shape[1] // 16) * 16
-    mine = core[0] == 0
-    for i in range(pairs):
-        first, second = col_blocks[2 * i], col_blocks[2 * i + 1]
+def stack_kernel(core, col_blocks, out):
+    deep = out.shape[0]
+    dim = -(-col_blocks.shape[2] // 16) * 16
+    for i in range(BLOCKS):
+        high, low = split(taller(col_blocks[i, 0], dim))
         here = slice(i * LANES, (i + 1) * LANES)
-        for out, value in ((far, jnp.where(mine, second, first)), (near, jnp.where(mine, first, second))):
-            high, low = split(taller(value, dim))
-            out[0:dim, here] = high
-            out[dim : 2 * dim, here] = low
-            out[2 * dim : 3 * dim, here] = high
-            out[3 * dim :, here] = jnp.zeros((deep - 3 * dim, LANES), BF16)
-
-
-def stack_cols(core, col_blocks, deep):
+        out[0:dim, here] = high
+        out[dim : 2 * dim, here] = low
+        out[2 * dim : 3 * dim, here] = high
+        out[3 * dim :, here] = jnp.zeros((deep - 3 * dim, LANES), BF16)
+
+
+def stack_cols(core, col_blocks, deep, near):
     n_col, dim, _ = col_blocks.shape
-    half = pltpu.HBM((deep, n_col // CORES * LANES), BF16)
-    out = pl.BlockSpec((deep, BLOCKS * LANES), lambda g, *_: (0, g))
+    seats = n_col // CORES
+    col_blocks = pltpu.with_memory_space_constraint(col_blocks.reshape(seats, CORES, dim, LANES), pltpu.HBM)
+    pick = lambda g, core: (g, core[0] if near else 1 - core[0], 0, 0)
     return pl.pallas_call(
         stack_kernel,
-        name="stack_columns",
+        name="stack_near" if near else "stack_far",
         grid_spec=pltpu.PrefetchScalarGridSpec(
             num_scalar_prefetch=1,
-            grid=(n_col // BLOCKS // CORES,),
-            in_specs=[pl.BlockSpec((BLOCKS * CORES, dim, LANES), lambda g, *_: (g, 0, 0))],
-            out_specs=[out, out],
+            grid=(seats // BLOCKS,),
+            in_specs=[pl.BlockSpec((BLOCKS, 1, dim, LANES), pick)],
+            out_specs=pl.BlockSpec((deep, BLOCKS * LANES), lambda g, *_: (0, g)),
         ),
-        out_shape=[half, half],
+        out_shape=pltpu.HBM((deep, seats * LANES), BF16),
         compiler_params=pltpu.CompilerParams(vmem_limit_bytes=14 << 20),
-    )(core, pltpu.with_memory_space_constraint(col_blocks, pltpu.HBM))
+    )(core, col_blocks)
 
 
 def part_kernel(
-    target, order, offsets, core, row_turned, row_stack, col_stack, counts, masses, *rest, near
+    order, spots, offsets, core, row_turned, row_stack, col_stack, counts_far, masses, *rest, near
 ):
-    col_term, row_term, scores, grads, row_bias, col_bias = rest[-6:]
+    col_term, row_term, scores, grads, row_bias, col_bias, counts, arrival = rest[-8:]
     padded, n_row = row_term.shape[1], row_term.shape[0]
     n_col = col_bias.shape[0]
     ct = pl.program_id(0)
     chunks = pl.num_programs(0)
-    shift = n_col.bit_length() - 1
     side = core[0] if near else 1 - core[0]
+
+    fetch = pltpu.make_async_copy(counts_far, counts, arrival)
 
     @pl.when(ct == 0)
     def _():
+        fetch.start()
         log_total = jnp.log(masses[n_col + n_row : n_col + n_row + 1, :])
         col_bias[...] = 0.5 * (jnp.log(masses[0:n_col, :]) - log_total)
         row_logs = 0.5 * jnp.log(masses[n_col : n_col + n_row, :])
@@ -244,18 +246,21 @@
         value = product[:, k * LANES : (k + 1) * LANES].reshape(-1, 8, LANES) + row_bias[...] + bias
         scores[:, k] = value
         grads[:, k] = 0.5 * jnp.tanh(value) + 0.5
-    at = ct + (chunks if near else 0)
-    begin = offsets[at]
-    end = offsets[at + 1]
+    here = ct + (chunks if near else 0)
+    begin = offsets[here]
+    end = offsets[here + 1]
+
+    @pl.when(ct == 0)
+    def _():
+        fetch.wait()
 
     def counted(step, carry):
         found = []
         for u in range(8):
-            p = order[jnp.minimum(begin + step * 8 + u, end - 1)]
-            place = target[p]
-            row = lax.shift_right_logical(place, shift)
-            k = lax.shift_right_logical(place & (n_col - 1), 1) & (BLOCKS - 1)
-            count = counts[p]
+            at = jnp.minimum(begin + step * 8 + u, end - 1)
+            spot = spots[at]
+            row, k = lax.shift_right_logical(spot, BLOCKS.bit_length() - 1), spot & (BLOCKS - 1)
+            count = counts[order[at]]
             fresh = (0.1 + 0.25 * jnp.sqrt(count)) * (2.0 * scores[row, k] - jnp.log(count))
             found.append((row, k, fresh))
         for row, k, fresh in found:
@@ -293,21 +298,24 @@
             grid=(blocks // BLOCKS,),
             in_specs=whole(2)
             + [pl.BlockSpec((deep, BLOCKS * LANES), lambda g, *_: (0, g))]
-            + whole(2 + len(ready)),
-            out_specs=[pl.BlockSpec((BLOCKS, padded, LANES), lambda g, *_: (g, 0, 0))] + whole(1),
+            + [pl.BlockSpec(memory_space=pltpu.HBM)]
+            + whole(1 + len(ready)),
+            out_specs=[pl.BlockSpec((BLOCKS, padded, LANES), lambda g, *_: (g, 0, 0)), pl.BlockSpec((words // LANES, padded, LANES), lambda g, *_: (0, 0, 0))],
             scratch_shapes=[
                 pltpu.VMEM((words // 8, BLOCKS, 8, LANES), F32),
                 pltpu.VMEM((words // 8, BLOCKS, 8, LANES), F32),
                 pltpu.VMEM((words // 8, 8, LANES), F32),
                 pltpu.VMEM((blocks * CORES, LANES), F32),
+                pltpu.VMEM(counts.shape, F32),
+                pltpu.SemaphoreType.DMA(()),
             ],
         ),
         out_shape=[
             jax.ShapeDtypeStruct((blocks, padded, LANES), F32),
-            jax.ShapeDtypeStruct((words // LANES, padded, LANES), F32),
+            (pltpu.HBM if near else jax.ShapeDtypeStruct)((words // LANES, padded, LANES), F32),
         ],
         compiler_params=pltpu.CompilerParams(vmem_limit_bytes=36 << 20),
-    )(*scalars, row_turned, row_stack, pltpu.with_memory_space_constraint(col_stack, pltpu.HBM), counts, masses, *ready)
+    )(*scalars, row_turned, row_stack, pltpu.with_memory_space_constraint(col_stack, pltpu.HBM), pltpu.with_memory_space_constraint(counts, pltpu.HBM), masses, *ready)
 
 
 def swap_sum(value, axis, size, bit):
@@ -326,9 +334,11 @@
     target = jnp.where(alive, places, places[:, :, :1]).reshape(-1)
     tile_rows, tile_cols = words * n_z, words * n_row_axis
     n_col, n_row = tile_cols // LANES, tile_rows // LANES
-    order, offsets = sort_slots(target, core, n_col)
+    order, spots, offsets = sort_slots(target, core, n_col)
     col_blocks = lax.all_gather(col_emb, ROW, axis=0)
-    row_emb_late, col_blocks, order, offsets = lax.optimization_barrier((row_emb, col_blocks, order, offsets))
+    row_emb_late, col_blocks, order, spots, offsets = lax.optimization_barrier(
+        (row_emb, col_blocks, order, spots, offsets)
+    )
     row_blocks = lax.all_gather(row_emb_late, "col", axis=0)
     sub_rows, sub_cols = blocks.shape[5:]
     slots_each = blocks.shape[4]
@@ -341,19 +351,22 @@
     row_part = part[n_col:]
     row_part = swap_sum(row_part, "col", n_z, 1)
     row_part = swap_sum(row_part, "col", n_z, 2)
-    row_part, core = lax.optimization_barrier((row_part, core))
-    far_stack, near_stack = stack_cols(core, col_blocks, deep)
     row_part = swap_sum(row_part, "col", n_z, 4)
-    row_part, far_stack, near_stack = lax.optimization_barrier((row_part, far_stack, near_stack))
     col_part = jnp.concatenate([part[:n_col], row_part[n_row:]], axis=0)
     col_part = swap_sum(col_part, "core", CORES, 1)
-    for axis, bit in (("y", 1), ("y", 2), ("x", 1)):
-        col_part = swap_sum(col_part, axis, GRID_X, bit)
+    col_part, col_blocks = lax.optimization_barrier((col_part, col_blocks))
+    col_part = swap_sum(col_part, "y", GRID_Y, 1)
+    far_stack = stack_cols(core, col_blocks, deep, False)
+    col_part, far_stack, col_blocks = lax.optimization_barrier((col_part, far_stack, col_blocks))
+    col_part = swap_sum(col_part, "y", GRID_Y, 2)
+    near_stack = stack_cols(core, col_blocks, deep, True)
+    col_part, near_stack = lax.optimization_barrier((col_part, near_stack))
+    col_part = swap_sum(col_part, "x", GRID_X, 1)
     col_part, row_blocks = lax.optimization_barrier((col_part, row_blocks))
     row_stack, row_turned = turn(row_blocks, padded, deep)
     col_part = swap_sum(col_part, "x", GRID_X, 2)
     masses = jnp.concatenate([col_part[:n_col], row_part[:n_row], col_part[n_col:]], axis=0)
-    scalars = (target, order, offsets, core)
+    scalars = (order, spots, offsets, core)
     far_term, row_term = part_grads(scalars, row_turned, row_stack, far_stack, counts, masses, None)
     swapped = lax.ppermute(far_term, "core", [(0, 1), (1, 0)])
     near_term, row_term = part_grads(scalars, row_turned, row_stack, near_stack, counts, masses, row_term)

time: 215 us -> 210 us (0.977)
  waiting for transfers between devices: 100 us -> 92.7 us
  Pallas kernels: 55.9 us -> 59.8 us
  local copies, waits for them, and re-layouts: 5.33 us -> 2.69 us
    ppermute x8, waiting for transfers between devices: 22.5 us -> 15.5 us  [swap_sum(): lax.ppermute(value, axis, [(i, i ^ bit) for i in range(size)])]
    unnamed x29 -> x25, local copies, waits for them, and re-layouts: 4.79 us -> 2.15 us
    pallas_call x1 -> x2, Pallas kernels: 6.77 us -> 9.14 us  [stack_cols(): pl.pallas_call(stack_kernel, name='stack_near' if near else 'stack_far',...]
  transfers between devices with their start and end apart: 14 -> 14, of which waited for: 12 -> 11; matrix products, arithmetic and copies ran while one was open for 3% -> 3% of each run, Pallas kernels for 18% -> 20%
where the time goes in v4:
time: 210 us
  waiting for transfers between devices  92.7 us (44%)
  Pallas kernels  59.8 us (28%)
  starting transfers between devices  33.6 us (16%)
  between operations  14 us (7%)
  other arithmetic  6.79 us (3%)
  local copies, waits for them, and re-layouts  2.69 us (1%)
    all_gather x1, waiting for transfers between devices, per_device(): col_blocks = lax.all_gather(col_emb, ROW, axis=0)  41.5 us
    pallas_call x2, Pallas kernels, part_grads(): pl.pallas_call(functools.partial(part_kernel, near=near), name='near_grad...  36.4 us
    reduce_scatter x1, waiting for transfers between devices, per_device(): lax.psum_scatter(row_term, 'col', scatter_dimension=0, tiled=False)  27.5 us
    ppermute x8, waiting for transfers between devices, swap_sum(): lax.ppermute(value, axis, [(i, i ^ bit) for i in range(size)])  15.5 us
    all_to_all x1, starting transfers between devices, per_device(): lax.all_to_all(blocks.reshape(-1, slots_each, sub_rows, sub_cols), ALL, s...  14.5 us
    ppermute x8, starting transfers between devices, swap_sum(): lax.ppermute(value, axis, [(i, i ^ bit) for i in range(size)])  11.6 us
    pallas_call x2, Pallas kernels, stack_cols(): pl.pallas_call(stack_kernel, name='stack_near' if near else 'stack_far',...  9.14 us
    pallas_call x1, Pallas kernels, sort_slots(): pl.pallas_call(functools.partial(sort_kernel, columns=columns), name='sor...  7.99 us
  transfers between devices with their start and end apart: 14, of which 11 were waited for; matrix products, arithmetic and copies ran while one was open for 3% of the time, Pallas kernels for 20%

profile of v4, /device:TPU:16, one launch (start us, length us, event | category | flops | bytes accessed | tf_op | source)
XLA Modules:
  0.0 209.5 jit_solution(286280516149602836)
XLA Ops:
  7.9 14.5 %all-to-all-start = ((f32[256,2,8,128]{3,2,1,0:T(8,128)}), f32[256,2,8,128]{3,2,1,0:T(8,128)S(1)}, u32[]{:S(2)}, u32[]{:S(2)}) async-start(f32[256,2,8,128]{3,2,1,0:T(8,128)} %bitcast.22), calls=%async_computation | async-start | bytes 4194304 | tf_op jit(solution)/shard_map/all_to_all | solution.py:345
  23.9 8.0 %sort_slots.1 = (s32[512]{0:T(512)}, s32[512]{0:T(512)}, s32[9]{0:T(128)}) custom-call(s32[512]{0:T(512)} %select_n.5.target, s32[1]{0:T(128)} %bitcast.4.core), custom_call_target="tpu_custom_call" | custom-call | tf_op jit(solution)/shard_map/sort_slots/pallas_call | solution.py:141
  31.9 41.5 %all-gather.7.cloned.1.call-done = f32[32,300,128]{2,1,0:T(8,128)} async-done(((f32[1,300,128]{2,1,0:T(8,128)}), f32[32,300,128]{2,1,0:T(8,128)}) %all-gather.7.cloned.1.call-update) | async-done | bytes 4915216 | tf_op jit(solution)/shard_map/all_gather | solution.py:338
  73.4 1.6 all-to-all-done
  75.7 5.6 %place_counts.1 = (f32[512,8,128]{2,1,0:T(8,128)S(1)}, f32[48,128]{1,0:T(8,128)S(1)}) custom-call(s32[512]{0:T(512)S(1)} %copy-done.2, s32[512]{0:T(512)S(1)} %convert_element_type.4.alive, f32[512,8,128]{2,1,0:T(8,128)S(1)} %bitcast.19), custom_call_target="tpu_custom_call" | custom-call | tf_op jit(solution)/shard_map/place_counts/pallas_call | solution.py:76
  81.3 1.3 collective-permute-start
  82.6 2.4 %collective-permute-done = f32[16,128]{1,0:T(8,128)S(1)} collective-permute-done((f32[16,128]{1,0:T(8,128)S(1)}, f32[16,128]{1,0:T(8,128)S(1)}, u32[]{:S(2)}, u32[]{:S(2)}) %collective-permute-start) | collective-permute-done | bytes 8224 | tf_op jit(solution)/shard_map/ppermute | solution.py:322
  85.9 3.7 %collective-permute-done.1 = f32[16,128]{1,0:T(8,128)S(1)} collective-permute-done((f32[16,128]{1,0:T(8,128)S(1)}, f32[16,128]{1,0:T(8,128)S(1)}, u32[]{:S(2)}, u32[]{:S(2)}) %collective-permute-start.1) | collective-permute-done | bytes 8224 | tf_op jit(solution)/shard_map/ppermute | solution.py:322
  89.6 3.5 %collective-permute-start.2 = (f32[16,128]{1,0:T(8,128)S(1)}, f32[16,128]{1,0:T(8,128)S(1)}, u32[]{:S(2)}, u32[]{:S(2)}) collective-permute-start(f32[16,128]{1,0:T(8,128)S(1)} %add.36), channel_id=1, source_target_pairs={{0,4},{1,5},{2,6},{3,7},{4,0},{5,1},{6,2},{7,3},{8,12},{9,13},{10,... | collective-permute-start | bytes 24584 | tf_op jit(solution)/shard_map/ppermute | solution.py:322
  93.1 4.1 %collective-permute-done.2 = f32[16,128]{1,0:T(8,128)S(1)} collective-permute-done((f32[16,128]{1,0:T(8,128)S(1)}, f32[16,128]{1,0:T(8,128)S(1)}, u32[]{:S(2)}, u32[]{:S(2)}) %collective-permute-start.2) | collective-permute-done | bytes 8224 | tf_op jit(solution)/shard_map/ppermute | solution.py:322
  97.3 1.2 collective-permute-done.3
  98.5 2.2 %collective-permute-start.4 = (f32[40,128]{1,0:T(8,128)S(1)}, f32[40,128]{1,0:T(8,128)S(1)}, u32[]{:S(2)}, u32[]{:S(2)}) collective-permute-start(f32[40,128]{1,0:T(8,128)S(1)} %fusion.1), channel_id=1, source_target_pairs={{0,16},{16,0},{32,48},{48,32},{1,17},{17,1},{33,49},{49,33},{2,18}... | collective-permute-start | bytes 61448 | tf_op jit(solution)/shard_map/ppermute | solution.py:322
  100.7 4.5 %stack_far.1.col_stack = bf16[1024,2048]{1,0:T(8,128)(2,1)} custom-call(s32[1]{0:T(128)} %bitcast.4.core, f32[16,2,300,128]{3,2,1,0:T(8,128)} %bitcast.20), custom_call_target="tpu_custom_call" | custom-call | tf_op jit(solution)/shard_map/stack_far/pallas_call | solution.py:206
  105.6 4.6 %stack_near.1.col_stack = bf16[1024,2048]{1,0:T(8,128)(2,1)} custom-call(s32[1]{0:T(128)} %bitcast.4.core, f32[16,2,300,128]{3,2,1,0:T(8,128)} %bitcast.21), custom_call_target="tpu_custom_call" | custom-call | tf_op jit(solution)/shard_map/stack_near/pallas_call | solution.py:206
  111.8 2.7 %collective-permute-done.6 = f32[40,128]{1,0:T(8,128)S(1)} collective-permute-done((f32[40,128]{1,0:T(8,128)S(1)}, f32[40,128]{1,0:T(8,128)S(1)}, u32[]{:S(2)}, u32[]{:S(2)}) %collective-permute-start.6) | collective-permute-done | bytes 20512 | tf_op jit(solution)/shard_map/ppermute | solution.py:322
  114.4 2.2 %collective-permute-start.7 = (f32[40,128]{1,0:T(8,128)S(1)}, f32[40,128]{1,0:T(8,128)S(1)}, u32[]{:S(2)}, u32[]{:S(2)}) collective-permute-start(f32[40,128]{1,0:T(8,128)S(1)} %add.41), channel_id=1, source_target_pairs={{0,128},{64,192},{128,0},{192,64},{1,129},{65,193},{129,1},{193,65... | collective-permute-start | bytes 61448 | tf_op jit(solution)/shard_map/ppermute | solution.py:322
  116.6 1.3 copy-done.1
  119.8 17.7 %far_grads.1 = (f32[16,304,128]{2,1,0:T(8,128)}, f32[8,304,128]{2,1,0:T(8,128)S(1)}) custom-call(s32[512]{0:T(512)S(1)} %copy-done.3, s32[512]{0:T(512)S(1)} %copy-done.4, s32[9]{0:T(128)S(1)} %copy-done.5, s32[1]{0:T(128)} %bitcast.4.core, bf16[1024,1024]{1,0:T(8,128)(2,1)S(1)} %get-tuple-element.44.row_turned, ...), custom_call_target="tpu_custom_call" | custom-call | tf_op jit(solution)/shard_map/far_grads/pallas_call | solution.py:293
  137.7 18.7 %near_grads.1 = (f32[16,304,128]{2,1,0:T(8,128)S(1)}, f32[8,304,128]{2,1,0:T(8,128)}) custom-call(s32[512]{0:T(512)S(1)} %copy-done.3, s32[512]{0:T(512)S(1)} %copy-done.4, s32[9]{0:T(128)S(1)} %copy-done.5, s32[1]{0:T(128)} %bitcast.4.core, bf16[1024,1024]{1,0:T(8,128)(2,1)S(1)} %get-tuple-element.44.row_turned, ...), custom_call_target="tpu_custom_call" | custom-call | tf_op jit(solution)/shard_map/near_grads/pallas_call | solution.py:293
  156.5 3.5 %add.44 = f32[16,304,128]{2,1,0:T(8,128)} add(f32[16,304,128]{2,1,0:T(8,128)S(1)} %get-tuple-element.52, f32[16,304,128]{2,1,0:T(8,128)} %collective-permute-done.8) | non-fusion elementwise | flops 622592 | bytes 7471104 | tf_op jit(solution)/shard_map/add | solution.py:374
  160.0 7.1 %all-to-all-start.1 = ((f32[16,304,128]{2,1,0:T(8,128)}), f32[16,304,128]{2,1,0:T(8,128)S(1)}, u32[]{:S(2)}, u32[]{:S(2)}) async-start(f32[16,304,128]{2,1,0:T(8,128)} %add.44), calls=%async_computation.2 | async-start | bytes 4980736 | tf_op jit(solution)/shard_map/all_to_all | solution.py:375
  167.1 27.5 %reduce-scatter.2.cloned.1.call-done = f32[1,304,128]{2,1,0:T(8,128)} async-done(((f32[8,304,128]{2,1,0:T(8,128)}), f32[1,304,128]{2,1,0:T(8,128)}) %reduce-scatter.2.cloned.1.call-update) | async-done | bytes 155664 | tf_op jit(solution)/shard_map/reduce_scatter | solution.py:373
  194.6 1.7 fusion
  196.3 5.8 %all-to-all-done.1 = f32[16,304,128]{2,1,0:T(8,128)S(1)} async-done(((f32[16,304,128]{2,1,0:T(8,128)}), f32[16,304,128]{2,1,0:T(8,128)S(1)}, u32[]{:S(2)}, u32[]{:S(2)}) %all-to-all-start.1) | async-done | bytes 2490400 | tf_op jit(solution)/shard_map/all_to_all | solution.py:375
  (66 shorter events, 8.8 us)
Async XLA Ops:
  7.2 15.3 %copy-start.10 = (s32[1,1,8,32,2]{3,4,2,1,0:T(2,128)S(1)}, s32[1,1,8,32,2]{3,4,2,1,0:T(2,128)}, u32[]{:S(2)}) copy-start(s32[1,1,8,32,2]{3,4,2,1,0:T(2,128)} %param.8) | copy-start | bytes 6148
  7.2 15.5 %copy-start.11 = (s32[1,1,8,32]{3,2,1,0:T(8,128)S(1)}, s32[1,1,8,32]{3,2,1,0:T(8,128)}, u32[]{:S(2)}) copy-start(s32[1,1,8,32]{3,2,1,0:T(8,128)} %param.9) | copy-start | bytes 3076
  7.2 66.2 %all-gather.7.cloned.1.call-start = ((), (), s32[]{:S(2)}) async-start(), calls=%async_computation.4 | async-start | bytes 5136384 | tf_op jit(solution)/shard_map/all_gather | solution.py:338
  7.9 67.1 %all-to-all-start = ((f32[256,2,8,128]{3,2,1,0:T(8,128)}), f32[256,2,8,128]{3,2,1,0:T(8,128)S(1)}, u32[]{:S(2)}, u32[]{:S(2)}) async-start(f32[256,2,8,128]{3,2,1,0:T(8,128)} %bitcast.22), calls=%async_computation | async-start | bytes 4194304 | tf_op jit(solution)/shard_map/all_to_all | solution.py:345
  22.4 92.0 %all-gather.9.cloned.1.call-start = ((), (), s32[]{:S(2)}) async-start(), calls=%async_computation.5 | async-start | bytes 1400832 | tf_op jit(solution)/shard_map/all_gather | solution.py:342
  73.4 121.2 %reduce-scatter.2.cloned.1.call-start = ((), (), s32[]{:S(2)}) async-start(), calls=%async_computation.3 | async-start | bytes 1400832 | tf_op jit(solution)/shard_map/reduce_scatter | solution.py:373
  81.3 23.9 %copy-start = (f32[512,8,128]{2,1,0:T(8,128)}, f32[512,8,128]{2,1,0:T(8,128)S(1)}, u32[]{:S(2)}) copy-start(f32[512,8,128]{2,1,0:T(8,128)S(1)} %get-tuple-element.47.counts_far) | copy-start | bytes 6291460
  81.3 3.7 %collective-permute-start = (f32[16,128]{1,0:T(8,128)S(1)}, f32[16,128]{1,0:T(8,128)S(1)}, u32[]{:S(2)}, u32[]{:S(2)}) collective-permute-start(f32[16,128]{1,0:T(8,128)S(1)} %slice.30), channel_id=1, source_target_pairs={{0,1},{1,0},{2,3},{3,2},{4,5},{5,4},{6,7},{7,6},{8,9},{9,8},{10,11... | collective-permute-start | bytes 24584 | tf_op jit(solution)/shard_map/ppermute | solution.py:322
  85.0 4.6 %collective-permute-start.1 = (f32[16,128]{1,0:T(8,128)S(1)}, f32[16,128]{1,0:T(8,128)S(1)}, u32[]{:S(2)}, u32[]{:S(2)}) collective-permute-start(f32[16,128]{1,0:T(8,128)S(1)} %slice_add_fusion), channel_id=1, source_target_pairs={{0,2},{1,3},{2,0},{3,1},{4,6},{5,7},{6,4},{7,5},{8,10},{9,11},{10,... | collective-permute-start | bytes 24584 | tf_op jit(solution)/shard_map/ppermute | solution.py:322
  89.6 7.6 %collective-permute-start.2 = (f32[16,128]{1,0:T(8,128)S(1)}, f32[16,128]{1,0:T(8,128)S(1)}, u32[]{:S(2)}, u32[]{:S(2)}) collective-permute-start(f32[16,128]{1,0:T(8,128)S(1)} %add.36), channel_id=1, source_target_pairs={{0,4},{1,5},{2,6},{3,7},{4,0},{5,1},{6,2},{7,3},{8,12},{9,13},{10,... | collective-permute-start | bytes 24584 | tf_op jit(solution)/shard_map/ppermute | solution.py:322
  97.2 1.3 collective-permute-start.3
  98.5 6.7 %collective-permute-start.4 = (f32[40,128]{1,0:T(8,128)S(1)}, f32[40,128]{1,0:T(8,128)S(1)}, u32[]{:S(2)}, u32[]{:S(2)}) collective-permute-start(f32[40,128]{1,0:T(8,128)S(1)} %fusion.1), channel_id=1, source_target_pairs={{0,16},{16,0},{32,48},{48,32},{1,17},{17,1},{33,49},{49,33},{2,18}... | collective-permute-start | bytes 61448 | tf_op jit(solution)/shard_map/ppermute | solution.py:322
  105.2 5.4 %collective-permute-start.5 = (f32[40,128]{1,0:T(8,128)S(1)}, f32[40,128]{1,0:T(8,128)S(1)}, u32[]{:S(2)}, u32[]{:S(2)}) collective-permute-start(f32[40,128]{1,0:T(8,128)S(1)} %add.39), channel_id=1, source_target_pairs={{0,32},{16,48},{32,0},{48,16},{1,33},{17,49},{33,1},{49,17},{2,34}... | collective-permute-start | bytes 61448 | tf_op jit(solution)/shard_map/ppermute | solution.py:322
  105.5 14.2 %copy-start.3 = (s32[512]{0:T(512)S(1)}, s32[512]{0:T(512)}, u32[]{:S(2)}) copy-start(s32[512]{0:T(512)} %get-tuple-element.32.order) | copy-start | bytes 6148
  105.5 14.2 %copy-start.4 = (s32[512]{0:T(512)S(1)}, s32[512]{0:T(512)}, u32[]{:S(2)}) copy-start(s32[512]{0:T(512)} %get-tuple-element.33.spots) | copy-start | bytes 6148
  105.6 14.2 %copy-start.5 = (s32[9]{0:T(128)S(1)}, s32[9]{0:T(128)}, u32[]{:S(2)}) copy-start(s32[9]{0:T(128)} %get-tuple-element.34.offsets) | copy-start | bytes 112
  110.6 3.8 %collective-permute-start.6 = (f32[40,128]{1,0:T(8,128)S(1)}, f32[40,128]{1,0:T(8,128)S(1)}, u32[]{:S(2)}, u32[]{:S(2)}) collective-permute-start(f32[40,128]{1,0:T(8,128)S(1)} %add.40), channel_id=1, source_target_pairs={{0,64},{64,0},{128,192},{192,128},{1,65},{65,1},{129,193},{193,129... | collective-permute-start | bytes 61448 | tf_op jit(solution)/shard_map/ppermute | solution.py:322
  114.4 5.3 %collective-permute-start.7 = (f32[40,128]{1,0:T(8,128)S(1)}, f32[40,128]{1,0:T(8,128)S(1)}, u32[]{:S(2)}, u32[]{:S(2)}) collective-permute-start(f32[40,128]{1,0:T(8,128)S(1)} %add.41), channel_id=1, source_target_pairs={{0,128},{64,192},{128,0},{192,64},{1,129},{65,193},{129,1},{193,65... | collective-permute-start | bytes 61448 | tf_op jit(solution)/shard_map/ppermute | solution.py:322
  137.4 19.0 %collective-permute-start.8 = (f32[16,304,128]{2,1,0:T(8,128)}, f32[16,304,128]{2,1,0:T(8,128)}, u32[]{:S(2)}, u32[]{:S(2)}) collective-permute-start(f32[16,304,128]{2,1,0:T(8,128)} %get-tuple-element.53), channel_id=1, source_target_pairs={{0,8},{8,0},{1,9},{9,1},{2,10},{10,2},{3,11},{11,3},{4,12},{12,4},... | collective-permute-start | bytes 7471112 | tf_op jit(solution)/shard_map/ppermute | solution.py:371
  160.0 34.6 %copy-start.6 = (f32[300,128]{1,0:T(8,128)S(1)}, f32[300,128]{1,0:T(8,128)}, u32[]{:S(2)}) copy-start(f32[300,128]{1,0:T(8,128)} %param.10) | copy-start | bytes 460804
  160.0 34.6 %copy-start.8 = (f32[300,128]{1,0:T(8,128)S(1)}, f32[300,128]{1,0:T(8,128)}, u32[]{:S(2)}) copy-start(f32[300,128]{1,0:T(8,128)} %param.12) | copy-start | bytes 460804
  160.0 42.1 %all-to-all-start.1 = ((f32[16,304,128]{2,1,0:T(8,128)}), f32[16,304,128]{2,1,0:T(8,128)S(1)}, u32[]{:S(2)}, u32[]{:S(2)}) async-start(f32[16,304,128]{2,1,0:T(8,128)} %add.44), calls=%async_computation.2 | async-start | bytes 4980736 | tf_op jit(solution)/shard_map/all_to_all | solution.py:375
  167.1 35.2 %copy-start.7 = (f32[300,128]{1,0:T(8,128)S(1)}, f32[300,128]{1,0:T(8,128)}, u32[]{:S(2)}) copy-start(f32[300,128]{1,0:T(8,128)} %param.11) | copy-start | bytes 460804
  167.1 35.2 %copy-start.9 = (f32[300,128]{1,0:T(8,128)S(1)}, f32[300,128]{1,0:T(8,128)}, u32[]{:S(2)}) copy-start(f32[300,128]{1,0:T(8,128)} %param.13) | copy-start | bytes 460804
  (2 other events, 2.0 us)
Sparse Core Ops, SparseCore 0:
  10.6 62.7 all-gather.6
  75.1 38.4 all-gather.8
  156.6 37.9 reduce-scatter.1

commit v5 on v4

--- a/solution.py
+++ b/solution.py
@@ -12,7 +12,7 @@
 ROW = ("x", "y", "core")
 ALL = ("col", "x", "y", "core")
 LANES = 128
-BLOCKS = 4
+BLOCKS = 8
 F32 = jnp.float32
 BF16 = jnp.bfloat16
 
@@ -186,10 +186,11 @@
     )(row_blocks)
 
 
-def stack_kernel(core, col_blocks, out):
+def stack_kernel(core, col_blocks, *rest):
+    out = rest[-1]
     deep = out.shape[0]
     dim = -(-col_blocks.shape[2] // 16) * 16
-    for i in range(BLOCKS):
+    for i in range(col_blocks.shape[0]):
         high, low = split(taller(col_blocks[i, 0], dim))
         here = slice(i * LANES, (i + 1) * LANES)
         out[0:dim, here] = high
@@ -198,23 +199,28 @@
         out[3 * dim :, here] = jnp.zeros((deep - 3 * dim, LANES), BF16)
 
 
-def stack_cols(core, col_blocks, deep, near):
+def stack_cols(core, col_blocks, deep, near, earlier=None):
     n_col, dim, _ = col_blocks.shape
     seats = n_col // CORES
+    step = BLOCKS // 2
+    first = 0 if earlier is None else seats // step // 2
+    ready = [] if earlier is None else [earlier]
     col_blocks = pltpu.with_memory_space_constraint(col_blocks.reshape(seats, CORES, dim, LANES), pltpu.HBM)
-    pick = lambda g, core: (g, core[0] if near else 1 - core[0], 0, 0)
+    pick = lambda g, core: (first + g, core[0] if near else 1 - core[0], 0, 0)
     return pl.pallas_call(
         stack_kernel,
         name="stack_near" if near else "stack_far",
         grid_spec=pltpu.PrefetchScalarGridSpec(
             num_scalar_prefetch=1,
-            grid=(seats // BLOCKS,),
-            in_specs=[pl.BlockSpec((BLOCKS, 1, dim, LANES), pick)],
-            out_specs=pl.BlockSpec((deep, BLOCKS * LANES), lambda g, *_: (0, g)),
+            grid=(seats // step // 2,),
+            in_specs=[pl.BlockSpec((step, 1, dim, LANES), pick)]
+            + [pl.BlockSpec(memory_space=pltpu.HBM)] * len(ready),
+            out_specs=pl.BlockSpec((deep, step * LANES), lambda g, *_: (0, first + g)),
         ),
         out_shape=pltpu.HBM((deep, seats * LANES), BF16),
+        input_output_aliases={2: 0} if ready else {},
         compiler_params=pltpu.CompilerParams(vmem_limit_bytes=14 << 20),
-    )(core, col_blocks)
+    )(core, col_blocks, *ready)
 
 
 def part_kernel(
@@ -346,22 +352,27 @@
         blocks.reshape(-1, slots_each, sub_rows, sub_cols), ALL, split_axis=0, concat_axis=0, tiled=True
     ).reshape(-1, sub_rows, sub_cols)
     counts, part = place(
-        target, alive.astype(jnp.int32).reshape(-1), arrived, tile_rows // sub_rows, n_col
+        pltpu.with_memory_space_constraint(target, pltpu.HBM), alive.astype(jnp.int32).reshape(-1), arrived, tile_rows // sub_rows, n_col
     )
     row_part = part[n_col:]
     row_part = swap_sum(row_part, "col", n_z, 1)
     row_part = swap_sum(row_part, "col", n_z, 2)
+    row_part, col_blocks = lax.optimization_barrier((row_part, col_blocks))
     row_part = swap_sum(row_part, "col", n_z, 4)
+    far_stack = stack_cols(core, col_blocks, deep, False)
+    row_part, far_stack = lax.optimization_barrier((row_part, far_stack))
     col_part = jnp.concatenate([part[:n_col], row_part[n_row:]], axis=0)
     col_part = swap_sum(col_part, "core", CORES, 1)
-    col_part, col_blocks = lax.optimization_barrier((col_part, col_blocks))
+    col_part, far_stack, col_blocks = lax.optimization_barrier((col_part, far_stack, col_blocks))
     col_part = swap_sum(col_part, "y", GRID_Y, 1)
-    far_stack = stack_cols(core, col_blocks, deep, False)
+    far_stack = stack_cols(core, col_blocks, deep, False, far_stack)
     col_part, far_stack, col_blocks = lax.optimization_barrier((col_part, far_stack, col_blocks))
     col_part = swap_sum(col_part, "y", GRID_Y, 2)
     near_stack = stack_cols(core, col_blocks, deep, True)
+    col_part, near_stack, col_blocks = lax.optimization_barrier((col_part, near_stack, col_blocks))
+    col_part = swap_sum(col_part, "x", GRID_X, 1)
+    near_stack = stack_cols(core, col_blocks, deep, True, near_stack)
     col_part, near_stack = lax.optimization_barrier((col_part, near_stack))
-    col_part = swap_sum(col_part, "x", GRID_X, 1)
     col_part, row_blocks = lax.optimization_barrier((col_part, row_blocks))
     row_stack, row_turned = turn(row_blocks, padded, deep)
     col_part = swap_sum(col_part, "x", GRID_X, 2)

time: 210 us -> 208 us (level)
  waiting for transfers between devices: 92.7 us -> 90.2 us
    ppermute x8, waiting for transfers between devices: 15.5 us -> 11.4 us  [swap_sum(): lax.ppermute(value, axis, [(i, i ^ bit) for i in range(size)])]
    pallas_call x2 -> x4, Pallas kernels: 9.14 us -> 10.5 us  [stack_cols(): pl.pallas_call(stack_kernel, name='stack_near' if near else 'stack_far',...]
  transfers between devices with their start and end apart: 14 -> 14, of which waited for: 11 -> 12; matrix products, arithmetic and copies ran while one was open for 3% -> 3% of each run, Pallas kernels for 20% -> 21%
where the time goes in v5:
time: 208 us
  waiting for transfers between devices  90.2 us (43%)
  Pallas kernels  60 us (29%)
  starting transfers between devices  34.7 us (17%)
  between operations  14 us (7%)
  other arithmetic  6.79 us (3%)
    all_gather x1, waiting for transfers between devices, per_device(): col_blocks = lax.all_gather(col_emb, ROW, axis=0)  41.5 us
    pallas_call x2, Pallas kernels, part_grads(): pl.pallas_call(functools.partial(part_kernel, near=near), name='near_grad...  35.1 us
    reduce_scatter x1, waiting for transfers between devices, per_device(): lax.psum_scatter(row_term, 'col', scatter_dimension=0, tiled=False)  27.2 us
    all_to_all x1, starting transfers between devices, per_device(): lax.all_to_all(blocks.reshape(-1, slots_each, sub_rows, sub_cols), ALL, s...  14.5 us
    ppermute x8, starting transfers between devices, swap_sum(): lax.ppermute(value, axis, [(i, i ^ bit) for i in range(size)])  12.5 us
    ppermute x8, waiting for transfers between devices, swap_sum(): lax.ppermute(value, axis, [(i, i ^ bit) for i in range(size)])  11.4 us
    pallas_call x4, Pallas kernels, stack_cols(): pl.pallas_call(stack_kernel, name='stack_near' if near else 'stack_far',...  10.5 us
    pallas_call x1, Pallas kernels, sort_slots(): pl.pallas_call(functools.partial(sort_kernel, columns=columns), name='sor...  7.99 us
  transfers between devices with their start and end apart: 14, of which 12 were waited for; matrix products, arithmetic and copies ran while one was open for 3% of the time, Pallas kernels for 21%

profile of v5, /device:TPU:16, one launch (start us, length us, event | category | flops | bytes accessed | tf_op | source)
XLA Modules:
  0.0 207.7 jit_solution(3425908864375400524)
XLA Ops:
  7.9 14.5 %all-to-all-start = ((f32[256,2,8,128]{3,2,1,0:T(8,128)}), f32[256,2,8,128]{3,2,1,0:T(8,128)S(1)}, u32[]{:S(2)}, u32[]{:S(2)}) async-start(f32[256,2,8,128]{3,2,1,0:T(8,128)} %bitcast.26), calls=%async_computation | async-start | bytes 4194304 | tf_op jit(solution)/shard_map/all_to_all | solution.py:351
  23.9 8.0 %sort_slots.1 = (s32[512]{0:T(512)}, s32[512]{0:T(512)}, s32[5]{0:T(128)}) custom-call(s32[512]{0:T(512)} %select_n.5.target, s32[1]{0:T(128)} %bitcast.4.core), custom_call_target="tpu_custom_call" | custom-call | tf_op jit(solution)/shard_map/sort_slots/pallas_call | solution.py:141
  31.9 41.5 %all-gather.7.cloned.1.call-done = f32[32,300,128]{2,1,0:T(8,128)} async-done(((f32[1,300,128]{2,1,0:T(8,128)}), f32[32,300,128]{2,1,0:T(8,128)}) %all-gather.7.cloned.1.call-update) | async-done | bytes 4915216 | tf_op jit(solution)/shard_map/all_gather | solution.py:344
  73.4 1.6 all-to-all-done
  75.0 5.7 %place_counts.1 = (f32[512,8,128]{2,1,0:T(8,128)S(1)}, f32[48,128]{1,0:T(8,128)S(1)}) custom-call(s32[512]{0:T(512)} %select_n.5.target, s32[512]{0:T(512)S(1)} %convert_element_type.4.alive, f32[512,8,128]{2,1,0:T(8,128)S(1)} %bitcast.21), custom_call_target="tpu_custom_call" | custom-call | tf_op jit(solution)/shard_map/place_counts/pallas_call | solution.py:76
  82.0 2.4 %collective-permute-done = f32[16,128]{1,0:T(8,128)S(1)} collective-permute-done((f32[16,128]{1,0:T(8,128)S(1)}, f32[16,128]{1,0:T(8,128)S(1)}, u32[]{:S(2)}, u32[]{:S(2)}) %collective-permute-start) | collective-permute-done | bytes 8224 | tf_op jit(solution)/shard_map/ppermute | solution.py:328
  85.3 3.8 %collective-permute-done.1 = f32[16,128]{1,0:T(8,128)S(1)} collective-permute-done((f32[16,128]{1,0:T(8,128)S(1)}, f32[16,128]{1,0:T(8,128)S(1)}, u32[]{:S(2)}, u32[]{:S(2)}) %collective-permute-start.1) | collective-permute-done | bytes 8224 | tf_op jit(solution)/shard_map/ppermute | solution.py:328
  89.1 3.4 %collective-permute-start.2 = (f32[16,128]{1,0:T(8,128)S(1)}, f32[16,128]{1,0:T(8,128)S(1)}, u32[]{:S(2)}, u32[]{:S(2)}) collective-permute-start(f32[16,128]{1,0:T(8,128)S(1)} %add.36), channel_id=1, source_target_pairs={{0,4},{1,5},{2,6},{3,7},{4,0},{5,1},{6,2},{7,3},{8,12},{9,13},{10,... | collective-permute-start | bytes 24584 | tf_op jit(solution)/shard_map/ppermute | solution.py:328
  92.6 2.6 %stack_far.2.rest_0_ = bf16[1024,2048]{1,0:T(8,128)(2,1)} custom-call(s32[1]{0:T(128)} %bitcast.4.core, f32[16,2,300,128]{3,2,1,0:T(8,128)} %bitcast.22), custom_call_target="tpu_custom_call" | custom-call | tf_op jit(solution)/shard_map/stack_far/pallas_call | solution.py:210
  95.2 1.5 collective-permute-done.2
  98.0 2.1 %collective-permute-start.4 = (f32[40,128]{1,0:T(8,128)S(1)}, f32[40,128]{1,0:T(8,128)S(1)}, u32[]{:S(2)}, u32[]{:S(2)}) collective-permute-start(f32[40,128]{1,0:T(8,128)S(1)} %fusion.1), channel_id=1, source_target_pairs={{0,16},{16,0},{32,48},{48,32},{1,17},{17,1},{33,49},{49,33},{2,18}... | collective-permute-start | bytes 61448 | tf_op jit(solution)/shard_map/ppermute | solution.py:328
  100.1 2.6 %stack_far.3.col_stack = bf16[1024,2048]{1,0:T(8,128)(2,1)} custom-call(s32[1]{0:T(128)} %bitcast.4.core, f32[16,2,300,128]{3,2,1,0:T(8,128)} %bitcast.23, bf16[1024,2048]{1,0:T(8,128)(2,1)} %stack_far.2.rest_0_), custom_call_target="tpu_custom_call", output_to_operand_aliasing={{}: (2, {})} | custom-call | tf_op jit(solution)/shard_map/stack_far/pallas_call | solution.py:210
  103.5 2.6 %stack_near.2.rest_0_ = bf16[1024,2048]{1,0:T(8,128)(2,1)} custom-call(s32[1]{0:T(128)} %bitcast.4.core, f32[16,2,300,128]{3,2,1,0:T(8,128)} %bitcast.24), custom_call_target="tpu_custom_call" | custom-call | tf_op jit(solution)/shard_map/stack_near/pallas_call | solution.py:210
  106.1 2.0 collective-permute-done.5
  108.8 2.6 %stack_near.3.col_stack = bf16[1024,2048]{1,0:T(8,128)(2,1)} custom-call(s32[1]{0:T(128)} %bitcast.4.core, f32[16,2,300,128]{3,2,1,0:T(8,128)} %bitcast.25, bf16[1024,2048]{1,0:T(8,128)(2,1)} %stack_near.2.rest_0_), custom_call_target="tpu_custom_call", output_to_operand_aliasing={{}: (2, {})} | custom-call | tf_op jit(solution)/shard_map/stack_near/pallas_call | solution.py:210
  111.9 1.6 all-gather.9.cloned.1.call-done.row_blocks
  113.4 3.2 %collective-permute-start.7 = (f32[40,128]{1,0:T(8,128)S(1)}, f32[40,128]{1,0:T(8,128)S(1)}, u32[]{:S(2)}, u32[]{:S(2)}) collective-permute-start(f32[40,128]{1,0:T(8,128)S(1)} %add.41), channel_id=1, source_target_pairs={{0,128},{64,192},{128,0},{192,64},{1,129},{65,193},{129,1},{193,65... | collective-permute-start | bytes 61448 | tf_op jit(solution)/shard_map/ppermute | solution.py:328
  118.8 17.1 %far_grads.1 = (f32[16,304,128]{2,1,0:T(8,128)}, f32[8,304,128]{2,1,0:T(8,128)S(1)}) custom-call(s32[512]{0:T(512)S(1)} %copy-done.2, s32[512]{0:T(512)S(1)} %copy-done.3, s32[5]{0:T(128)S(1)} %copy-done.4, s32[1]{0:T(128)} %bitcast.4.core, bf16[1024,1024]{1,0:T(8,128)(2,1)S(1)} %get-tuple-element.60.row_turned, ...), custom_call_target="tpu_custom_call" | custom-call | tf_op jit(solution)/shard_map/far_grads/pallas_call | solution.py:299
  136.0 18.0 %near_grads.1 = (f32[16,304,128]{2,1,0:T(8,128)S(1)}, f32[8,304,128]{2,1,0:T(8,128)}) custom-call(s32[512]{0:T(512)S(1)} %copy-done.2, s32[512]{0:T(512)S(1)} %copy-done.3, s32[5]{0:T(128)S(1)} %copy-done.4, s32[1]{0:T(128)} %bitcast.4.core, bf16[1024,1024]{1,0:T(8,128)(2,1)S(1)} %get-tuple-element.60.row_turned, ...), custom_call_target="tpu_custom_call" | custom-call | tf_op jit(solution)/shard_map/near_grads/pallas_call | solution.py:299
  154.0 3.5 %add.44 = f32[16,304,128]{2,1,0:T(8,128)} add(f32[16,304,128]{2,1,0:T(8,128)S(1)} %get-tuple-element.68, f32[16,304,128]{2,1,0:T(8,128)} %collective-permute-done.8) | non-fusion elementwise | flops 622592 | bytes 7471104 | tf_op jit(solution)/shard_map/add | solution.py:385
  157.5 7.6 %all-to-all-start.1 = ((f32[16,304,128]{2,1,0:T(8,128)}), f32[16,304,128]{2,1,0:T(8,128)S(1)}, u32[]{:S(2)}, u32[]{:S(2)}) async-start(f32[16,304,128]{2,1,0:T(8,128)} %add.44), calls=%async_computation.2 | async-start | bytes 4980736 | tf_op jit(solution)/shard_map/all_to_all | solution.py:386
  165.1 27.2 %reduce-scatter.2.cloned.1.call-done = f32[1,304,128]{2,1,0:T(8,128)} async-done(((f32[8,304,128]{2,1,0:T(8,128)}), f32[1,304,128]{2,1,0:T(8,128)}) %reduce-scatter.2.cloned.1.call-update) | async-done | bytes 155664 | tf_op jit(solution)/shard_map/reduce_scatter | solution.py:384
  192.3 1.7 fusion
  194.0 6.3 %all-to-all-done.1 = f32[16,304,128]{2,1,0:T(8,128)S(1)} async-done(((f32[16,304,128]{2,1,0:T(8,128)}), f32[16,304,128]{2,1,0:T(8,128)S(1)}, u32[]{:S(2)}, u32[]{:S(2)}) %all-to-all-start.1) | async-done | bytes 2490400 | tf_op jit(solution)/shard_map/all_to_all | solution.py:386
  (66 shorter events, 10.7 us)
Async XLA Ops:
  7.2 15.3 %copy-start.10 = (s32[1,1,8,32]{3,2,1,0:T(8,128)S(1)}, s32[1,1,8,32]{3,2,1,0:T(8,128)}, u32[]{:S(2)}) copy-start(s32[1,1,8,32]{3,2,1,0:T(8,128)} %param.9) | copy-start | bytes 3076
  7.2 15.6 %copy-start.9 = (s32[1,1,8,32,2]{3,4,2,1,0:T(2,128)S(1)}, s32[1,1,8,32,2]{3,4,2,1,0:T(2,128)}, u32[]{:S(2)}) copy-start(s32[1,1,8,32,2]{3,4,2,1,0:T(2,128)} %param.8) | copy-start | bytes 6148
  7.2 66.1 %all-gather.7.cloned.1.call-start = ((), (), s32[]{:S(2)}) async-start(), calls=%async_computation.4 | async-start | bytes 5136384 | tf_op jit(solution)/shard_map/all_gather | solution.py:344
  7.9 67.1 %all-to-all-start = ((f32[256,2,8,128]{3,2,1,0:T(8,128)}), f32[256,2,8,128]{3,2,1,0:T(8,128)S(1)}, u32[]{:S(2)}, u32[]{:S(2)}) async-start(f32[256,2,8,128]{3,2,1,0:T(8,128)} %bitcast.26), calls=%async_computation | async-start | bytes 4194304 | tf_op jit(solution)/shard_map/all_to_all | solution.py:351
  22.4 91.0 %all-gather.9.cloned.1.call-start = ((), (), s32[]{:S(2)}) async-start(), calls=%async_computation.5 | async-start | bytes 1400832 | tf_op jit(solution)/shard_map/all_gather | solution.py:348
  73.4 119.0 %reduce-scatter.2.cloned.1.call-start = ((), (), s32[]{:S(2)}) async-start(), calls=%async_computation.3 | async-start | bytes 1400832 | tf_op jit(solution)/shard_map/reduce_scatter | solution.py:384
  80.7 14.5 %copy-start = (f32[512,8,128]{2,1,0:T(8,128)}, f32[512,8,128]{2,1,0:T(8,128)S(1)}, u32[]{:S(2)}) copy-start(f32[512,8,128]{2,1,0:T(8,128)S(1)} %get-tuple-element.63.counts_far) | copy-start | bytes 6291460
  80.7 3.7 %collective-permute-start = (f32[16,128]{1,0:T(8,128)S(1)}, f32[16,128]{1,0:T(8,128)S(1)}, u32[]{:S(2)}, u32[]{:S(2)}) collective-permute-start(f32[16,128]{1,0:T(8,128)S(1)} %slice.30), channel_id=1, source_target_pairs={{0,1},{1,0},{2,3},{3,2},{4,5},{5,4},{6,7},{7,6},{8,9},{9,8},{10,11... | collective-permute-start | bytes 24584 | tf_op jit(solution)/shard_map/ppermute | solution.py:328
  84.4 4.7 %collective-permute-start.1 = (f32[16,128]{1,0:T(8,128)S(1)}, f32[16,128]{1,0:T(8,128)S(1)}, u32[]{:S(2)}, u32[]{:S(2)}) collective-permute-start(f32[16,128]{1,0:T(8,128)S(1)} %slice_add_fusion), channel_id=1, source_target_pairs={{0,2},{1,3},{2,0},{3,1},{4,6},{5,7},{6,4},{7,5},{8,10},{9,11},{10,... | collective-permute-start | bytes 24584 | tf_op jit(solution)/shard_map/ppermute | solution.py:328
  89.1 7.6 %collective-permute-start.2 = (f32[16,128]{1,0:T(8,128)S(1)}, f32[16,128]{1,0:T(8,128)S(1)}, u32[]{:S(2)}, u32[]{:S(2)}) collective-permute-start(f32[16,128]{1,0:T(8,128)S(1)} %add.36), channel_id=1, source_target_pairs={{0,4},{1,5},{2,6},{3,7},{4,0},{5,1},{6,2},{7,3},{8,12},{9,13},{10,... | collective-permute-start | bytes 24584 | tf_op jit(solution)/shard_map/ppermute | solution.py:328
  96.7 1.3 collective-permute-start.3
  98.0 4.7 %collective-permute-start.4 = (f32[40,128]{1,0:T(8,128)S(1)}, f32[40,128]{1,0:T(8,128)S(1)}, u32[]{:S(2)}, u32[]{:S(2)}) collective-permute-start(f32[40,128]{1,0:T(8,128)S(1)} %fusion.1), channel_id=1, source_target_pairs={{0,16},{16,0},{32,48},{48,32},{1,17},{17,1},{33,49},{49,33},{2,18}... | collective-permute-start | bytes 61448 | tf_op jit(solution)/shard_map/ppermute | solution.py:328
  102.7 5.4 %collective-permute-start.5 = (f32[40,128]{1,0:T(8,128)S(1)}, f32[40,128]{1,0:T(8,128)S(1)}, u32[]{:S(2)}, u32[]{:S(2)}) collective-permute-start(f32[40,128]{1,0:T(8,128)S(1)} %add.39), channel_id=1, source_target_pairs={{0,32},{16,48},{32,0},{48,16},{1,33},{17,49},{33,1},{49,17},{2,34}... | collective-permute-start | bytes 61448 | tf_op jit(solution)/shard_map/ppermute | solution.py:328
  108.1 3.8 %collective-permute-start.6 = (f32[40,128]{1,0:T(8,128)S(1)}, f32[40,128]{1,0:T(8,128)S(1)}, u32[]{:S(2)}, u32[]{:S(2)}) collective-permute-start(f32[40,128]{1,0:T(8,128)S(1)} %add.40), channel_id=1, source_target_pairs={{0,64},{64,0},{128,192},{192,128},{1,65},{65,1},{129,193},{193,129... | collective-permute-start | bytes 61448 | tf_op jit(solution)/shard_map/ppermute | solution.py:328
  108.8 10.0 %copy-start.2 = (s32[512]{0:T(512)S(1)}, s32[512]{0:T(512)}, u32[]{:S(2)}) copy-start(s32[512]{0:T(512)} %get-tuple-element.40.order) | copy-start | bytes 6148
  108.8 10.0 %copy-start.3 = (s32[512]{0:T(512)S(1)}, s32[512]{0:T(512)}, u32[]{:S(2)}) copy-start(s32[512]{0:T(512)} %get-tuple-element.41.spots) | copy-start | bytes 6148
  108.8 10.0 %copy-start.4 = (s32[5]{0:T(128)S(1)}, s32[5]{0:T(128)}, u32[]{:S(2)}) copy-start(s32[5]{0:T(128)} %get-tuple-element.42.offsets) | copy-start | bytes 64
  113.4 5.3 %collective-permute-start.7 = (f32[40,128]{1,0:T(8,128)S(1)}, f32[40,128]{1,0:T(8,128)S(1)}, u32[]{:S(2)}, u32[]{:S(2)}) collective-permute-start(f32[40,128]{1,0:T(8,128)S(1)} %add.41), channel_id=1, source_target_pairs={{0,128},{64,192},{128,0},{192,64},{1,129},{65,193},{129,1},{193,65... | collective-permute-start | bytes 61448 | tf_op jit(solution)/shard_map/ppermute | solution.py:328
  135.9 18.1 %collective-permute-start.8 = (f32[16,304,128]{2,1,0:T(8,128)}, f32[16,304,128]{2,1,0:T(8,128)}, u32[]{:S(2)}, u32[]{:S(2)}) collective-permute-start(f32[16,304,128]{2,1,0:T(8,128)} %get-tuple-element.69), channel_id=1, source_target_pairs={{0,8},{8,0},{1,9},{9,1},{2,10},{10,2},{3,11},{11,3},{4,12},{12,4},... | collective-permute-start | bytes 7471112 | tf_op jit(solution)/shard_map/ppermute | solution.py:382
  157.5 34.8 %copy-start.5 = (f32[300,128]{1,0:T(8,128)S(1)}, f32[300,128]{1,0:T(8,128)}, u32[]{:S(2)}) copy-start(f32[300,128]{1,0:T(8,128)} %param.10) | copy-start | bytes 460804
  157.5 34.8 %copy-start.7 = (f32[300,128]{1,0:T(8,128)S(1)}, f32[300,128]{1,0:T(8,128)}, u32[]{:S(2)}) copy-start(f32[300,128]{1,0:T(8,128)} %param.12) | copy-start | bytes 460804
  157.5 42.7 %all-to-all-start.1 = ((f32[16,304,128]{2,1,0:T(8,128)}), f32[16,304,128]{2,1,0:T(8,128)S(1)}, u32[]{:S(2)}, u32[]{:S(2)}) async-start(f32[16,304,128]{2,1,0:T(8,128)} %add.44), calls=%async_computation.2 | async-start | bytes 4980736 | tf_op jit(solution)/shard_map/all_to_all | solution.py:386
  165.1 35.3 %copy-start.6 = (f32[300,128]{1,0:T(8,128)S(1)}, f32[300,128]{1,0:T(8,128)}, u32[]{:S(2)}) copy-start(f32[300,128]{1,0:T(8,128)} %param.11) | copy-start | bytes 460804
  165.1 35.3 %copy-start.8 = (f32[300,128]{1,0:T(8,128)S(1)}, f32[300,128]{1,0:T(8,128)}, u32[]{:S(2)}) copy-start(f32[300,128]{1,0:T(8,128)} %param.13) | copy-start | bytes 460804
  (1 other events, 1.3 us)
Sparse Core Ops, SparseCore 0:
  10.6 62.7 all-gather.6
  75.1 38.2 all-gather.8
  154.1 38.1 reduce-scatter.1

commit v6 on v5

--- a/solution.py
+++ b/solution.py
@@ -188,18 +188,15 @@
 
 def stack_kernel(core, col_blocks, *rest):
     out = rest[-1]
-    deep = out.shape[0]
-    dim = -(-col_blocks.shape[2] // 16) * 16
+    dim = out.shape[0] // 2
     for i in range(col_blocks.shape[0]):
         high, low = split(taller(col_blocks[i, 0], dim))
         here = slice(i * LANES, (i + 1) * LANES)
         out[0:dim, here] = high
-        out[dim : 2 * dim, here] = low
-        out[2 * dim : 3 * dim, here] = high
-        out[3 * dim :, here] = jnp.zeros((deep - 3 * dim, LANES), BF16)
-
-
-def stack_cols(core, col_blocks, deep, near, earlier=None):
+        out[dim:, here] = low
+
+
+def stack_cols(core, col_blocks, padded, near, earlier=None):
     n_col, dim, _ = col_blocks.shape
     seats = n_col // CORES
     step = BLOCKS // 2
@@ -215,29 +212,43 @@
             grid=(seats // step // 2,),
             in_specs=[pl.BlockSpec((step, 1, dim, LANES), pick)]
             + [pl.BlockSpec(memory_space=pltpu.HBM)] * len(ready),
-            out_specs=pl.BlockSpec((deep, step * LANES), lambda g, *_: (0, first + g)),
+            out_specs=pl.BlockSpec((2 * padded, step * LANES), lambda g, *_: (0, first + g)),
         ),
-        out_shape=pltpu.HBM((deep, seats * LANES), BF16),
+        out_shape=pltpu.HBM((2 * padded, seats * LANES), BF16),
         input_output_aliases={2: 0} if ready else {},
         compiler_params=pltpu.CompilerParams(vmem_limit_bytes=14 << 20),
     )(core, col_blocks, *ready)
 
 
 def part_kernel(
-    order, spots, offsets, core, row_turned, row_stack, col_stack, counts_far, masses, *rest, near
+    order, spots, offsets, core, row_turned, row_stack, stack_far, counts_far, masses, *rest, near, first, merge
 ):
-    col_term, row_term, scores, grads, row_bias, col_bias, counts, arrival = rest[-8:]
+    merging = []
+    if merge:
+        *merging, rest = rest[1], rest[2], *rest[-2:], rest[:1] + rest[3:-2]
+    col_term, row_term, scores, grads, row_bias, col_bias, counts, stacks = rest[-10:-2]
+    arrival, stack_arrivals = rest[-2:]
     padded, n_row = row_term.shape[1], row_term.shape[0]
     n_col = col_bias.shape[0]
-    ct = pl.program_id(0)
-    chunks = pl.num_programs(0)
+    step = pl.program_id(0)
+    ct = step + first
+    half_chunks = n_col // CORES // BLOCKS
     side = core[0] if near else 1 - core[0]
 
+    width = BLOCKS * LANES
     fetch = pltpu.make_async_copy(counts_far, counts, arrival)
 
-    @pl.when(ct == 0)
+    def bring(chunk):
+        cols = pl.ds(pl.multiple_of((first + chunk) * width, width), width)
+        kept = stacks.at[chunk, pl.ds(0, 2 * padded), :]
+        return pltpu.make_async_copy(stack_far.at[:, cols], kept, stack_arrivals.at[chunk])
+
+    @pl.when(step == 0)
     def _():
+        bring(0).start()
         fetch.start()
+        for chunk in range(1, stacks.shape[0]):
+            bring(chunk).start()
         log_total = jnp.log(masses[n_col + n_row : n_col + n_row + 1, :])
         col_bias[...] = 0.5 * (jnp.log(masses[0:n_col, :]) - log_total)
         row_logs = 0.5 * jnp.log(masses[n_col : n_col + n_row, :])
@@ -246,24 +257,27 @@
             row_bias[i * LANES // 8 : (i + 1) * LANES // 8] = turned.reshape(-1, 8, LANES)
         row_term[...] = rest[0][...] if near else jnp.zeros(row_term.shape, F32)
 
-    product = jnp.dot(row_turned[...], col_stack[...], preferred_element_type=F32)
+    bring(step).wait()
+    stacks[step, 2 * padded : 3 * padded, :] = stacks[step, 0:padded, :]
+    stacks[step, 3 * padded :, :] = jnp.zeros((stacks.shape[1] - 3 * padded, width), BF16)
+    product = jnp.dot(row_turned[...], stacks[step], preferred_element_type=F32)
     for k in range(BLOCKS):
         bias = col_bias[pl.ds((ct * BLOCKS + k) * 2 + side, 1), :]
         value = product[:, k * LANES : (k + 1) * LANES].reshape(-1, 8, LANES) + row_bias[...] + bias
         scores[:, k] = value
         grads[:, k] = 0.5 * jnp.tanh(value) + 0.5
-    here = ct + (chunks if near else 0)
+    here = ct + (half_chunks if near else 0)
     begin = offsets[here]
     end = offsets[here + 1]
 
-    @pl.when(ct == 0)
+    @pl.when(step == 0)
     def _():
         fetch.wait()
 
-    def counted(step, carry):
+    def counted(group, carry):
         found = []
         for u in range(8):
-            at = jnp.minimum(begin + step * 8 + u, end - 1)
+            at = jnp.minimum(begin + group * 8 + u, end - 1)
             spot = spots[at]
             row, k = lax.shift_right_logical(spot, BLOCKS.bit_length() - 1), spot & (BLOCKS - 1)
             count = counts[order[at]]
@@ -274,6 +288,15 @@
         return carry
 
     lax.fori_loop(0, lax.shift_right_logical(end - begin + 7, 3), counted, 0)
+    if merge:
+        piece, swapped, merged, leaves = merging
+        merged[0 : first * BLOCKS] = swapped[0 : first * BLOCKS] + piece[...]
+        parts = [pl.ds(0, first * BLOCKS), pl.ds(first * BLOCKS, BLOCKS)]
+        leave = [
+            pltpu.make_async_copy(merged.at[part], col_term.at[part], leaves.at[i])
+            for i, part in enumerate(parts)
+        ]
+        leave[0].start()
     pieces = [split(grads[:, k].reshape(-1, LANES)) for k in range(BLOCKS)]
     high = jnp.concatenate([piece[0] for piece in pieces], axis=1)
     low = jnp.concatenate([piece[1] for piece in pieces], axis=1)
@@ -281,47 +304,69 @@
     rest_ = jnp.dot(row_stack[0:padded, :], low, preferred_element_type=F32)
     total = both[0:padded] + both[padded:] + rest_
     for k in range(BLOCKS):
-        col_term[k] = total[:, k * LANES : (k + 1) * LANES]
+        block = total[:, k * LANES : (k + 1) * LANES]
+        if merge:
+            merged[first * BLOCKS + k] = swapped[first * BLOCKS + k] + block
+        else:
+            col_term[k] = block
+    if merge:
+        leave[1].start()
     turned = (((1,), (1,)), ((), ()))
-    both = lax.dot_general(col_stack[0 : 2 * padded, :], high, turned, preferred_element_type=F32)
-    rest_ = lax.dot_general(col_stack[0:padded, :], low, turned, preferred_element_type=F32)
+    both = lax.dot_general(stacks[step, 0 : 2 * padded, :], high, turned, preferred_element_type=F32)
+    rest_ = lax.dot_general(stacks[step, 0:padded, :], low, turned, preferred_element_type=F32)
     total = both[0:padded] + both[padded:] + rest_
     for i in range(n_row):
         row_term[i] = row_term[i] + total[:, i * LANES : (i + 1) * LANES]
-
-
-def part_grads(scalars, row_turned, row_stack, col_stack, counts, masses, earlier):
+    if merge:
+        for copy in leave:
+            copy.wait()
+
+
+def part_grads(scalars, row_turned, row_stack, col_stack, counts, masses, earlier, first, count, extra=()):
     words, deep = row_turned.shape
     padded = row_stack.shape[0] // 2
     blocks = col_stack.shape[1] // LANES
     near = earlier is not None
+    merge = bool(extra)
     ready = [earlier] if near else []
+    out_blocks = blocks if merge else count * BLOCKS
+    scratch = [
+        pltpu.VMEM((blocks, padded, LANES), F32),
+        pltpu.SemaphoreType.DMA((2,)),
+    ]
     return pl.pallas_call(
-        functools.partial(part_kernel, near=near),
-        name="near_grads" if near else "far_grads",
+        functools.partial(part_kernel, near=near, first=first, merge=merge),
+        name="merge_grads" if merge else "near_grads" if near else "far_grads",
         grid_spec=pltpu.PrefetchScalarGridSpec(
             num_scalar_prefetch=4,
-            grid=(blocks // BLOCKS,),
+            grid=(count,),
             in_specs=whole(2)
-            + [pl.BlockSpec((deep, BLOCKS * LANES), lambda g, *_: (0, g))]
-            + [pl.BlockSpec(memory_space=pltpu.HBM)]
-            + whole(1 + len(ready)),
-            out_specs=[pl.BlockSpec((BLOCKS, padded, LANES), lambda g, *_: (g, 0, 0)), pl.BlockSpec((words // LANES, padded, LANES), lambda g, *_: (0, 0, 0))],
+            + [pl.BlockSpec(memory_space=pltpu.HBM)] * 2
+            + whole(1 + len(ready) + len(extra)),
+            out_specs=[
+                pl.BlockSpec(memory_space=pltpu.HBM)
+                if merge
+                else pl.BlockSpec((BLOCKS, padded, LANES), lambda g, *_: (g, 0, 0)),
+                pl.BlockSpec((words // LANES, padded, LANES), lambda g, *_: (0, 0, 0)),
+            ],
             scratch_shapes=[
                 pltpu.VMEM((words // 8, BLOCKS, 8, LANES), F32),
                 pltpu.VMEM((words // 8, BLOCKS, 8, LANES), F32),
                 pltpu.VMEM((words // 8, 8, LANES), F32),
                 pltpu.VMEM((blocks * CORES, LANES), F32),
                 pltpu.VMEM(counts.shape, F32),
+                pltpu.VMEM((count, deep, BLOCKS * LANES), BF16),
                 pltpu.SemaphoreType.DMA(()),
-            ],
+                pltpu.SemaphoreType.DMA((count,)),
+            ]
+            + (scratch if merge else []),
         ),
         out_shape=[
-            jax.ShapeDtypeStruct((blocks, padded, LANES), F32),
-            (pltpu.HBM if near else jax.ShapeDtypeStruct)((words // LANES, padded, LANES), F32),
+            (pltpu.HBM if merge else jax.ShapeDtypeStruct)((out_blocks, padded, LANES), F32),
+            (pltpu.HBM if merge else jax.ShapeDtypeStruct)((words // LANES, padded, LANES), F32),
         ],
-        compiler_params=pltpu.CompilerParams(vmem_limit_bytes=36 << 20),
-    )(*scalars, row_turned, row_stack, pltpu.with_memory_space_constraint(col_stack, pltpu.HBM), pltpu.with_memory_space_constraint(counts, pltpu.HBM), masses, *ready)
+        compiler_params=pltpu.CompilerParams(vmem_limit_bytes=40 << 20),
+    )(*scalars, row_turned, row_stack, pltpu.with_memory_space_constraint(col_stack, pltpu.HBM), pltpu.with_memory_space_constraint(counts, pltpu.HBM), masses, *ready, *extra)
 
 
 def swap_sum(value, axis, size, bit):
@@ -359,30 +404,35 @@
     row_part = swap_sum(row_part, "col", n_z, 2)
     row_part, col_blocks = lax.optimization_barrier((row_part, col_blocks))
     row_part = swap_sum(row_part, "col", n_z, 4)
-    far_stack = stack_cols(core, col_blocks, deep, False)
+    far_stack = stack_cols(core, col_blocks, padded, False)
     row_part, far_stack = lax.optimization_barrier((row_part, far_stack))
     col_part = jnp.concatenate([part[:n_col], row_part[n_row:]], axis=0)
     col_part = swap_sum(col_part, "core", CORES, 1)
     col_part, far_stack, col_blocks = lax.optimization_barrier((col_part, far_stack, col_blocks))
     col_part = swap_sum(col_part, "y", GRID_Y, 1)
-    far_stack = stack_cols(core, col_blocks, deep, False, far_stack)
+    far_stack = stack_cols(core, col_blocks, padded, False, far_stack)
     col_part, far_stack, col_blocks = lax.optimization_barrier((col_part, far_stack, col_blocks))
     col_part = swap_sum(col_part, "y", GRID_Y, 2)
-    near_stack = stack_cols(core, col_blocks, deep, True)
+    near_stack = stack_cols(core, col_blocks, padded, True)
     col_part, near_stack, col_blocks = lax.optimization_barrier((col_part, near_stack, col_blocks))
     col_part = swap_sum(col_part, "x", GRID_X, 1)
-    near_stack = stack_cols(core, col_blocks, deep, True, near_stack)
+    near_stack = stack_cols(core, col_blocks, padded, True, near_stack)
     col_part, near_stack = lax.optimization_barrier((col_part, near_stack))
     col_part, row_blocks = lax.optimization_barrier((col_part, row_blocks))
     row_stack, row_turned = turn(row_blocks, padded, deep)
     col_part = swap_sum(col_part, "x", GRID_X, 2)
     masses = jnp.concatenate([col_part[:n_col], row_part[:n_row], col_part[n_col:]], axis=0)
     scalars = (order, spots, offsets, core)
-    far_term, row_term = part_grads(scalars, row_turned, row_stack, far_stack, counts, masses, None)
+    chunks = n_col // CORES // BLOCKS
+    early = chunks // 2
+    inputs = (scalars, row_turned, row_stack)
+    far_term, row_term = part_grads(*inputs, far_stack, counts, masses, None, 0, chunks)
     swapped = lax.ppermute(far_term, "core", [(0, 1), (1, 0)])
-    near_term, row_term = part_grads(scalars, row_turned, row_stack, near_stack, counts, masses, row_term)
+    piece, row_term = part_grads(*inputs, near_stack, counts, masses, row_term, 0, early)
+    half, row_term = part_grads(
+        *inputs, near_stack, counts, masses, row_term, early, chunks - early, (piece, swapped)
+    )
     row_grad = lax.psum_scatter(row_term, "col", scatter_dimension=0, tiled=False)
-    half = near_term + swapped
     col_grad = jnp.sum(lax.all_to_all(half, ("x", "y"), split_axis=0, concat_axis=0, tiled=True), axis=0)
     loss_scale = 4.0 * float(words * n_z * n_row_axis) ** (-0.5)
     row_share = row_grad[:dim] * loss_scale

time: 208 us -> 214 us (1.029)
  waiting for transfers between devices: 90.2 us -> 98.2 us
  other arithmetic: 6.79 us -> 3.29 us
    all_to_all x1, waiting for transfers between devices: 6.26 us -> 34.5 us  [per_device(): lax.all_to_all(half, ('x', 'y'), split_axis=0, concat_axis=0, tiled=True)]
    reduce_scatter x1, waiting for transfers between devices: 27.2 us -> 5.13 us  [per_device(): lax.psum_scatter(row_term, 'col', scatter_dimension=0, tiled=False)]
    add x1 -> x0, other arithmetic: 3.52 us -> none  [per_device(): half = near_term + swapped]
    pallas_call x2 -> x3, Pallas kernels: 35.1 us -> 37.4 us  [part_grads(): pl.pallas_call(functools.partial(part_kernel, near=near, first=first, mer...]
  transfers between devices with their start and end apart: 14 -> 14, of which waited for: 12 -> 12; matrix products, arithmetic and copies ran while one was open for 3% -> 1% of each run, Pallas kernels for 21% -> 16%
where the time goes in v6:
time: 214 us; the launch traced here: 213 us
  waiting for transfers between devices  98.2 us (46%)
  Pallas kernels  61 us (29%)
  starting transfers between devices  34.8 us (16%)
  between operations  14 us (7%)
  other arithmetic  3.29 us (2%)
    all_gather x1, waiting for transfers between devices, per_device(): col_blocks = lax.all_gather(col_emb, ROW, axis=0)  41.5 us
    pallas_call x3, Pallas kernels, part_grads(): pl.pallas_call(functools.partial(part_kernel, near=near, first=first, mer...  37.4 us
    all_to_all x1, waiting for transfers between devices, per_device(): lax.all_to_all(half, ('x', 'y'), split_axis=0, concat_axis=0, tiled=True)  34.5 us
    all_to_all x1, starting transfers between devices, per_device(): lax.all_to_all(blocks.reshape(-1, slots_each, sub_rows, sub_cols), ALL, s...  14.5 us
    ppermute x8, starting transfers between devices, swap_sum(): lax.ppermute(value, axis, [(i, i ^ bit) for i in range(size)])  12.6 us
    ppermute x8, waiting for transfers between devices, swap_sum(): lax.ppermute(value, axis, [(i, i ^ bit) for i in range(size)])  12.2 us
    pallas_call x4, Pallas kernels, stack_cols(): pl.pallas_call(stack_kernel, name='stack_near' if near else 'stack_far',...  9.19 us
    pallas_call x1, Pallas kernels, sort_slots(): pl.pallas_call(functools.partial(sort_kernel, columns=columns), name='sor...  7.99 us
  transfers between devices with their start and end apart: 14, of which 12 were waited for; matrix products, arithmetic and copies ran while one was open for 1% of the time, Pallas kernels for 16%

profile of v6, /device:TPU:16, one launch (start us, length us, event | category | flops | bytes accessed | tf_op | source)
XLA Modules:
  0.0 213.2 jit_solution(4222101214209176424)
XLA Ops:
  7.9 14.5 %all-to-all-start = ((f32[256,2,8,128]{3,2,1,0:T(8,128)}), f32[256,2,8,128]{3,2,1,0:T(8,128)S(1)}, u32[]{:S(2)}, u32[]{:S(2)}) async-start(f32[256,2,8,128]{3,2,1,0:T(8,128)} %bitcast.26), calls=%async_computation | async-start | bytes 4194304 | tf_op jit(solution)/shard_map/all_to_all | solution.py:396
  23.9 8.0 %sort_slots.1 = (s32[512]{0:T(512)}, s32[512]{0:T(512)}, s32[5]{0:T(128)}) custom-call(s32[512]{0:T(512)} %select_n.5.target, s32[1]{0:T(128)} %bitcast.4.core), custom_call_target="tpu_custom_call" | custom-call | tf_op jit(solution)/shard_map/sort_slots/pallas_call | solution.py:141
  31.9 41.5 %all-gather.7.cloned.1.call-done = f32[32,300,128]{2,1,0:T(8,128)} async-done(((f32[1,300,128]{2,1,0:T(8,128)}), f32[32,300,128]{2,1,0:T(8,128)}) %all-gather.7.cloned.1.call-update) | async-done | bytes 4915216 | tf_op jit(solution)/shard_map/all_gather | solution.py:389
  73.4 1.6 all-to-all-done
  75.0 5.7 %place_counts.1 = (f32[512,8,128]{2,1,0:T(8,128)S(1)}, f32[48,128]{1,0:T(8,128)S(1)}) custom-call(s32[512]{0:T(512)} %select_n.5.target, s32[512]{0:T(512)S(1)} %convert_element_type.4.alive, f32[512,8,128]{2,1,0:T(8,128)S(1)} %bitcast.21), custom_call_target="tpu_custom_call" | custom-call | tf_op jit(solution)/shard_map/place_counts/pallas_call | solution.py:76
  82.0 2.4 %collective-permute-done = f32[16,128]{1,0:T(8,128)S(1)} collective-permute-done((f32[16,128]{1,0:T(8,128)S(1)}, f32[16,128]{1,0:T(8,128)S(1)}, u32[]{:S(2)}, u32[]{:S(2)}) %collective-permute-start) | collective-permute-done | bytes 8224 | tf_op jit(solution)/shard_map/ppermute | solution.py:373
  85.3 3.8 %collective-permute-done.1 = f32[16,128]{1,0:T(8,128)S(1)} collective-permute-done((f32[16,128]{1,0:T(8,128)S(1)}, f32[16,128]{1,0:T(8,128)S(1)}, u32[]{:S(2)}, u32[]{:S(2)}) %collective-permute-start.1) | collective-permute-done | bytes 8224 | tf_op jit(solution)/shard_map/ppermute | solution.py:373
  89.1 3.3 %collective-permute-start.2 = (f32[16,128]{1,0:T(8,128)S(1)}, f32[16,128]{1,0:T(8,128)S(1)}, u32[]{:S(2)}, u32[]{:S(2)}) collective-permute-start(f32[16,128]{1,0:T(8,128)S(1)} %add.33), channel_id=1, source_target_pairs={{0,4},{1,5},{2,6},{3,7},{4,0},{5,1},{6,2},{7,3},{8,12},{9,13},{10,... | collective-permute-start | bytes 24584 | tf_op jit(solution)/shard_map/ppermute | solution.py:373
  92.4 2.3 %stack_far.2.rest_0_ = bf16[608,2048]{1,0:T(8,128)(2,1)} custom-call(s32[1]{0:T(128)} %bitcast.4.core, f32[16,2,300,128]{3,2,1,0:T(8,128)} %bitcast.22), custom_call_target="tpu_custom_call" | custom-call | tf_op jit(solution)/shard_map/stack_far/pallas_call | solution.py:207
  94.7 1.9 collective-permute-done.2
  98.0 2.1 %collective-permute-start.4 = (f32[40,128]{1,0:T(8,128)S(1)}, f32[40,128]{1,0:T(8,128)S(1)}, u32[]{:S(2)}, u32[]{:S(2)}) collective-permute-start(f32[40,128]{1,0:T(8,128)S(1)} %fusion.1), channel_id=1, source_target_pairs={{0,16},{16,0},{32,48},{48,32},{1,17},{17,1},{33,49},{49,33},{2,18}... | collective-permute-start | bytes 61448 | tf_op jit(solution)/shard_map/ppermute | solution.py:373
  100.1 2.3 %stack_far.3 = bf16[608,2048]{1,0:T(8,128)(2,1)} custom-call(s32[1]{0:T(128)} %bitcast.4.core, f32[16,2,300,128]{3,2,1,0:T(8,128)} %bitcast.23, bf16[608,2048]{1,0:T(8,128)(2,1)} %stack_far.2.rest_0_), custom_call_target="tpu_custom_call", output_to_operand_aliasing={{}: (2, {})} | custom-call | tf_op jit(solution)/shard_map/stack_far/pallas_call | solution.py:207
  103.5 2.3 %stack_near.2.rest_0_ = bf16[608,2048]{1,0:T(8,128)(2,1)} custom-call(s32[1]{0:T(128)} %bitcast.4.core, f32[16,2,300,128]{3,2,1,0:T(8,128)} %bitcast.24), custom_call_target="tpu_custom_call" | custom-call | tf_op jit(solution)/shard_map/stack_near/pallas_call | solution.py:207
  105.8 2.0 collective-permute-done.5
  108.5 2.3 %stack_near.3.stack_far = bf16[608,2048]{1,0:T(8,128)(2,1)} custom-call(s32[1]{0:T(128)} %bitcast.4.core, f32[16,2,300,128]{3,2,1,0:T(8,128)} %bitcast.25, bf16[608,2048]{1,0:T(8,128)(2,1)} %stack_near.2.rest_0_), custom_call_target="tpu_custom_call", output_to_operand_aliasing={{}: (2, {})} | custom-call | tf_op jit(solution)/shard_map/stack_near/pallas_call | solution.py:207
  111.6 1.9 all-gather.9.cloned.1.call-done.row_blocks
  113.5 3.2 %collective-permute-start.7 = (f32[40,128]{1,0:T(8,128)S(1)}, f32[40,128]{1,0:T(8,128)S(1)}, u32[]{:S(2)}, u32[]{:S(2)}) collective-permute-start(f32[40,128]{1,0:T(8,128)S(1)} %add.38), channel_id=1, source_target_pairs={{0,128},{64,192},{128,0},{192,64},{1,129},{65,193},{129,1},{193,65... | collective-permute-start | bytes 61448 | tf_op jit(solution)/shard_map/ppermute | solution.py:373
  118.8 16.4 %far_grads.1 = (f32[16,304,128]{2,1,0:T(8,128)S(1)}, f32[8,304,128]{2,1,0:T(8,128)S(1)}) custom-call(s32[512]{0:T(512)S(1)} %copy-done.2, s32[512]{0:T(512)S(1)} %copy-done.3, s32[5]{0:T(128)S(1)} %copy-done.4, s32[1]{0:T(128)} %bitcast.4.core, bf16[1024,1024]{1,0:T(8,128)(2,1)S(1)} %get-tuple-element.62.row_turned, ...), custom_call_target="tpu_custom_call" | custom-call | tf_op jit(solution)/shard_map/far_grads/pallas_call | solution.py:337
  135.3 10.0 %near_grads.1 = (f32[8,304,128]{2,1,0:T(8,128)S(1)}, f32[8,304,128]{2,1,0:T(8,128)S(1)}) custom-call(s32[512]{0:T(512)S(1)} %copy-done.2, s32[512]{0:T(512)S(1)} %copy-done.3, s32[5]{0:T(128)S(1)} %copy-done.4, s32[1]{0:T(128)} %bitcast.4.core, bf16[1024,1024]{1,0:T(8,128)(2,1)S(1)} %get-tuple-element.62.row_turned, ...), custom_call_target="tpu_custom_call" | custom-call | tf_op jit(solution)/shard_map/near_grads/pallas_call | solution.py:337
  145.3 11.0 %merge_grads.1 = (f32[16,304,128]{2,1,0:T(8,128)}, f32[8,304,128]{2,1,0:T(8,128)}) custom-call(s32[512]{0:T(512)S(1)} %copy-done.2, s32[512]{0:T(512)S(1)} %copy-done.3, s32[5]{0:T(128)S(1)} %copy-done.4, s32[1]{0:T(128)} %bitcast.4.core, bf16[1024,1024]{1,0:T(8,128)(2,1)S(1)} %get-tuple-element.62.row_turned, ...), custom_call_target="tpu_custom_call" | custom-call | tf_op jit(solution)/shard_map/merge_grads/pallas_call | solution.py:337
  156.3 7.4 %all-to-all-start.1 = ((f32[16,304,128]{2,1,0:T(8,128)}), f32[16,304,128]{2,1,0:T(8,128)S(1)}, u32[]{:S(2)}, u32[]{:S(2)}) async-start(f32[16,304,128]{2,1,0:T(8,128)} %get-tuple-element.73), calls=%async_computation.2 | async-start | bytes 4980736 | tf_op jit(solution)/shard_map/all_to_all | solution.py:436
  164.5 34.5 %all-to-all-done.1 = f32[16,304,128]{2,1,0:T(8,128)S(1)} async-done(((f32[16,304,128]{2,1,0:T(8,128)}), f32[16,304,128]{2,1,0:T(8,128)S(1)}, u32[]{:S(2)}, u32[]{:S(2)}) %all-to-all-start.1) | async-done | bytes 2490400 | tf_op jit(solution)/shard_map/all_to_all | solution.py:436
  199.9 5.1 %reduce-scatter.2.cloned.1.call-done = f32[1,304,128]{2,1,0:T(8,128)} async-done(((f32[8,304,128]{2,1,0:T(8,128)}), f32[1,304,128]{2,1,0:T(8,128)}) %reduce-scatter.2.cloned.1.call-update) | async-done | bytes 155664 | tf_op jit(solution)/shard_map/reduce_scatter | solution.py:435
  205.0 1.7 fusion
  (66 shorter events, 12.1 us)
Async XLA Ops:
  7.2 66.2 %all-gather.7.cloned.1.call-start = ((), (), s32[]{:S(2)}) async-start(), calls=%async_computation.4 | async-start | bytes 5136384 | tf_op jit(solution)/shard_map/all_gather | solution.py:389
  7.9 14.6 %copy-start.9 = (s32[1,1,8,32,2]{3,4,2,1,0:T(2,128)S(1)}, s32[1,1,8,32,2]{3,4,2,1,0:T(2,128)}, u32[]{:S(2)}) copy-start(s32[1,1,8,32,2]{3,4,2,1,0:T(2,128)} %param.8) | copy-start | bytes 6148
  7.9 14.7 %copy-start.10 = (s32[1,1,8,32]{3,2,1,0:T(8,128)S(1)}, s32[1,1,8,32]{3,2,1,0:T(8,128)}, u32[]{:S(2)}) copy-start(s32[1,1,8,32]{3,2,1,0:T(8,128)} %param.9) | copy-start | bytes 3076
  7.9 67.1 %all-to-all-start = ((f32[256,2,8,128]{3,2,1,0:T(8,128)}), f32[256,2,8,128]{3,2,1,0:T(8,128)S(1)}, u32[]{:S(2)}, u32[]{:S(2)}) async-start(f32[256,2,8,128]{3,2,1,0:T(8,128)} %bitcast.26), calls=%async_computation | async-start | bytes 4194304 | tf_op jit(solution)/shard_map/all_to_all | solution.py:396
  22.4 91.0 %all-gather.9.cloned.1.call-start = ((), (), s32[]{:S(2)}) async-start(), calls=%async_computation.5 | async-start | bytes 1400832 | tf_op jit(solution)/shard_map/all_gather | solution.py:393
  80.7 14.0 %copy-start = (f32[512,8,128]{2,1,0:T(8,128)}, f32[512,8,128]{2,1,0:T(8,128)S(1)}, u32[]{:S(2)}) copy-start(f32[512,8,128]{2,1,0:T(8,128)S(1)} %get-tuple-element.65.counts_far) | copy-start | bytes 6291460
  80.7 3.7 %collective-permute-start = (f32[16,128]{1,0:T(8,128)S(1)}, f32[16,128]{1,0:T(8,128)S(1)}, u32[]{:S(2)}, u32[]{:S(2)}) collective-permute-start(f32[16,128]{1,0:T(8,128)S(1)} %slice.30), channel_id=1, source_target_pairs={{0,1},{1,0},{2,3},{3,2},{4,5},{5,4},{6,7},{7,6},{8,9},{9,8},{10,11... | collective-permute-start | bytes 24584 | tf_op jit(solution)/shard_map/ppermute | solution.py:373
  84.4 4.7 %collective-permute-start.1 = (f32[16,128]{1,0:T(8,128)S(1)}, f32[16,128]{1,0:T(8,128)S(1)}, u32[]{:S(2)}, u32[]{:S(2)}) collective-permute-start(f32[16,128]{1,0:T(8,128)S(1)} %slice_add_fusion), channel_id=1, source_target_pairs={{0,2},{1,3},{2,0},{3,1},{4,6},{5,7},{6,4},{7,5},{8,10},{9,11},{10,... | collective-permute-start | bytes 24584 | tf_op jit(solution)/shard_map/ppermute | solution.py:373
  89.1 7.6 %collective-permute-start.2 = (f32[16,128]{1,0:T(8,128)S(1)}, f32[16,128]{1,0:T(8,128)S(1)}, u32[]{:S(2)}, u32[]{:S(2)}) collective-permute-start(f32[16,128]{1,0:T(8,128)S(1)} %add.33), channel_id=1, source_target_pairs={{0,4},{1,5},{2,6},{3,7},{4,0},{5,1},{6,2},{7,3},{8,12},{9,13},{10,... | collective-permute-start | bytes 24584 | tf_op jit(solution)/shard_map/ppermute | solution.py:373
  96.7 1.3 collective-permute-start.3
  98.0 4.4 %collective-permute-start.4 = (f32[40,128]{1,0:T(8,128)S(1)}, f32[40,128]{1,0:T(8,128)S(1)}, u32[]{:S(2)}, u32[]{:S(2)}) collective-permute-start(f32[40,128]{1,0:T(8,128)S(1)} %fusion.1), channel_id=1, source_target_pairs={{0,16},{16,0},{32,48},{48,32},{1,17},{17,1},{33,49},{49,33},{2,18}... | collective-permute-start | bytes 61448 | tf_op jit(solution)/shard_map/ppermute | solution.py:373
  102.4 5.4 %collective-permute-start.5 = (f32[40,128]{1,0:T(8,128)S(1)}, f32[40,128]{1,0:T(8,128)S(1)}, u32[]{:S(2)}, u32[]{:S(2)}) collective-permute-start(f32[40,128]{1,0:T(8,128)S(1)} %add.36), channel_id=1, source_target_pairs={{0,32},{16,48},{32,0},{48,16},{1,33},{17,49},{33,1},{49,17},{2,34}... | collective-permute-start | bytes 61448 | tf_op jit(solution)/shard_map/ppermute | solution.py:373
  107.8 3.8 %collective-permute-start.6 = (f32[40,128]{1,0:T(8,128)S(1)}, f32[40,128]{1,0:T(8,128)S(1)}, u32[]{:S(2)}, u32[]{:S(2)}) collective-permute-start(f32[40,128]{1,0:T(8,128)S(1)} %add.37), channel_id=1, source_target_pairs={{0,64},{64,0},{128,192},{192,128},{1,65},{65,1},{129,193},{193,129... | collective-permute-start | bytes 61448 | tf_op jit(solution)/shard_map/ppermute | solution.py:373
  108.4 10.3 %copy-start.2 = (s32[512]{0:T(512)S(1)}, s32[512]{0:T(512)}, u32[]{:S(2)}) copy-start(s32[512]{0:T(512)} %get-tuple-element.42.order) | copy-start | bytes 6148
  108.4 10.3 %copy-start.3 = (s32[512]{0:T(512)S(1)}, s32[512]{0:T(512)}, u32[]{:S(2)}) copy-start(s32[512]{0:T(512)} %get-tuple-element.43.spots) | copy-start | bytes 6148
  108.5 10.3 %copy-start.4 = (s32[5]{0:T(128)S(1)}, s32[5]{0:T(128)}, u32[]{:S(2)}) copy-start(s32[5]{0:T(128)} %get-tuple-element.44.offsets) | copy-start | bytes 64
  113.5 5.3 %collective-permute-start.7 = (f32[40,128]{1,0:T(8,128)S(1)}, f32[40,128]{1,0:T(8,128)S(1)}, u32[]{:S(2)}, u32[]{:S(2)}) collective-permute-start(f32[40,128]{1,0:T(8,128)S(1)} %add.38), channel_id=1, source_target_pairs={{0,128},{64,192},{128,0},{192,64},{1,129},{65,193},{129,1},{193,65... | collective-permute-start | bytes 61448 | tf_op jit(solution)/shard_map/ppermute | solution.py:373
  135.2 10.1 %collective-permute-start.8 = (f32[16,304,128]{2,1,0:T(8,128)S(1)}, f32[16,304,128]{2,1,0:T(8,128)S(1)}, u32[]{:S(2)}, u32[]{:S(2)}) collective-permute-start(f32[16,304,128]{2,1,0:T(8,128)S(1)} %get-tuple-element.71), channel_id=1, source_target_pairs={{0,8},{8,0},{1,9},{9,1},{2,10},{10,2},{3,11},{11,3},{4,12},{12,4},... | collective-permute-start | bytes 7471112 | tf_op jit(solution)/shard_map/ppermute | solution.py:430
  156.3 42.6 %all-to-all-start.1 = ((f32[16,304,128]{2,1,0:T(8,128)}), f32[16,304,128]{2,1,0:T(8,128)S(1)}, u32[]{:S(2)}, u32[]{:S(2)}) async-start(f32[16,304,128]{2,1,0:T(8,128)} %get-tuple-element.73), calls=%async_computation.2 | async-start | bytes 4980736 | tf_op jit(solution)/shard_map/all_to_all | solution.py:436
  163.7 35.3 %copy-start.5 = (f32[300,128]{1,0:T(8,128)S(1)}, f32[300,128]{1,0:T(8,128)}, u32[]{:S(2)}) copy-start(f32[300,128]{1,0:T(8,128)} %param.11) | copy-start | bytes 460804
  163.7 35.4 %copy-start.7 = (f32[300,128]{1,0:T(8,128)S(1)}, f32[300,128]{1,0:T(8,128)}, u32[]{:S(2)}) copy-start(f32[300,128]{1,0:T(8,128)} %param.13) | copy-start | bytes 460804
  163.8 41.2 %reduce-scatter.2.cloned.1.call-start = ((), (), s32[]{:S(2)}) async-start(), calls=%async_computation.3 | async-start | bytes 1400832 | tf_op jit(solution)/shard_map/reduce_scatter | solution.py:435
  163.8 41.2 %copy-start.6 = (f32[300,128]{1,0:T(8,128)S(1)}, f32[300,128]{1,0:T(8,128)}, u32[]{:S(2)}) copy-start(f32[300,128]{1,0:T(8,128)} %param.10) | copy-start | bytes 460804
  163.8 41.2 %copy-start.8 = (f32[300,128]{1,0:T(8,128)S(1)}, f32[300,128]{1,0:T(8,128)}, u32[]{:S(2)}) copy-start(f32[300,128]{1,0:T(8,128)} %param.12) | copy-start | bytes 460804
  (1 other events, 1.3 us)
Sparse Core Ops, SparseCore 0:
  10.5 62.7 all-gather.6
  75.1 38.2 all-gather.8
  167.1 37.8 reduce-scatter.1

commit v7 on v6

--- a/solution.py
+++ b/solution.py
@@ -432,17 +432,17 @@
     half, row_term = part_grads(
         *inputs, near_stack, counts, masses, row_term, early, chunks - early, (piece, swapped)
     )
+    loss_scale = 4.0 * float(words * n_z * n_row_axis) ** (-0.5)
     row_grad = lax.psum_scatter(row_term, "col", scatter_dimension=0, tiled=False)
-    col_grad = jnp.sum(lax.all_to_all(half, ("x", "y"), split_axis=0, concat_axis=0, tiled=True), axis=0)
-    loss_scale = 4.0 * float(words * n_z * n_row_axis) ** (-0.5)
+    arrived_cols = lax.all_to_all(half, ("x", "y"), split_axis=0, concat_axis=0, tiled=True)
     row_share = row_grad[:dim] * loss_scale
-    col_share = col_grad[:dim] * loss_scale
     new_row_acc = row_acc + row_share * row_share
+    new_row_emb = row_emb - LEARNING_RATE * row_share / jnp.sqrt(new_row_acc)
+    arrived_cols, new_row_acc, new_row_emb = lax.optimization_barrier((arrived_cols, new_row_acc, new_row_emb))
+    col_share = jnp.sum(arrived_cols, axis=0)[:dim] * loss_scale
     new_col_acc = col_acc + col_share * col_share
-    new_row_emb = row_emb - LEARNING_RATE * row_share / jnp.sqrt(new_row_acc)
     new_col_emb = col_emb - LEARNING_RATE * col_share / jnp.sqrt(new_col_acc)
     return (new_row_emb, new_col_emb, new_row_acc, new_col_acc)
-
 
 def solution(mesh):
     n_z = mesh.devices.shape[1]

time: 214 us -> 207 us (0.967)
  waiting for transfers between devices: 98.2 us -> 91.3 us
    all_to_all x1, waiting for transfers between devices: 34.5 us -> 2.84 us  [per_device(): lax.all_to_all(half, ('x', 'y'), split_axis=0, concat_axis=0, tiled=True)]
    reduce_scatter x1, waiting for transfers between devices: 5.13 us -> 30.7 us  [per_device(): lax.psum_scatter(row_term, 'col', scatter_dimension=0, tiled=False)]
where the time goes in v7:
time: 207 us
  waiting for transfers between devices  91.3 us (44%)
  Pallas kernels  61 us (29%)
  starting transfers between devices  35 us (17%)
  between operations  14 us (7%)
  other arithmetic  3.29 us (2%)
    all_gather x1, waiting for transfers between devices, per_device(): col_blocks = lax.all_gather(col_emb, ROW, axis=0)  41.5 us
    pallas_call x3, Pallas kernels, part_grads(): pl.pallas_call(functools.partial(part_kernel, near=near, first=first, mer...  37.4 us
    reduce_scatter x1, waiting for transfers between devices, per_device(): lax.psum_scatter(row_term, 'col', scatter_dimension=0, tiled=False)  30.7 us
    all_to_all x1, starting transfers between devices, per_device(): lax.all_to_all(blocks.reshape(-1, slots_each, sub_rows, sub_cols), ALL, s...  14.5 us
    ppermute x8, starting transfers between devices, swap_sum(): lax.ppermute(value, axis, [(i, i ^ bit) for i in range(size)])  12.8 us
    ppermute x8, waiting for transfers between devices, swap_sum(): lax.ppermute(value, axis, [(i, i ^ bit) for i in range(size)])  12.1 us
    pallas_call x4, Pallas kernels, stack_cols(): pl.pallas_call(stack_kernel, name='stack_near' if near else 'stack_far',...  9.19 us
    pallas_call x1, Pallas kernels, sort_slots(): pl.pallas_call(functools.partial(sort_kernel, columns=columns), name='sor...  7.99 us
  transfers between devices with their start and end apart: 14, of which 12 were waited for; matrix products, arithmetic and copies ran while one was open for 1% of the time, Pallas kernels for 16%

profile of v7, /device:TPU:16, one launch (start us, length us, event | category | flops | bytes accessed | tf_op | source)
XLA Modules:
  0.0 206.6 jit_solution(1367213344664739590)
XLA Ops:
  7.9 14.5 %all-to-all-start = ((f32[256,2,8,128]{3,2,1,0:T(8,128)}), f32[256,2,8,128]{3,2,1,0:T(8,128)S(1)}, u32[]{:S(2)}, u32[]{:S(2)}) async-start(f32[256,2,8,128]{3,2,1,0:T(8,128)} %bitcast.26), calls=%async_computation | async-start | bytes 4194304 | tf_op jit(solution)/shard_map/all_to_all | solution.py:396
  23.9 8.0 %sort_slots.1 = (s32[512]{0:T(512)}, s32[512]{0:T(512)}, s32[5]{0:T(128)}) custom-call(s32[512]{0:T(512)} %select_n.5.target, s32[1]{0:T(128)} %bitcast.4.core), custom_call_target="tpu_custom_call" | custom-call | tf_op jit(solution)/shard_map/sort_slots/pallas_call | solution.py:141
  31.9 41.5 %all-gather.7.cloned.1.call-done = f32[32,300,128]{2,1,0:T(8,128)} async-done(((f32[1,300,128]{2,1,0:T(8,128)}), f32[32,300,128]{2,1,0:T(8,128)}) %all-gather.7.cloned.1.call-update) | async-done | bytes 4915216 | tf_op jit(solution)/shard_map/all_gather | solution.py:389
  73.4 1.6 all-to-all-done
  75.0 5.7 %place_counts.1 = (f32[512,8,128]{2,1,0:T(8,128)S(1)}, f32[48,128]{1,0:T(8,128)S(1)}) custom-call(s32[512]{0:T(512)} %select_n.5.target, s32[512]{0:T(512)S(1)} %convert_element_type.4.alive, f32[512,8,128]{2,1,0:T(8,128)S(1)} %bitcast.21), custom_call_target="tpu_custom_call" | custom-call | tf_op jit(solution)/shard_map/place_counts/pallas_call | solution.py:76
  82.0 2.4 %collective-permute-done = f32[16,128]{1,0:T(8,128)S(1)} collective-permute-done((f32[16,128]{1,0:T(8,128)S(1)}, f32[16,128]{1,0:T(8,128)S(1)}, u32[]{:S(2)}, u32[]{:S(2)}) %collective-permute-start) | collective-permute-done | bytes 8224 | tf_op jit(solution)/shard_map/ppermute | solution.py:373
  85.3 3.8 %collective-permute-done.1 = f32[16,128]{1,0:T(8,128)S(1)} collective-permute-done((f32[16,128]{1,0:T(8,128)S(1)}, f32[16,128]{1,0:T(8,128)S(1)}, u32[]{:S(2)}, u32[]{:S(2)}) %collective-permute-start.1) | collective-permute-done | bytes 8224 | tf_op jit(solution)/shard_map/ppermute | solution.py:373
  89.1 3.4 %collective-permute-start.2 = (f32[16,128]{1,0:T(8,128)S(1)}, f32[16,128]{1,0:T(8,128)S(1)}, u32[]{:S(2)}, u32[]{:S(2)}) collective-permute-start(f32[16,128]{1,0:T(8,128)S(1)} %add.33), channel_id=1, source_target_pairs={{0,4},{1,5},{2,6},{3,7},{4,0},{5,1},{6,2},{7,3},{8,12},{9,13},{10,... | collective-permute-start | bytes 24584 | tf_op jit(solution)/shard_map/ppermute | solution.py:373
  92.6 2.3 %stack_far.2.rest_0_ = bf16[608,2048]{1,0:T(8,128)(2,1)} custom-call(s32[1]{0:T(128)} %bitcast.4.core, f32[16,2,300,128]{3,2,1,0:T(8,128)} %bitcast.22), custom_call_target="tpu_custom_call" | custom-call | tf_op jit(solution)/shard_map/stack_far/pallas_call | solution.py:207
  94.9 1.8 collective-permute-done.2
  98.0 2.1 %collective-permute-start.4 = (f32[40,128]{1,0:T(8,128)S(1)}, f32[40,128]{1,0:T(8,128)S(1)}, u32[]{:S(2)}, u32[]{:S(2)}) collective-permute-start(f32[40,128]{1,0:T(8,128)S(1)} %fusion.1), channel_id=1, source_target_pairs={{0,16},{16,0},{32,48},{48,32},{1,17},{17,1},{33,49},{49,33},{2,18}... | collective-permute-start | bytes 61448 | tf_op jit(solution)/shard_map/ppermute | solution.py:373
  100.1 2.3 %stack_far.3 = bf16[608,2048]{1,0:T(8,128)(2,1)} custom-call(s32[1]{0:T(128)} %bitcast.4.core, f32[16,2,300,128]{3,2,1,0:T(8,128)} %bitcast.23, bf16[608,2048]{1,0:T(8,128)(2,1)} %stack_far.2.rest_0_), custom_call_target="tpu_custom_call", output_to_operand_aliasing={{}: (2, {})} | custom-call | tf_op jit(solution)/shard_map/stack_far/pallas_call | solution.py:207
  103.5 2.3 %stack_near.2.rest_0_ = bf16[608,2048]{1,0:T(8,128)(2,1)} custom-call(s32[1]{0:T(128)} %bitcast.4.core, f32[16,2,300,128]{3,2,1,0:T(8,128)} %bitcast.24), custom_call_target="tpu_custom_call" | custom-call | tf_op jit(solution)/shard_map/stack_near/pallas_call | solution.py:207
  105.8 2.0 collective-permute-done.5
  108.5 2.3 %stack_near.3.stack_far = bf16[608,2048]{1,0:T(8,128)(2,1)} custom-call(s32[1]{0:T(128)} %bitcast.4.core, f32[16,2,300,128]{3,2,1,0:T(8,128)} %bitcast.25, bf16[608,2048]{1,0:T(8,128)(2,1)} %stack_near.2.rest_0_), custom_call_target="tpu_custom_call", output_to_operand_aliasing={{}: (2, {})} | custom-call | tf_op jit(solution)/shard_map/stack_near/pallas_call | solution.py:207
  111.6 1.9 all-gather.9.cloned.1.call-done.row_blocks
  113.5 3.2 %collective-permute-start.7 = (f32[40,128]{1,0:T(8,128)S(1)}, f32[40,128]{1,0:T(8,128)S(1)}, u32[]{:S(2)}, u32[]{:S(2)}) collective-permute-start(f32[40,128]{1,0:T(8,128)S(1)} %add.38), channel_id=1, source_target_pairs={{0,128},{64,192},{128,0},{192,64},{1,129},{65,193},{129,1},{193,65... | collective-permute-start | bytes 61448 | tf_op jit(solution)/shard_map/ppermute | solution.py:373
  118.8 16.4 %far_grads.1 = (f32[16,304,128]{2,1,0:T(8,128)S(1)}, f32[8,304,128]{2,1,0:T(8,128)S(1)}) custom-call(s32[512]{0:T(512)S(1)} %copy-done.2, s32[512]{0:T(512)S(1)} %copy-done.3, s32[5]{0:T(128)S(1)} %copy-done.4, s32[1]{0:T(128)} %bitcast.4.core, bf16[1024,1024]{1,0:T(8,128)(2,1)S(1)} %get-tuple-element.65.row_turned, ...), custom_call_target="tpu_custom_call" | custom-call | tf_op jit(solution)/shard_map/far_grads/pallas_call | solution.py:337
  135.3 10.0 %near_grads.1 = (f32[8,304,128]{2,1,0:T(8,128)S(1)}, f32[8,304,128]{2,1,0:T(8,128)S(1)}) custom-call(s32[512]{0:T(512)S(1)} %copy-done.2, s32[512]{0:T(512)S(1)} %copy-done.3, s32[5]{0:T(128)S(1)} %copy-done.4, s32[1]{0:T(128)} %bitcast.4.core, bf16[1024,1024]{1,0:T(8,128)(2,1)S(1)} %get-tuple-element.65.row_turned, ...), custom_call_target="tpu_custom_call" | custom-call | tf_op jit(solution)/shard_map/near_grads/pallas_call | solution.py:337
  145.4 11.0 %merge_grads.1 = (f32[16,304,128]{2,1,0:T(8,128)}, f32[8,304,128]{2,1,0:T(8,128)}) custom-call(s32[512]{0:T(512)S(1)} %copy-done.2, s32[512]{0:T(512)S(1)} %copy-done.3, s32[5]{0:T(128)S(1)} %copy-done.4, s32[1]{0:T(128)} %bitcast.4.core, bf16[1024,1024]{1,0:T(8,128)(2,1)S(1)} %get-tuple-element.65.row_turned, ...), custom_call_target="tpu_custom_call" | custom-call | tf_op jit(solution)/shard_map/merge_grads/pallas_call | solution.py:337
  156.4 7.5 %all-to-all-start.1 = ((f32[16,304,128]{2,1,0:T(8,128)}), f32[16,304,128]{2,1,0:T(8,128)S(1)}, u32[]{:S(2)}, u32[]{:S(2)}) async-start(f32[16,304,128]{2,1,0:T(8,128)} %get-tuple-element.75), calls=%async_computation.1 | async-start | bytes 4980736 | tf_op jit(solution)/shard_map/all_to_all | solution.py:437
  164.0 30.7 %reduce-scatter.2.cloned.1.call-done = f32[1,304,128]{2,1,0:T(8,128)} async-done(((f32[8,304,128]{2,1,0:T(8,128)}), f32[1,304,128]{2,1,0:T(8,128)}) %reduce-scatter.2.cloned.1.call-update) | async-done | bytes 155664 | tf_op jit(solution)/shard_map/reduce_scatter | solution.py:436
  194.7 1.7 fusion
  196.3 2.8 %all-to-all-done.1 = f32[16,304,128]{2,1,0:T(8,128)S(1)} async-done(((f32[16,304,128]{2,1,0:T(8,128)}), f32[16,304,128]{2,1,0:T(8,128)S(1)}, u32[]{:S(2)}, u32[]{:S(2)}) %all-to-all-start.1) | async-done | bytes 2490400 | tf_op jit(solution)/shard_map/all_to_all | solution.py:437
  (66 shorter events, 11.4 us)
Async XLA Ops:
  7.2 66.2 %all-gather.7.cloned.1.call-start = ((), (), s32[]{:S(2)}) async-start(), calls=%async_computation.4 | async-start | bytes 5136384 | tf_op jit(solution)/shard_map/all_gather | solution.py:389
  7.9 14.6 %copy-start.9 = (s32[1,1,8,32,2]{3,4,2,1,0:T(2,128)S(1)}, s32[1,1,8,32,2]{3,4,2,1,0:T(2,128)}, u32[]{:S(2)}) copy-start(s32[1,1,8,32,2]{3,4,2,1,0:T(2,128)} %param.8) | copy-start | bytes 6148
  7.9 14.7 %copy-start.10 = (s32[1,1,8,32]{3,2,1,0:T(8,128)S(1)}, s32[1,1,8,32]{3,2,1,0:T(8,128)}, u32[]{:S(2)}) copy-start(s32[1,1,8,32]{3,2,1,0:T(8,128)} %param.9) | copy-start | bytes 3076
  7.9 67.1 %all-to-all-start = ((f32[256,2,8,128]{3,2,1,0:T(8,128)}), f32[256,2,8,128]{3,2,1,0:T(8,128)S(1)}, u32[]{:S(2)}, u32[]{:S(2)}) async-start(f32[256,2,8,128]{3,2,1,0:T(8,128)} %bitcast.26), calls=%async_computation | async-start | bytes 4194304 | tf_op jit(solution)/shard_map/all_to_all | solution.py:396
  22.4 91.0 %all-gather.9.cloned.1.call-start = ((), (), s32[]{:S(2)}) async-start(), calls=%async_computation.5 | async-start | bytes 1400832 | tf_op jit(solution)/shard_map/all_gather | solution.py:393
  73.4 121.3 %reduce-scatter.2.cloned.1.call-start = ((), (), s32[]{:S(2)}) async-start(), calls=%async_computation.3 | async-start | bytes 1400832 | tf_op jit(solution)/shard_map/reduce_scatter | solution.py:436
  80.7 14.2 %copy-start = (f32[512,8,128]{2,1,0:T(8,128)}, f32[512,8,128]{2,1,0:T(8,128)S(1)}, u32[]{:S(2)}) copy-start(f32[512,8,128]{2,1,0:T(8,128)S(1)} %get-tuple-element.68.counts_far) | copy-start | bytes 6291460
  80.7 3.7 %collective-permute-start = (f32[16,128]{1,0:T(8,128)S(1)}, f32[16,128]{1,0:T(8,128)S(1)}, u32[]{:S(2)}, u32[]{:S(2)}) collective-permute-start(f32[16,128]{1,0:T(8,128)S(1)} %slice.30), channel_id=1, source_target_pairs={{0,1},{1,0},{2,3},{3,2},{4,5},{5,4},{6,7},{7,6},{8,9},{9,8},{10,11... | collective-permute-start | bytes 24584 | tf_op jit(solution)/shard_map/ppermute | solution.py:373
  84.4 4.7 %collective-permute-start.1 = (f32[16,128]{1,0:T(8,128)S(1)}, f32[16,128]{1,0:T(8,128)S(1)}, u32[]{:S(2)}, u32[]{:S(2)}) collective-permute-start(f32[16,128]{1,0:T(8,128)S(1)} %slice_add_fusion), channel_id=1, source_target_pairs={{0,2},{1,3},{2,0},{3,1},{4,6},{5,7},{6,4},{7,5},{8,10},{9,11},{10,... | collective-permute-start | bytes 24584 | tf_op jit(solution)/shard_map/ppermute | solution.py:373
  89.1 7.6 %collective-permute-start.2 = (f32[16,128]{1,0:T(8,128)S(1)}, f32[16,128]{1,0:T(8,128)S(1)}, u32[]{:S(2)}, u32[]{:S(2)}) collective-permute-start(f32[16,128]{1,0:T(8,128)S(1)} %add.33), channel_id=1, source_target_pairs={{0,4},{1,5},{2,6},{3,7},{4,0},{5,1},{6,2},{7,3},{8,12},{9,13},{10,... | collective-permute-start | bytes 24584 | tf_op jit(solution)/shard_map/ppermute | solution.py:373
  96.7 1.3 collective-permute-start.3
  98.0 4.4 %collective-permute-start.4 = (f32[40,128]{1,0:T(8,128)S(1)}, f32[40,128]{1,0:T(8,128)S(1)}, u32[]{:S(2)}, u32[]{:S(2)}) collective-permute-start(f32[40,128]{1,0:T(8,128)S(1)} %fusion.1), channel_id=1, source_target_pairs={{0,16},{16,0},{32,48},{48,32},{1,17},{17,1},{33,49},{49,33},{2,18}... | collective-permute-start | bytes 61448 | tf_op jit(solution)/shard_map/ppermute | solution.py:373
  102.4 5.4 %collective-permute-start.5 = (f32[40,128]{1,0:T(8,128)S(1)}, f32[40,128]{1,0:T(8,128)S(1)}, u32[]{:S(2)}, u32[]{:S(2)}) collective-permute-start(f32[40,128]{1,0:T(8,128)S(1)} %add.36), channel_id=1, source_target_pairs={{0,32},{16,48},{32,0},{48,16},{1,33},{17,49},{33,1},{49,17},{2,34}... | collective-permute-start | bytes 61448 | tf_op jit(solution)/shard_map/ppermute | solution.py:373
  107.8 3.8 %collective-permute-start.6 = (f32[40,128]{1,0:T(8,128)S(1)}, f32[40,128]{1,0:T(8,128)S(1)}, u32[]{:S(2)}, u32[]{:S(2)}) collective-permute-start(f32[40,128]{1,0:T(8,128)S(1)} %add.37), channel_id=1, source_target_pairs={{0,64},{64,0},{128,192},{192,128},{1,65},{65,1},{129,193},{193,129... | collective-permute-start | bytes 61448 | tf_op jit(solution)/shard_map/ppermute | solution.py:373
  108.4 10.3 %copy-start.2 = (s32[512]{0:T(512)S(1)}, s32[512]{0:T(512)}, u32[]{:S(2)}) copy-start(s32[512]{0:T(512)} %get-tuple-element.45.order) | copy-start | bytes 6148
  108.5 10.3 %copy-start.3 = (s32[512]{0:T(512)S(1)}, s32[512]{0:T(512)}, u32[]{:S(2)}) copy-start(s32[512]{0:T(512)} %get-tuple-element.46.spots) | copy-start | bytes 6148
  108.5 10.3 %copy-start.4 = (s32[5]{0:T(128)S(1)}, s32[5]{0:T(128)}, u32[]{:S(2)}) copy-start(s32[5]{0:T(128)} %get-tuple-element.47.offsets) | copy-start | bytes 64
  113.5 5.3 %collective-permute-start.7 = (f32[40,128]{1,0:T(8,128)S(1)}, f32[40,128]{1,0:T(8,128)S(1)}, u32[]{:S(2)}, u32[]{:S(2)}) collective-permute-start(f32[40,128]{1,0:T(8,128)S(1)} %add.38), channel_id=1, source_target_pairs={{0,128},{64,192},{128,0},{192,64},{1,129},{65,193},{129,1},{193,65... | collective-permute-start | bytes 61448 | tf_op jit(solution)/shard_map/ppermute | solution.py:373
  135.2 10.1 %collective-permute-start.8 = (f32[16,304,128]{2,1,0:T(8,128)S(1)}, f32[16,304,128]{2,1,0:T(8,128)S(1)}, u32[]{:S(2)}, u32[]{:S(2)}) collective-permute-start(f32[16,304,128]{2,1,0:T(8,128)S(1)} %get-tuple-element.74), channel_id=1, source_target_pairs={{0,8},{8,0},{1,9},{9,1},{2,10},{10,2},{3,11},{11,3},{4,12},{12,4},... | collective-permute-start | bytes 7471112 | tf_op jit(solution)/shard_map/ppermute | solution.py:430
  156.4 38.3 %copy-start.5 = (f32[300,128]{1,0:T(8,128)S(1)}, f32[300,128]{1,0:T(8,128)}, u32[]{:S(2)}) copy-start(f32[300,128]{1,0:T(8,128)} %param.10) | copy-start | bytes 460804
  156.4 38.3 %copy-start.7 = (f32[300,128]{1,0:T(8,128)S(1)}, f32[300,128]{1,0:T(8,128)}, u32[]{:S(2)}) copy-start(f32[300,128]{1,0:T(8,128)} %param.12) | copy-start | bytes 460804
  156.4 42.8 %all-to-all-start.1 = ((f32[16,304,128]{2,1,0:T(8,128)}), f32[16,304,128]{2,1,0:T(8,128)S(1)}, u32[]{:S(2)}, u32[]{:S(2)}) async-start(f32[16,304,128]{2,1,0:T(8,128)} %get-tuple-element.75), calls=%async_computation.1 | async-start | bytes 4980736 | tf_op jit(solution)/shard_map/all_to_all | solution.py:437
  163.9 35.4 %copy-start.6 = (f32[300,128]{1,0:T(8,128)S(1)}, f32[300,128]{1,0:T(8,128)}, u32[]{:S(2)}) copy-start(f32[300,128]{1,0:T(8,128)} %param.11) | copy-start | bytes 460804
  164.0 35.4 %copy-start.8 = (f32[300,128]{1,0:T(8,128)S(1)}, f32[300,128]{1,0:T(8,128)}, u32[]{:S(2)}) copy-start(f32[300,128]{1,0:T(8,128)} %param.13) | copy-start | bytes 460804
  (1 other events, 1.3 us)
Sparse Core Ops, SparseCore 0:
  10.5 62.7 all-gather.6
  75.1 38.2 all-gather.8
  156.5 38.0 reduce-scatter.1

commit v8 on v7

--- a/solution.py
+++ b/solution.py
@@ -245,10 +245,11 @@
 
     @pl.when(step == 0)
     def _():
-        bring(0).start()
-        fetch.start()
-        for chunk in range(1, stacks.shape[0]):
-            bring(chunk).start()
+        if not near:
+            bring(0).start()
+            fetch.start()
+            for chunk in range(1, stacks.shape[0]):
+                bring(chunk).start()
         log_total = jnp.log(masses[n_col + n_row : n_col + n_row + 1, :])
         col_bias[...] = 0.5 * (jnp.log(masses[0:n_col, :]) - log_total)
         row_logs = 0.5 * jnp.log(masses[n_col : n_col + n_row, :])
@@ -257,7 +258,10 @@
             row_bias[i * LANES // 8 : (i + 1) * LANES // 8] = turned.reshape(-1, 8, LANES)
         row_term[...] = rest[0][...] if near else jnp.zeros(row_term.shape, F32)
 
-    bring(step).wait()
+    if near:
+        stacks[step, 0 : 2 * padded, :] = stack_far[:, first * width : (first + 1) * width]
+    else:
+        bring(step).wait()
     stacks[step, 2 * padded : 3 * padded, :] = stacks[step, 0:padded, :]
     stacks[step, 3 * padded :, :] = jnp.zeros((stacks.shape[1] - 3 * padded, width), BF16)
     product = jnp.dot(row_turned[...], stacks[step], preferred_element_type=F32)
@@ -270,9 +274,11 @@
     begin = offsets[here]
     end = offsets[here + 1]
 
-    @pl.when(step == 0)
-    def _():
-        fetch.wait()
+    if not near:
+
+        @pl.when(step == 0)
+        def _():
+            fetch.wait()
 
     def counted(group, carry):
         found = []
@@ -280,7 +286,7 @@
             at = jnp.minimum(begin + group * 8 + u, end - 1)
             spot = spots[at]
             row, k = lax.shift_right_logical(spot, BLOCKS.bit_length() - 1), spot & (BLOCKS - 1)
-            count = counts[order[at]]
+            count = (counts_far if near else counts)[order[at]]
             fresh = (0.1 + 0.25 * jnp.sqrt(count)) * (2.0 * scores[row, k] - jnp.log(count))
             found.append((row, k, fresh))
         for row, k, fresh in found:
@@ -329,6 +335,7 @@
     near = earlier is not None
     merge = bool(extra)
     ready = [earlier] if near else []
+    placed = (col_stack, counts) if near else [pltpu.with_memory_space_constraint(value, pltpu.HBM) for value in (col_stack, counts)]
     out_blocks = blocks if merge else count * BLOCKS
     scratch = [
         pltpu.VMEM((blocks, padded, LANES), F32),
@@ -341,7 +348,7 @@
             num_scalar_prefetch=4,
             grid=(count,),
             in_specs=whole(2)
-            + [pl.BlockSpec(memory_space=pltpu.HBM)] * 2
+            + [pl.BlockSpec(memory_space=pltpu.VMEM if near else pltpu.HBM)] * 2
             + whole(1 + len(ready) + len(extra)),
             out_specs=[
                 pl.BlockSpec(memory_space=pltpu.HBM)
@@ -354,7 +361,7 @@
                 pltpu.VMEM((words // 8, BLOCKS, 8, LANES), F32),
                 pltpu.VMEM((words // 8, 8, LANES), F32),
                 pltpu.VMEM((blocks * CORES, LANES), F32),
-                pltpu.VMEM(counts.shape, F32),
+                pltpu.VMEM((8, 8, LANES) if near else counts.shape, F32),
                 pltpu.VMEM((count, deep, BLOCKS * LANES), BF16),
                 pltpu.SemaphoreType.DMA(()),
                 pltpu.SemaphoreType.DMA((count,)),
@@ -365,8 +372,8 @@
             (pltpu.HBM if merge else jax.ShapeDtypeStruct)((out_blocks, padded, LANES), F32),
             (pltpu.HBM if merge else jax.ShapeDtypeStruct)((words // LANES, padded, LANES), F32),
         ],
-        compiler_params=pltpu.CompilerParams(vmem_limit_bytes=40 << 20),
-    )(*scalars, row_turned, row_stack, pltpu.with_memory_space_constraint(col_stack, pltpu.HBM), pltpu.with_memory_space_constraint(counts, pltpu.HBM), masses, *ready, *extra)
+        compiler_params=pltpu.CompilerParams(vmem_limit_bytes=36 << 20),
+    )(*scalars, row_turned, row_stack, *placed, masses, *ready, *extra)
 
 
 def swap_sum(value, axis, size, bit):

time: 207 us -> 204 us (0.986)
  Pallas kernels: 61 us -> 57.7 us
    pallas_call x3, Pallas kernels: 37.4 us -> 34.1 us  [part_grads(): pl.pallas_call(functools.partial(part_kernel, near=near, first=first, mer...]
  transfers between devices with their start and end apart: 14 -> 14, of which waited for: 12 -> 12; matrix products, arithmetic and copies ran while one was open for 1% -> 2% of each run, Pallas kernels for 16% -> 16%
where the time goes in v8:
time: 204 us; the launch traced here: 203 us
  waiting for transfers between devices  91.2 us (45%)
  Pallas kernels  57.7 us (28%)
  starting transfers between devices  35 us (17%)
  between operations  14 us (7%)
  other arithmetic  3.29 us (2%)
    all_gather x1, waiting for transfers between devices, per_device(): col_blocks = lax.all_gather(col_emb, ROW, axis=0)  41.5 us
    pallas_call x3, Pallas kernels, part_grads(): pl.pallas_call(functools.partial(part_kernel, near=near, first=first, mer...  34.1 us
    reduce_scatter x1, waiting for transfers between devices, per_device(): lax.psum_scatter(row_term, 'col', scatter_dimension=0, tiled=False)  30.6 us
    all_to_all x1, starting transfers between devices, per_device(): lax.all_to_all(blocks.reshape(-1, slots_each, sub_rows, sub_cols), ALL, s...  14.5 us
    ppermute x8, starting transfers between devices, swap_sum(): lax.ppermute(value, axis, [(i, i ^ bit) for i in range(size)])  12.8 us
    ppermute x8, waiting for transfers between devices, swap_sum(): lax.ppermute(value, axis, [(i, i ^ bit) for i in range(size)])  12 us
    pallas_call x4, Pallas kernels, stack_cols(): pl.pallas_call(stack_kernel, name='stack_near' if near else 'stack_far',...  9.21 us
    pallas_call x1, Pallas kernels, sort_slots(): pl.pallas_call(functools.partial(sort_kernel, columns=columns), name='sor...  7.99 us
  transfers between devices with their start and end apart: 14, of which 12 were waited for; matrix products, arithmetic and copies ran while one was open for 2% of the time, Pallas kernels for 16%

profile of v8, /device:TPU:16, one launch (start us, length us, event | category | flops | bytes accessed | tf_op | source)
XLA Modules:
  0.0 203.4 jit_solution(1377497745668422379)
XLA Ops:
  7.9 14.5 %all-to-all-start = ((f32[256,2,8,128]{3,2,1,0:T(8,128)}), f32[256,2,8,128]{3,2,1,0:T(8,128)S(1)}, u32[]{:S(2)}, u32[]{:S(2)}) async-start(f32[256,2,8,128]{3,2,1,0:T(8,128)} %bitcast.26), calls=%async_computation | async-start | bytes 4194304 | tf_op jit(solution)/shard_map/all_to_all | solution.py:403
  23.9 8.0 %sort_slots.1 = (s32[512]{0:T(512)}, s32[512]{0:T(512)}, s32[5]{0:T(128)}) custom-call(s32[512]{0:T(512)} %select_n.5.target, s32[1]{0:T(128)} %bitcast.4.core), custom_call_target="tpu_custom_call" | custom-call | tf_op jit(solution)/shard_map/sort_slots/pallas_call | solution.py:141
  31.9 41.5 %all-gather.7.cloned.1.call-done = f32[32,300,128]{2,1,0:T(8,128)} async-done(((f32[1,300,128]{2,1,0:T(8,128)}), f32[32,300,128]{2,1,0:T(8,128)}) %all-gather.7.cloned.1.call-update) | async-done | bytes 4915216 | tf_op jit(solution)/shard_map/all_gather | solution.py:396
  73.4 1.6 all-to-all-done
  75.0 5.7 %place_counts.1 = (f32[512,8,128]{2,1,0:T(8,128)S(1)}, f32[48,128]{1,0:T(8,128)S(1)}) custom-call(s32[512]{0:T(512)} %select_n.5.target, s32[512]{0:T(512)S(1)} %convert_element_type.4.alive, f32[512,8,128]{2,1,0:T(8,128)S(1)} %bitcast.21), custom_call_target="tpu_custom_call" | custom-call | tf_op jit(solution)/shard_map/place_counts/pallas_call | solution.py:76
  82.0 2.4 %collective-permute-done = f32[16,128]{1,0:T(8,128)S(1)} collective-permute-done((f32[16,128]{1,0:T(8,128)S(1)}, f32[16,128]{1,0:T(8,128)S(1)}, u32[]{:S(2)}, u32[]{:S(2)}) %collective-permute-start) | collective-permute-done | bytes 8224 | tf_op jit(solution)/shard_map/ppermute | solution.py:380
  85.3 3.8 %collective-permute-done.1 = f32[16,128]{1,0:T(8,128)S(1)} collective-permute-done((f32[16,128]{1,0:T(8,128)S(1)}, f32[16,128]{1,0:T(8,128)S(1)}, u32[]{:S(2)}, u32[]{:S(2)}) %collective-permute-start.1) | collective-permute-done | bytes 8224 | tf_op jit(solution)/shard_map/ppermute | solution.py:380
  89.1 3.4 %collective-permute-start.2 = (f32[16,128]{1,0:T(8,128)S(1)}, f32[16,128]{1,0:T(8,128)S(1)}, u32[]{:S(2)}, u32[]{:S(2)}) collective-permute-start(f32[16,128]{1,0:T(8,128)S(1)} %add.33), channel_id=1, source_target_pairs={{0,4},{1,5},{2,6},{3,7},{4,0},{5,1},{6,2},{7,3},{8,12},{9,13},{10,... | collective-permute-start | bytes 24584 | tf_op jit(solution)/shard_map/ppermute | solution.py:380
  92.6 2.3 %stack_far.2.rest_0_ = bf16[608,2048]{1,0:T(8,128)(2,1)} custom-call(s32[1]{0:T(128)} %bitcast.4.core, f32[16,2,300,128]{3,2,1,0:T(8,128)} %bitcast.22), custom_call_target="tpu_custom_call" | custom-call | tf_op jit(solution)/shard_map/stack_far/pallas_call | solution.py:207
  94.9 1.8 collective-permute-done.2
  98.0 2.1 %collective-permute-start.4 = (f32[40,128]{1,0:T(8,128)S(1)}, f32[40,128]{1,0:T(8,128)S(1)}, u32[]{:S(2)}, u32[]{:S(2)}) collective-permute-start(f32[40,128]{1,0:T(8,128)S(1)} %fusion.1), channel_id=1, source_target_pairs={{0,16},{16,0},{32,48},{48,32},{1,17},{17,1},{33,49},{49,33},{2,18}... | collective-permute-start | bytes 61448 | tf_op jit(solution)/shard_map/ppermute | solution.py:380
  100.1 2.3 %stack_far.3 = bf16[608,2048]{1,0:T(8,128)(2,1)} custom-call(s32[1]{0:T(128)} %bitcast.4.core, f32[16,2,300,128]{3,2,1,0:T(8,128)} %bitcast.23, bf16[608,2048]{1,0:T(8,128)(2,1)} %stack_far.2.rest_0_), custom_call_target="tpu_custom_call", output_to_operand_aliasing={{}: (2, {})} | custom-call | tf_op jit(solution)/shard_map/stack_far/pallas_call | solution.py:207
  103.5 2.3 %stack_near.2.rest_0_ = bf16[608,2048]{1,0:T(8,128)(2,1)} custom-call(s32[1]{0:T(128)} %bitcast.4.core, f32[16,2,300,128]{3,2,1,0:T(8,128)} %bitcast.24), custom_call_target="tpu_custom_call" | custom-call | tf_op jit(solution)/shard_map/stack_near/pallas_call | solution.py:207
  105.8 2.0 collective-permute-done.5
  108.5 2.3 %stack_near.3.stack_far = bf16[608,2048]{1,0:T(8,128)(2,1)} custom-call(s32[1]{0:T(128)} %bitcast.4.core, f32[16,2,300,128]{3,2,1,0:T(8,128)} %bitcast.25, bf16[608,2048]{1,0:T(8,128)(2,1)} %stack_near.2.rest_0_), custom_call_target="tpu_custom_call", output_to_operand_aliasing={{}: (2, {})} | custom-call | tf_op jit(solution)/shard_map/stack_near/pallas_call | solution.py:207
  111.6 1.9 all-gather.9.cloned.1.call-done.row_blocks
  113.5 3.2 %collective-permute-start.7 = (f32[40,128]{1,0:T(8,128)S(1)}, f32[40,128]{1,0:T(8,128)S(1)}, u32[]{:S(2)}, u32[]{:S(2)}) collective-permute-start(f32[40,128]{1,0:T(8,128)S(1)} %add.38), channel_id=1, source_target_pairs={{0,128},{64,192},{128,0},{192,64},{1,129},{65,193},{129,1},{193,65... | collective-permute-start | bytes 61448 | tf_op jit(solution)/shard_map/ppermute | solution.py:380
  118.8 16.7 %far_grads.1 = (f32[16,304,128]{2,1,0:T(8,128)S(1)}, f32[8,304,128]{2,1,0:T(8,128)S(1)}) custom-call(s32[512]{0:T(512)S(1)} %copy-done.4, s32[512]{0:T(512)S(1)} %copy-done.5, s32[5]{0:T(128)S(1)} %copy-done.6, s32[1]{0:T(128)} %bitcast.4.core, bf16[1024,1024]{1,0:T(8,128)(2,1)S(1)} %get-tuple-element.65.row_turned, ...), custom_call_target="tpu_custom_call" | custom-call | tf_op jit(solution)/shard_map/far_grads/pallas_call | solution.py:344
  135.7 8.2 %near_grads.1 = (f32[8,304,128]{2,1,0:T(8,128)S(1)}, f32[8,304,128]{2,1,0:T(8,128)S(1)}) custom-call(s32[512]{0:T(512)S(1)} %copy-done.4, s32[512]{0:T(512)S(1)} %copy-done.5, s32[5]{0:T(128)S(1)} %copy-done.6, s32[1]{0:T(128)} %bitcast.4.core, bf16[1024,1024]{1,0:T(8,128)(2,1)S(1)} %get-tuple-element.65.row_turned, ...), custom_call_target="tpu_custom_call" | custom-call | tf_op jit(solution)/shard_map/near_grads/pallas_call | solution.py:344
  143.9 9.2 %merge_grads.1 = (f32[16,304,128]{2,1,0:T(8,128)}, f32[8,304,128]{2,1,0:T(8,128)}) custom-call(s32[512]{0:T(512)S(1)} %copy-done.4, s32[512]{0:T(512)S(1)} %copy-done.5, s32[5]{0:T(128)S(1)} %copy-done.6, s32[1]{0:T(128)} %bitcast.4.core, bf16[1024,1024]{1,0:T(8,128)(2,1)S(1)} %get-tuple-element.65.row_turned, ...), custom_call_target="tpu_custom_call" | custom-call | tf_op jit(solution)/shard_map/merge_grads/pallas_call | solution.py:344
  153.2 7.5 %all-to-all-start.1 = ((f32[16,304,128]{2,1,0:T(8,128)}), f32[16,304,128]{2,1,0:T(8,128)S(1)}, u32[]{:S(2)}, u32[]{:S(2)}) async-start(f32[16,304,128]{2,1,0:T(8,128)} %get-tuple-element.75), calls=%async_computation.1 | async-start | bytes 4980736 | tf_op jit(solution)/shard_map/all_to_all | solution.py:444
  160.7 30.6 %reduce-scatter.2.cloned.1.call-done = f32[1,304,128]{2,1,0:T(8,128)} async-done(((f32[8,304,128]{2,1,0:T(8,128)}), f32[1,304,128]{2,1,0:T(8,128)}) %reduce-scatter.2.cloned.1.call-update) | async-done | bytes 155664 | tf_op jit(solution)/shard_map/reduce_scatter | solution.py:443
  191.3 1.7 fusion
  193.0 3.0 %all-to-all-done.1 = f32[16,304,128]{2,1,0:T(8,128)S(1)} async-done(((f32[16,304,128]{2,1,0:T(8,128)}), f32[16,304,128]{2,1,0:T(8,128)S(1)}, u32[]{:S(2)}, u32[]{:S(2)}) %all-to-all-start.1) | async-done | bytes 2490400 | tf_op jit(solution)/shard_map/all_to_all | solution.py:444
  (70 shorter events, 11.4 us)
Async XLA Ops:
  7.2 66.2 %all-gather.7.cloned.1.call-start = ((), (), s32[]{:S(2)}) async-start(), calls=%async_computation.4 | async-start | bytes 5136384 | tf_op jit(solution)/shard_map/all_gather | solution.py:396
  7.9 14.6 %copy-start.11 = (s32[1,1,8,32,2]{3,4,2,1,0:T(2,128)S(1)}, s32[1,1,8,32,2]{3,4,2,1,0:T(2,128)}, u32[]{:S(2)}) copy-start(s32[1,1,8,32,2]{3,4,2,1,0:T(2,128)} %param.8) | copy-start | bytes 6148
  7.9 14.7 %copy-start.12 = (s32[1,1,8,32]{3,2,1,0:T(8,128)S(1)}, s32[1,1,8,32]{3,2,1,0:T(8,128)}, u32[]{:S(2)}) copy-start(s32[1,1,8,32]{3,2,1,0:T(8,128)} %param.9) | copy-start | bytes 3076
  7.9 67.1 %all-to-all-start = ((f32[256,2,8,128]{3,2,1,0:T(8,128)}), f32[256,2,8,128]{3,2,1,0:T(8,128)S(1)}, u32[]{:S(2)}, u32[]{:S(2)}) async-start(f32[256,2,8,128]{3,2,1,0:T(8,128)} %bitcast.26), calls=%async_computation | async-start | bytes 4194304 | tf_op jit(solution)/shard_map/all_to_all | solution.py:403
  22.4 91.0 %all-gather.9.cloned.1.call-start = ((), (), s32[]{:S(2)}) async-start(), calls=%async_computation.5 | async-start | bytes 1400832 | tf_op jit(solution)/shard_map/all_gather | solution.py:400
  73.4 117.9 %reduce-scatter.2.cloned.1.call-start = ((), (), s32[]{:S(2)}) async-start(), calls=%async_computation.3 | async-start | bytes 1400832 | tf_op jit(solution)/shard_map/reduce_scatter | solution.py:443
  80.7 14.2 %copy-start.1 = (f32[512,8,128]{2,1,0:T(8,128)}, f32[512,8,128]{2,1,0:T(8,128)S(1)}, u32[]{:S(2)}) copy-start(f32[512,8,128]{2,1,0:T(8,128)S(1)} %get-tuple-element.68.counts_far) | copy-start | bytes 6291460
  80.7 3.7 %collective-permute-start = (f32[16,128]{1,0:T(8,128)S(1)}, f32[16,128]{1,0:T(8,128)S(1)}, u32[]{:S(2)}, u32[]{:S(2)}) collective-permute-start(f32[16,128]{1,0:T(8,128)S(1)} %slice.30), channel_id=1, source_target_pairs={{0,1},{1,0},{2,3},{3,2},{4,5},{5,4},{6,7},{7,6},{8,9},{9,8},{10,11... | collective-permute-start | bytes 24584 | tf_op jit(solution)/shard_map/ppermute | solution.py:380
  84.4 4.7 %collective-permute-start.1 = (f32[16,128]{1,0:T(8,128)S(1)}, f32[16,128]{1,0:T(8,128)S(1)}, u32[]{:S(2)}, u32[]{:S(2)}) collective-permute-start(f32[16,128]{1,0:T(8,128)S(1)} %slice_add_fusion), channel_id=1, source_target_pairs={{0,2},{1,3},{2,0},{3,1},{4,6},{5,7},{6,4},{7,5},{8,10},{9,11},{10,... | collective-permute-start | bytes 24584 | tf_op jit(solution)/shard_map/ppermute | solution.py:380
  89.1 7.6 %collective-permute-start.2 = (f32[16,128]{1,0:T(8,128)S(1)}, f32[16,128]{1,0:T(8,128)S(1)}, u32[]{:S(2)}, u32[]{:S(2)}) collective-permute-start(f32[16,128]{1,0:T(8,128)S(1)} %add.33), channel_id=1, source_target_pairs={{0,4},{1,5},{2,6},{3,7},{4,0},{5,1},{6,2},{7,3},{8,12},{9,13},{10,... | collective-permute-start | bytes 24584 | tf_op jit(solution)/shard_map/ppermute | solution.py:380
  96.7 1.3 collective-permute-start.3
  98.0 4.4 %collective-permute-start.4 = (f32[40,128]{1,0:T(8,128)S(1)}, f32[40,128]{1,0:T(8,128)S(1)}, u32[]{:S(2)}, u32[]{:S(2)}) collective-permute-start(f32[40,128]{1,0:T(8,128)S(1)} %fusion.1), channel_id=1, source_target_pairs={{0,16},{16,0},{32,48},{48,32},{1,17},{17,1},{33,49},{49,33},{2,18}... | collective-permute-start | bytes 61448 | tf_op jit(solution)/shard_map/ppermute | solution.py:380
  102.4 5.4 %collective-permute-start.5 = (f32[40,128]{1,0:T(8,128)S(1)}, f32[40,128]{1,0:T(8,128)S(1)}, u32[]{:S(2)}, u32[]{:S(2)}) collective-permute-start(f32[40,128]{1,0:T(8,128)S(1)} %add.36), channel_id=1, source_target_pairs={{0,32},{16,48},{32,0},{48,16},{1,33},{17,49},{33,1},{49,17},{2,34}... | collective-permute-start | bytes 61448 | tf_op jit(solution)/shard_map/ppermute | solution.py:380
  107.8 3.8 %collective-permute-start.6 = (f32[40,128]{1,0:T(8,128)S(1)}, f32[40,128]{1,0:T(8,128)S(1)}, u32[]{:S(2)}, u32[]{:S(2)}) collective-permute-start(f32[40,128]{1,0:T(8,128)S(1)} %add.37), channel_id=1, source_target_pairs={{0,64},{64,0},{128,192},{192,128},{1,65},{65,1},{129,193},{193,129... | collective-permute-start | bytes 61448 | tf_op jit(solution)/shard_map/ppermute | solution.py:380
  108.5 10.3 %copy-start.6 = (s32[5]{0:T(128)S(1)}, s32[5]{0:T(128)}, u32[]{:S(2)}) copy-start(s32[5]{0:T(128)} %get-tuple-element.47.offsets) | copy-start | bytes 64
  113.5 5.3 %collective-permute-start.7 = (f32[40,128]{1,0:T(8,128)S(1)}, f32[40,128]{1,0:T(8,128)S(1)}, u32[]{:S(2)}, u32[]{:S(2)}) collective-permute-start(f32[40,128]{1,0:T(8,128)S(1)} %add.38), channel_id=1, source_target_pairs={{0,128},{64,192},{128,0},{192,64},{1,129},{65,193},{129,1},{193,65... | collective-permute-start | bytes 61448 | tf_op jit(solution)/shard_map/ppermute | solution.py:380
  118.8 16.9 %copy-start = (bf16[608,2048]{1,0:T(8,128)(2,1)S(1)}, bf16[608,2048]{1,0:T(8,128)(2,1)}, u32[]{:S(2)}) copy-start(bf16[608,2048]{1,0:T(8,128)(2,1)} %stack_near.3.stack_far) | copy-start | bytes 7471108
  118.8 16.9 %copy-start.2 = (f32[512,8,128]{2,1,0:T(8,128)S(1)}, f32[512,8,128]{2,1,0:T(8,128)}, u32[]{:S(2)}) copy-start(f32[512,8,128]{2,1,0:T(8,128)} %copy-done.1) | copy-start | bytes 6291460
  135.6 8.3 %collective-permute-start.8 = (f32[16,304,128]{2,1,0:T(8,128)S(1)}, f32[16,304,128]{2,1,0:T(8,128)S(1)}, u32[]{:S(2)}, u32[]{:S(2)}) collective-permute-start(f32[16,304,128]{2,1,0:T(8,128)S(1)} %get-tuple-element.74), channel_id=1, source_target_pairs={{0,8},{8,0},{1,9},{9,1},{2,10},{10,2},{3,11},{11,3},{4,12},{12,4},... | collective-permute-start | bytes 7471112 | tf_op jit(solution)/shard_map/ppermute | solution.py:437
  153.1 38.2 %copy-start.7 = (f32[300,128]{1,0:T(8,128)S(1)}, f32[300,128]{1,0:T(8,128)}, u32[]{:S(2)}) copy-start(f32[300,128]{1,0:T(8,128)} %param.10) | copy-start | bytes 460804
  153.1 38.1 %copy-start.9 = (f32[300,128]{1,0:T(8,128)S(1)}, f32[300,128]{1,0:T(8,128)}, u32[]{:S(2)}) copy-start(f32[300,128]{1,0:T(8,128)} %param.12) | copy-start | bytes 460804
  153.2 42.8 %all-to-all-start.1 = ((f32[16,304,128]{2,1,0:T(8,128)}), f32[16,304,128]{2,1,0:T(8,128)S(1)}, u32[]{:S(2)}, u32[]{:S(2)}) async-start(f32[16,304,128]{2,1,0:T(8,128)} %get-tuple-element.75), calls=%async_computation.1 | async-start | bytes 4980736 | tf_op jit(solution)/shard_map/all_to_all | solution.py:444
  160.7 35.3 %copy-start.8 = (f32[300,128]{1,0:T(8,128)S(1)}, f32[300,128]{1,0:T(8,128)}, u32[]{:S(2)}) copy-start(f32[300,128]{1,0:T(8,128)} %param.11) | copy-start | bytes 460804
  160.7 35.4 %copy-start.10 = (f32[300,128]{1,0:T(8,128)S(1)}, f32[300,128]{1,0:T(8,128)}, u32[]{:S(2)}) copy-start(f32[300,128]{1,0:T(8,128)} %param.13) | copy-start | bytes 460804
  (3 other events, 21.9 us)
Sparse Core Ops, SparseCore 0:
  10.5 62.7 all-gather.6
  75.1 38.2 all-gather.8
  153.2 37.9 reduce-scatter.1

commit v9 on v8

--- a/solution.py
+++ b/solution.py
@@ -226,7 +226,10 @@
     merging = []
     if merge:
         *merging, rest = rest[1], rest[2], *rest[-2:], rest[:1] + rest[3:-2]
-    col_term, row_term, scores, grads, row_bias, col_bias, counts, stacks = rest[-10:-2]
+    if near:
+        row_bias, col_bias, col_term, row_term, scores, grads, counts, stacks = rest[-10:-2]
+    else:
+        col_term, row_term, row_bias, col_bias, scores, grads, counts, stacks = rest[-10:-2]
     arrival, stack_arrivals = rest[-2:]
     padded, n_row = row_term.shape[1], row_term.shape[0]
     n_col = col_bias.shape[0]
@@ -250,12 +253,13 @@
             fetch.start()
             for chunk in range(1, stacks.shape[0]):
                 bring(chunk).start()
-        log_total = jnp.log(masses[n_col + n_row : n_col + n_row + 1, :])
-        col_bias[...] = 0.5 * (jnp.log(masses[0:n_col, :]) - log_total)
-        row_logs = 0.5 * jnp.log(masses[n_col : n_col + n_row, :])
-        for i in range(n_row):
-            turned = jnp.broadcast_to(row_logs[i : i + 1, :], (LANES, LANES)).T
-            row_bias[i * LANES // 8 : (i + 1) * LANES // 8] = turned.reshape(-1, 8, LANES)
+        if not near:
+            log_total = jnp.log(masses[n_col + n_row : n_col + n_row + 1, :])
+            col_bias[...] = 0.5 * (jnp.log(masses[0:n_col, :]) - log_total)
+            row_logs = 0.5 * jnp.log(masses[n_col : n_col + n_row, :])
+            for i in range(n_row):
+                turned = jnp.broadcast_to(row_logs[i : i + 1, :], (LANES, LANES)).T
+                row_bias[i * LANES // 8 : (i + 1) * LANES // 8] = turned.reshape(-1, 8, LANES)
         row_term[...] = rest[0][...] if near else jnp.zeros(row_term.shape, F32)
 
     if near:
@@ -334,7 +338,7 @@
     blocks = col_stack.shape[1] // LANES
     near = earlier is not None
     merge = bool(extra)
-    ready = [earlier] if near else []
+    ready, biases = ([earlier[0]], list(earlier[1:])) if near else ([], [])
     placed = (col_stack, counts) if near else [pltpu.with_memory_space_constraint(value, pltpu.HBM) for value in (col_stack, counts)]
     out_blocks = blocks if merge else count * BLOCKS
     scratch = [
@@ -349,18 +353,17 @@
             grid=(count,),
             in_specs=whole(2)
             + [pl.BlockSpec(memory_space=pltpu.VMEM if near else pltpu.HBM)] * 2
-            + whole(1 + len(ready) + len(extra)),
+            + whole(1 + len(ready) + len(extra) + len(biases)),
             out_specs=[
                 pl.BlockSpec(memory_space=pltpu.HBM)
                 if merge
                 else pl.BlockSpec((BLOCKS, padded, LANES), lambda g, *_: (g, 0, 0)),
                 pl.BlockSpec((words // LANES, padded, LANES), lambda g, *_: (0, 0, 0)),
-            ],
+            ]
+            + whole(0 if near else 2),
             scratch_shapes=[
                 pltpu.VMEM((words // 8, BLOCKS, 8, LANES), F32),
                 pltpu.VMEM((words // 8, BLOCKS, 8, LANES), F32),
-                pltpu.VMEM((words // 8, 8, LANES), F32),
-                pltpu.VMEM((blocks * CORES, LANES), F32),
                 pltpu.VMEM((8, 8, LANES) if near else counts.shape, F32),
                 pltpu.VMEM((count, deep, BLOCKS * LANES), BF16),
                 pltpu.SemaphoreType.DMA(()),
@@ -371,9 +374,10 @@
         out_shape=[
             (pltpu.HBM if merge else jax.ShapeDtypeStruct)((out_blocks, padded, LANES), F32),
             (pltpu.HBM if merge else jax.ShapeDtypeStruct)((words // LANES, padded, LANES), F32),
-        ],
+        ]
+        + ([] if near else [jax.ShapeDtypeStruct((words // 8, 8, LANES), F32), jax.ShapeDtypeStruct((blocks * CORES, LANES), F32)]),
         compiler_params=pltpu.CompilerParams(vmem_limit_bytes=36 << 20),
-    )(*scalars, row_turned, row_stack, *placed, masses, *ready, *extra)
+    )(*scalars, row_turned, row_stack, *placed, masses, *ready, *extra, *biases)
 
 
 def swap_sum(value, axis, size, bit):
@@ -433,11 +437,11 @@
     chunks = n_col // CORES // BLOCKS
     early = chunks // 2
     inputs = (scalars, row_turned, row_stack)
-    far_term, row_term = part_grads(*inputs, far_stack, counts, masses, None, 0, chunks)
+    far_term, row_term, *biases = part_grads(*inputs, far_stack, counts, masses, None, 0, chunks)
     swapped = lax.ppermute(far_term, "core", [(0, 1), (1, 0)])
-    piece, row_term = part_grads(*inputs, near_stack, counts, masses, row_term, 0, early)
+    piece, row_term = part_grads(*inputs, near_stack, counts, masses, (row_term, *biases), 0, early)
     half, row_term = part_grads(
-        *inputs, near_stack, counts, masses, row_term, early, chunks - early, (piece, swapped)
+        *inputs, near_stack, counts, masses, (row_term, *biases), early, chunks - early, (piece, swapped)
     )
     loss_scale = 4.0 * float(words * n_z * n_row_axis) ** (-0.5)
     row_grad = lax.psum_scatter(row_term, "col", scatter_dimension=0, tiled=False)

time: 204 us -> 204 us (level)
  no operation moved by 1% of the time
where the time goes in v9:
time: 204 us; the launch traced here: 203 us
  waiting for transfers between devices  91.2 us (45%)
  Pallas kernels  57.7 us (28%)
  starting transfers between devices  35 us (17%)
  between operations  14 us (7%)
  other arithmetic  3.29 us (2%)
    all_gather x1, waiting for transfers between devices, per_device(): col_blocks = lax.all_gather(col_emb, ROW, axis=0)  41.5 us
    pallas_call x3, Pallas kernels, part_grads(): pl.pallas_call(functools.partial(part_kernel, near=near, first=first, mer...  34.1 us
    reduce_scatter x1, waiting for transfers between devices, per_device(): lax.psum_scatter(row_term, 'col', scatter_dimension=0, tiled=False)  30.7 us
    all_to_all x1, starting transfers between devices, per_device(): lax.all_to_all(blocks.reshape(-1, slots_each, sub_rows, sub_cols), ALL, s...  14.5 us
    ppermute x8, starting transfers between devices, swap_sum(): lax.ppermute(value, axis, [(i, i ^ bit) for i in range(size)])  12.8 us
    ppermute x8, waiting for transfers between devices, swap_sum(): lax.ppermute(value, axis, [(i, i ^ bit) for i in range(size)])  12 us
    pallas_call x4, Pallas kernels, stack_cols(): pl.pallas_call(stack_kernel, name='stack_near' if near else 'stack_far',...  9.21 us
    pallas_call x1, Pallas kernels, sort_slots(): pl.pallas_call(functools.partial(sort_kernel, columns=columns), name='sor...  7.99 us
  transfers between devices with their start and end apart: 14, of which 12 were waited for; matrix products, arithmetic and copies ran while one was open for 2% of the time, Pallas kernels for 16%

profile of v9, /device:TPU:16, one launch (start us, length us, event | category | flops | bytes accessed | tf_op | source)
XLA Modules:
  0.0 203.3 jit_solution(13216676001997104840)
XLA Ops:
  7.9 14.5 %all-to-all-start = ((f32[256,2,8,128]{3,2,1,0:T(8,128)}), f32[256,2,8,128]{3,2,1,0:T(8,128)S(1)}, u32[]{:S(2)}, u32[]{:S(2)}) async-start(f32[256,2,8,128]{3,2,1,0:T(8,128)} %bitcast.26), calls=%async_computation | async-start | bytes 4194304 | tf_op jit(solution)/shard_map/all_to_all | solution.py:407
  23.9 8.0 %sort_slots.1 = (s32[512]{0:T(512)}, s32[512]{0:T(512)}, s32[5]{0:T(128)}) custom-call(s32[512]{0:T(512)} %select_n.5.target, s32[1]{0:T(128)} %bitcast.4.core), custom_call_target="tpu_custom_call" | custom-call | tf_op jit(solution)/shard_map/sort_slots/pallas_call | solution.py:141
  31.9 41.5 %all-gather.7.cloned.1.call-done = f32[32,300,128]{2,1,0:T(8,128)} async-done(((f32[1,300,128]{2,1,0:T(8,128)}), f32[32,300,128]{2,1,0:T(8,128)}) %all-gather.7.cloned.1.call-update) | async-done | bytes 4915216 | tf_op jit(solution)/shard_map/all_gather | solution.py:400
  73.4 1.6 all-to-all-done
  75.0 5.7 %place_counts.1 = (f32[512,8,128]{2,1,0:T(8,128)S(1)}, f32[48,128]{1,0:T(8,128)S(1)}) custom-call(s32[512]{0:T(512)} %select_n.5.target, s32[512]{0:T(512)S(1)} %convert_element_type.4.alive, f32[512,8,128]{2,1,0:T(8,128)S(1)} %bitcast.21), custom_call_target="tpu_custom_call" | custom-call | tf_op jit(solution)/shard_map/place_counts/pallas_call | solution.py:76
  82.0 2.4 %collective-permute-done = f32[16,128]{1,0:T(8,128)S(1)} collective-permute-done((f32[16,128]{1,0:T(8,128)S(1)}, f32[16,128]{1,0:T(8,128)S(1)}, u32[]{:S(2)}, u32[]{:S(2)}) %collective-permute-start) | collective-permute-done | bytes 8224 | tf_op jit(solution)/shard_map/ppermute | solution.py:384
  85.3 3.8 %collective-permute-done.1 = f32[16,128]{1,0:T(8,128)S(1)} collective-permute-done((f32[16,128]{1,0:T(8,128)S(1)}, f32[16,128]{1,0:T(8,128)S(1)}, u32[]{:S(2)}, u32[]{:S(2)}) %collective-permute-start.1) | collective-permute-done | bytes 8224 | tf_op jit(solution)/shard_map/ppermute | solution.py:384
  89.1 3.4 %collective-permute-start.2 = (f32[16,128]{1,0:T(8,128)S(1)}, f32[16,128]{1,0:T(8,128)S(1)}, u32[]{:S(2)}, u32[]{:S(2)}) collective-permute-start(f32[16,128]{1,0:T(8,128)S(1)} %add.33), channel_id=1, source_target_pairs={{0,4},{1,5},{2,6},{3,7},{4,0},{5,1},{6,2},{7,3},{8,12},{9,13},{10,... | collective-permute-start | bytes 24584 | tf_op jit(solution)/shard_map/ppermute | solution.py:384
  92.6 2.3 %stack_far.2.rest_0_ = bf16[608,2048]{1,0:T(8,128)(2,1)} custom-call(s32[1]{0:T(128)} %bitcast.4.core, f32[16,2,300,128]{3,2,1,0:T(8,128)} %bitcast.22), custom_call_target="tpu_custom_call" | custom-call | tf_op jit(solution)/shard_map/stack_far/pallas_call | solution.py:207
  94.9 1.8 collective-permute-done.2
  98.0 2.1 %collective-permute-start.4 = (f32[40,128]{1,0:T(8,128)S(1)}, f32[40,128]{1,0:T(8,128)S(1)}, u32[]{:S(2)}, u32[]{:S(2)}) collective-permute-start(f32[40,128]{1,0:T(8,128)S(1)} %fusion.1), channel_id=1, source_target_pairs={{0,16},{16,0},{32,48},{48,32},{1,17},{17,1},{33,49},{49,33},{2,18}... | collective-permute-start | bytes 61448 | tf_op jit(solution)/shard_map/ppermute | solution.py:384
  100.1 2.3 %stack_far.3 = bf16[608,2048]{1,0:T(8,128)(2,1)} custom-call(s32[1]{0:T(128)} %bitcast.4.core, f32[16,2,300,128]{3,2,1,0:T(8,128)} %bitcast.23, bf16[608,2048]{1,0:T(8,128)(2,1)} %stack_far.2.rest_0_), custom_call_target="tpu_custom_call", output_to_operand_aliasing={{}: (2, {})} | custom-call | tf_op jit(solution)/shard_map/stack_far/pallas_call | solution.py:207
  103.5 2.3 %stack_near.2.rest_0_ = bf16[608,2048]{1,0:T(8,128)(2,1)} custom-call(s32[1]{0:T(128)} %bitcast.4.core, f32[16,2,300,128]{3,2,1,0:T(8,128)} %bitcast.24), custom_call_target="tpu_custom_call" | custom-call | tf_op jit(solution)/shard_map/stack_near/pallas_call | solution.py:207
  105.8 2.0 collective-permute-done.5
  108.5 2.3 %stack_near.3.stack_far = bf16[608,2048]{1,0:T(8,128)(2,1)} custom-call(s32[1]{0:T(128)} %bitcast.4.core, f32[16,2,300,128]{3,2,1,0:T(8,128)} %bitcast.25, bf16[608,2048]{1,0:T(8,128)(2,1)} %stack_near.2.rest_0_), custom_call_target="tpu_custom_call", output_to_operand_aliasing={{}: (2, {})} | custom-call | tf_op jit(solution)/shard_map/stack_near/pallas_call | solution.py:207
  111.6 1.9 all-gather.9.cloned.1.call-done.row_blocks
  113.5 3.2 %collective-permute-start.7 = (f32[40,128]{1,0:T(8,128)S(1)}, f32[40,128]{1,0:T(8,128)S(1)}, u32[]{:S(2)}, u32[]{:S(2)}) collective-permute-start(f32[40,128]{1,0:T(8,128)S(1)} %add.38), channel_id=1, source_target_pairs={{0,128},{64,192},{128,0},{192,64},{1,129},{65,193},{129,1},{193,65... | collective-permute-start | bytes 61448 | tf_op jit(solution)/shard_map/ppermute | solution.py:384
  118.8 16.7 %far_grads.1 = (f32[16,304,128]{2,1,0:T(8,128)S(1)}, f32[8,304,128]{2,1,0:T(8,128)S(1)}, f32[128,8,128]{2,1,0:T(8,128)S(1)}, f32[32,128]{1,0:T(8,128)S(1)}) custom-call(s32[512]{0:T(512)S(1)} %copy-done.4, s32[512]{0:T(512)S(1)} %copy-done.5, s32[5]{0:T(128)S(1)} %copy-done.6, s32[1]{0:T(128)} %bitcast.4.core, ...), custom_call_target="tpu_custom_call" | custom-call | tf_op jit(solution)/shard_map/far_grads/pallas_call | solution.py:348
  135.7 8.2 %near_grads.1 = (f32[8,304,128]{2,1,0:T(8,128)S(1)}, f32[8,304,128]{2,1,0:T(8,128)S(1)}) custom-call(s32[512]{0:T(512)S(1)} %copy-done.4, s32[512]{0:T(512)S(1)} %copy-done.5, s32[5]{0:T(128)S(1)} %copy-done.6, s32[1]{0:T(128)} %bitcast.4.core, bf16[1024,1024]{1,0:T(8,128)(2,1)S(1)} %get-tuple-element.67.row_turned, ...), custom_call_target="tpu_custom_call" | custom-call | tf_op jit(solution)/shard_map/near_grads/pallas_call | solution.py:348
  143.9 9.2 %merge_grads.1 = (f32[16,304,128]{2,1,0:T(8,128)}, f32[8,304,128]{2,1,0:T(8,128)}) custom-call(s32[512]{0:T(512)S(1)} %copy-done.4, s32[512]{0:T(512)S(1)} %copy-done.5, s32[5]{0:T(128)S(1)} %copy-done.6, s32[1]{0:T(128)} %bitcast.4.core, bf16[1024,1024]{1,0:T(8,128)(2,1)S(1)} %get-tuple-element.67.row_turned, ...), custom_call_target="tpu_custom_call" | custom-call | tf_op jit(solution)/shard_map/merge_grads/pallas_call | solution.py:348
  153.1 7.5 %all-to-all-start.1 = ((f32[16,304,128]{2,1,0:T(8,128)}), f32[16,304,128]{2,1,0:T(8,128)S(1)}, u32[]{:S(2)}, u32[]{:S(2)}) async-start(f32[16,304,128]{2,1,0:T(8,128)} %get-tuple-element.79), calls=%async_computation.1 | async-start | bytes 4980736 | tf_op jit(solution)/shard_map/all_to_all | solution.py:448
  160.7 30.7 %reduce-scatter.2.cloned.1.call-done = f32[1,304,128]{2,1,0:T(8,128)} async-done(((f32[8,304,128]{2,1,0:T(8,128)}), f32[1,304,128]{2,1,0:T(8,128)}) %reduce-scatter.2.cloned.1.call-update) | async-done | bytes 155664 | tf_op jit(solution)/shard_map/reduce_scatter | solution.py:447
  191.4 1.7 fusion
  193.1 2.8 %all-to-all-done.1 = f32[16,304,128]{2,1,0:T(8,128)S(1)} async-done(((f32[16,304,128]{2,1,0:T(8,128)}), f32[16,304,128]{2,1,0:T(8,128)S(1)}, u32[]{:S(2)}, u32[]{:S(2)}) %all-to-all-start.1) | async-done | bytes 2490400 | tf_op jit(solution)/shard_map/all_to_all | solution.py:448
  (70 shorter events, 11.4 us)
Async XLA Ops:
  7.2 66.2 %all-gather.7.cloned.1.call-start = ((), (), s32[]{:S(2)}) async-start(), calls=%async_computation.4 | async-start | bytes 5136384 | tf_op jit(solution)/shard_map/all_gather | solution.py:400
  7.9 14.6 %copy-start.11 = (s32[1,1,8,32,2]{3,4,2,1,0:T(2,128)S(1)}, s32[1,1,8,32,2]{3,4,2,1,0:T(2,128)}, u32[]{:S(2)}) copy-start(s32[1,1,8,32,2]{3,4,2,1,0:T(2,128)} %param.8) | copy-start | bytes 6148
  7.9 14.7 %copy-start.12 = (s32[1,1,8,32]{3,2,1,0:T(8,128)S(1)}, s32[1,1,8,32]{3,2,1,0:T(8,128)}, u32[]{:S(2)}) copy-start(s32[1,1,8,32]{3,2,1,0:T(8,128)} %param.9) | copy-start | bytes 3076
  7.9 67.1 %all-to-all-start = ((f32[256,2,8,128]{3,2,1,0:T(8,128)}), f32[256,2,8,128]{3,2,1,0:T(8,128)S(1)}, u32[]{:S(2)}, u32[]{:S(2)}) async-start(f32[256,2,8,128]{3,2,1,0:T(8,128)} %bitcast.26), calls=%async_computation | async-start | bytes 4194304 | tf_op jit(solution)/shard_map/all_to_all | solution.py:407
  22.4 91.0 %all-gather.9.cloned.1.call-start = ((), (), s32[]{:S(2)}) async-start(), calls=%async_computation.5 | async-start | bytes 1400832 | tf_op jit(solution)/shard_map/all_gather | solution.py:404
  73.4 118.0 %reduce-scatter.2.cloned.1.call-start = ((), (), s32[]{:S(2)}) async-start(), calls=%async_computation.3 | async-start | bytes 1400832 | tf_op jit(solution)/shard_map/reduce_scatter | solution.py:447
  80.7 14.2 %copy-start.1 = (f32[512,8,128]{2,1,0:T(8,128)}, f32[512,8,128]{2,1,0:T(8,128)S(1)}, u32[]{:S(2)}) copy-start(f32[512,8,128]{2,1,0:T(8,128)S(1)} %get-tuple-element.70.counts_far) | copy-start | bytes 6291460
  80.7 3.7 %collective-permute-start = (f32[16,128]{1,0:T(8,128)S(1)}, f32[16,128]{1,0:T(8,128)S(1)}, u32[]{:S(2)}, u32[]{:S(2)}) collective-permute-start(f32[16,128]{1,0:T(8,128)S(1)} %slice.30), channel_id=1, source_target_pairs={{0,1},{1,0},{2,3},{3,2},{4,5},{5,4},{6,7},{7,6},{8,9},{9,8},{10,11... | collective-permute-start | bytes 24584 | tf_op jit(solution)/shard_map/ppermute | solution.py:384
  84.4 4.7 %collective-permute-start.1 = (f32[16,128]{1,0:T(8,128)S(1)}, f32[16,128]{1,0:T(8,128)S(1)}, u32[]{:S(2)}, u32[]{:S(2)}) collective-permute-start(f32[16,128]{1,0:T(8,128)S(1)} %slice_add_fusion), channel_id=1, source_target_pairs={{0,2},{1,3},{2,0},{3,1},{4,6},{5,7},{6,4},{7,5},{8,10},{9,11},{10,... | collective-permute-start | bytes 24584 | tf_op jit(solution)/shard_map/ppermute | solution.py:384
  89.1 7.6 %collective-permute-start.2 = (f32[16,128]{1,0:T(8,128)S(1)}, f32[16,128]{1,0:T(8,128)S(1)}, u32[]{:S(2)}, u32[]{:S(2)}) collective-permute-start(f32[16,128]{1,0:T(8,128)S(1)} %add.33), channel_id=1, source_target_pairs={{0,4},{1,5},{2,6},{3,7},{4,0},{5,1},{6,2},{7,3},{8,12},{9,13},{10,... | collective-permute-start | bytes 24584 | tf_op jit(solution)/shard_map/ppermute | solution.py:384
  96.7 1.3 collective-permute-start.3
  98.0 4.4 %collective-permute-start.4 = (f32[40,128]{1,0:T(8,128)S(1)}, f32[40,128]{1,0:T(8,128)S(1)}, u32[]{:S(2)}, u32[]{:S(2)}) collective-permute-start(f32[40,128]{1,0:T(8,128)S(1)} %fusion.1), channel_id=1, source_target_pairs={{0,16},{16,0},{32,48},{48,32},{1,17},{17,1},{33,49},{49,33},{2,18}... | collective-permute-start | bytes 61448 | tf_op jit(solution)/shard_map/ppermute | solution.py:384
  102.4 5.4 %collective-permute-start.5 = (f32[40,128]{1,0:T(8,128)S(1)}, f32[40,128]{1,0:T(8,128)S(1)}, u32[]{:S(2)}, u32[]{:S(2)}) collective-permute-start(f32[40,128]{1,0:T(8,128)S(1)} %add.36), channel_id=1, source_target_pairs={{0,32},{16,48},{32,0},{48,16},{1,33},{17,49},{33,1},{49,17},{2,34}... | collective-permute-start | bytes 61448 | tf_op jit(solution)/shard_map/ppermute | solution.py:384
  107.8 3.8 %collective-permute-start.6 = (f32[40,128]{1,0:T(8,128)S(1)}, f32[40,128]{1,0:T(8,128)S(1)}, u32[]{:S(2)}, u32[]{:S(2)}) collective-permute-start(f32[40,128]{1,0:T(8,128)S(1)} %add.37), channel_id=1, source_target_pairs={{0,64},{64,0},{128,192},{192,128},{1,65},{65,1},{129,193},{193,129... | collective-permute-start | bytes 61448 | tf_op jit(solution)/shard_map/ppermute | solution.py:384
  108.5 10.3 %copy-start.6 = (s32[5]{0:T(128)S(1)}, s32[5]{0:T(128)}, u32[]{:S(2)}) copy-start(s32[5]{0:T(128)} %get-tuple-element.49.offsets) | copy-start | bytes 64
  113.5 5.3 %collective-permute-start.7 = (f32[40,128]{1,0:T(8,128)S(1)}, f32[40,128]{1,0:T(8,128)S(1)}, u32[]{:S(2)}, u32[]{:S(2)}) collective-permute-start(f32[40,128]{1,0:T(8,128)S(1)} %add.38), channel_id=1, source_target_pairs={{0,128},{64,192},{128,0},{192,64},{1,129},{65,193},{129,1},{193,65... | collective-permute-start | bytes 61448 | tf_op jit(solution)/shard_map/ppermute | solution.py:384
  118.8 16.8 %copy-start = (bf16[608,2048]{1,0:T(8,128)(2,1)S(1)}, bf16[608,2048]{1,0:T(8,128)(2,1)}, u32[]{:S(2)}) copy-start(bf16[608,2048]{1,0:T(8,128)(2,1)} %stack_near.3.stack_far) | copy-start | bytes 7471108
  118.8 16.8 %copy-start.2 = (f32[512,8,128]{2,1,0:T(8,128)S(1)}, f32[512,8,128]{2,1,0:T(8,128)}, u32[]{:S(2)}) copy-start(f32[512,8,128]{2,1,0:T(8,128)} %copy-done.1) | copy-start | bytes 6291460
  135.5 8.3 %collective-permute-start.8 = (f32[16,304,128]{2,1,0:T(8,128)S(1)}, f32[16,304,128]{2,1,0:T(8,128)S(1)}, u32[]{:S(2)}, u32[]{:S(2)}) collective-permute-start(f32[16,304,128]{2,1,0:T(8,128)S(1)} %get-tuple-element.78), channel_id=1, source_target_pairs={{0,8},{8,0},{1,9},{9,1},{2,10},{10,2},{3,11},{11,3},{4,12},{12,4},... | collective-permute-start | bytes 7471112 | tf_op jit(solution)/shard_map/ppermute | solution.py:441
  153.1 38.3 %copy-start.7 = (f32[300,128]{1,0:T(8,128)S(1)}, f32[300,128]{1,0:T(8,128)}, u32[]{:S(2)}) copy-start(f32[300,128]{1,0:T(8,128)} %param.10) | copy-start | bytes 460804
  153.1 38.3 %copy-start.9 = (f32[300,128]{1,0:T(8,128)S(1)}, f32[300,128]{1,0:T(8,128)}, u32[]{:S(2)}) copy-start(f32[300,128]{1,0:T(8,128)} %param.12) | copy-start | bytes 460804
  153.1 42.8 %all-to-all-start.1 = ((f32[16,304,128]{2,1,0:T(8,128)}), f32[16,304,128]{2,1,0:T(8,128)S(1)}, u32[]{:S(2)}, u32[]{:S(2)}) async-start(f32[16,304,128]{2,1,0:T(8,128)} %get-tuple-element.79), calls=%async_computation.1 | async-start | bytes 4980736 | tf_op jit(solution)/shard_map/all_to_all | solution.py:448
  160.7 35.3 %copy-start.8 = (f32[300,128]{1,0:T(8,128)S(1)}, f32[300,128]{1,0:T(8,128)}, u32[]{:S(2)}) copy-start(f32[300,128]{1,0:T(8,128)} %param.11) | copy-start | bytes 460804
  160.7 35.4 %copy-start.10 = (f32[300,128]{1,0:T(8,128)S(1)}, f32[300,128]{1,0:T(8,128)}, u32[]{:S(2)}) copy-start(f32[300,128]{1,0:T(8,128)} %param.13) | copy-start | bytes 460804
  (3 other events, 21.9 us)
Sparse Core Ops, SparseCore 0:
  10.5 62.7 all-gather.6
  75.1 38.2 all-gather.8
  153.2 38.1 reduce-scatter.1
